TPU v7x, 32 devices: a whole 2x2x4 slice. The times are simulated.
32 devices in a mesh: grp: 2 (over x), seq: 16 (over z, y, core).
Axes of the slice: x: 2, y: 2, z: 4, core: 2. Of those that a mesh axis runs over, the one named last changes fastest.
Arguments:
- image_qkv: bfloat16 [3, 8, 16, 896, 128], P(None, 'grp', None, 'seq'), parts along dimension 1, may hold values from -16 to 16
- text_kv: bfloat16 [2, 2, 8, 16, 512, 128], P(None, None, 'grp', None, 'seq'), parts along dimension 2, may hold values from -6 to 6
- prompt_ids: int32 [2, 8, 512], P(None, 'grp'), parts along dimension 1, may hold values from 0 to 32127, as said below
- timesteps: int32 [8], P('grp'), parts along dimension 0, may hold values from 0 to 999
- image_states: bfloat16 [8, 896, 1536], P('grp', 'seq'), parts along dimension 0, may hold values from -6 to 6
- frozen_out: bfloat16 [2048, 1536], P('seq'), may hold values from -0.125 to 0.125
- trainee_out: bfloat16 [4096, 1536], P(('grp', 'seq')), parts along dimension 0, may hold values from -0.125 to 0.125
- time_mod: bfloat16 [256, 3072], replicated, may hold values from -0.375 to 0.375
- final_head: bfloat16 [1536, 64], replicated, may hold values from -0.15625 to 0.15625
Outputs:
- weight_grad: float32 [4096, 1536], P(('grp', 'seq')), parts along dimension 0
There are 2 independent parts, one for each index of `grp`. A program takes and returns all parts, laid end to end along the dimension named above; an argument that names none is the same for every part. Nothing has to cross between parts.
Inputs may be any that keep to these rules, and one draw needn't show every extreme that they name: `prompt_ids`: zero marks padding; in each row of 512 ids the padding is a suffix and position 0 is never padding.
All inputs are finite; a program needn't handle non-finite values.
Results may differ from a plain program's by a relative error of at most 0.011.
Values may be sent and summed in bfloat16 or wider, within the bound.
No kernel may reach another device: no remote copies, remote signals or barrier semaphores. Data moves between devices by JAX's collectives and lax.ppermute only.
A program may use at most 128 MiB of HBM per device.

v0:
```python
import math

import jax
import jax.numpy as jnp
from jax import lax
from jax.sharding import PartitionSpec as P

SAMPLES = 4
HEADS = 16
HEAD_DIM = 128
WIDTH = 1536
TIME_DIM = 256


def image_block(queries, image_keys, image_values):
    factor = HEAD_DIM ** (-0.5)
    image_scores = jnp.dot(queries, image_keys.T, preferred_element_type=jnp.float32) * factor
    image_max = jnp.max(image_scores, axis=1, keepdims=True)
    image_exp = jnp.exp(image_scores - image_max)
    image_total = jnp.sum(image_exp, axis=1, keepdims=True)
    image_part = jnp.dot(
        image_exp.astype(jnp.bfloat16), image_values, preferred_element_type=jnp.float32
    )
    return (image_max, image_total, image_part)


def text_finish(queries, image_stats, text_keys, text_values, allowed_text):
    factor = HEAD_DIM ** (-0.5)
    image_max, image_total, image_part = image_stats
    text_scores = jnp.dot(queries, text_keys.T, preferred_element_type=jnp.float32) * factor
    text_scores = jnp.where(allowed_text[None, :], text_scores, -jnp.inf)
    pass_max = jnp.maximum(image_max, jnp.max(text_scores, axis=1, keepdims=True))
    ratio = jnp.exp(image_max - pass_max)
    text_exp = jnp.exp(text_scores - pass_max)
    text_part = jnp.dot(
        text_exp.astype(jnp.bfloat16), text_values, preferred_element_type=jnp.float32
    )
    numer = ratio * image_part + text_part
    denom = ratio * image_total + jnp.sum(text_exp, axis=1, keepdims=True)
    return (numer / denom).astype(jnp.bfloat16)


def head_out(branch, states, gate, scale, final_head):
    mixed = states.astype(jnp.float32) + gate[:, None, :] * branch
    normed = (
        mixed
        * lax.rsqrt(jnp.mean(mixed * mixed, axis=-1, keepdims=True) + 1e-06)
        * (1.0 + scale[:, None, :])
    )
    normed = normed.astype(jnp.bfloat16)
    return jnp.einsum("bic,cd->bid", normed, final_head, preferred_element_type=jnp.float32)


def shards(
    image_qkv,
    text_kv,
    prompt_ids,
    timesteps,
    image_states,
    frozen_out,
    trainee_out,
    time_mod,
    final_head,
):
    group_size = lax.axis_size("seq")
    position = lax.axis_index("seq")
    image_dev = image_qkv.shape[3]
    text_dev = text_kv.shape[4]
    item_count = SAMPLES * HEADS
    owned_count = item_count // group_size
    token_rows = SAMPLES * image_dev
    image_all = image_dev * group_size
    block_rows = image_dev * min(group_size, 8)
    block_count = image_all // block_rows
    image_local = image_qkv.transpose(0, 2, 1, 3, 4).reshape(3, item_count, image_dev, HEAD_DIM)
    text_local = text_kv.transpose(0, 1, 3, 2, 4, 5).reshape(4, item_count, text_dev, HEAD_DIM)
    image_heads, text_heads = (
        lax.all_to_all(image_local, "seq", split_axis=1, concat_axis=2, tiled=True),
        lax.all_to_all(text_local, "seq", split_axis=1, concat_axis=2, tiled=True),
    )
    owned_items = position * owned_count + jnp.arange(owned_count, dtype=jnp.int32)
    sample_of = owned_items % SAMPLES
    selector = (sample_of[:, None] == jnp.arange(SAMPLES, dtype=jnp.int32)[None, :]).astype(
        jnp.float32
    )
    live_all = (prompt_ids != 0).astype(jnp.float32)
    live_owned = jnp.einsum("jb,pbt->pjt", selector, live_all) > 0.5

    def query_blocks(item_index):
        return image_heads[0, item_index].reshape(block_count, block_rows, HEAD_DIM)

    def joint_item(item_index):
        image_keys = image_heads[1, item_index]
        image_values = image_heads[2, item_index]

        def per_block(queries):
            stats = image_block(queries, image_keys, image_values)
            concept = text_finish(
                queries,
                stats,
                text_heads[0, item_index],
                text_heads[1, item_index],
                live_owned[0, item_index],
            )
            null = text_finish(
                queries,
                stats,
                text_heads[2, item_index],
                text_heads[3, item_index],
                live_owned[1, item_index],
            )
            return jnp.stack([concept, null])

        blocks = lax.map(per_block, query_blocks(item_index))
        return blocks.transpose(1, 0, 2, 3).reshape(2, image_all, HEAD_DIM)

    both_passes = lax.map(joint_item, jnp.arange(owned_count, dtype=jnp.int32)).transpose(
        1, 0, 2, 3
    )
    returned = lax.all_to_all(both_passes, "seq", split_axis=2, concat_axis=1, tiled=True)
    attention = returned.reshape(2, HEADS, SAMPLES, image_dev, HEAD_DIM).transpose(0, 2, 3, 1, 4)
    attention = attention.reshape(2, token_rows, HEADS * HEAD_DIM)
    half_dim = TIME_DIM // 2
    freqs = jnp.exp(-math.log(10000.0) * jnp.arange(half_dim, dtype=jnp.float32) / half_dim)
    angles = timesteps.astype(jnp.float32)[:, None] * freqs[None, :]
    embedding = jnp.concatenate([jnp.cos(angles), jnp.sin(angles)], 1)
    modulation = jnp.dot(embedding, time_mod.astype(jnp.float32), precision=lax.Precision.HIGHEST)
    gate = modulation[:, :WIDTH]
    scale = modulation[:, WIDTH:]
    piece_frozen = lax.all_gather(frozen_out, "seq", axis=0, tiled=True)
    piece_trainee = lax.all_gather(trainee_out, "seq", axis=0, tiled=True)
    columns_c = attention[0]
    columns_n = attention[1]
    branch_c = jnp.dot(columns_c, piece_frozen, preferred_element_type=jnp.float32)
    branch_n = jnp.dot(columns_n, piece_frozen, preferred_element_type=jnp.float32)
    branch_s = jnp.dot(columns_c, piece_trainee, preferred_element_type=jnp.float32)
    branch_c = branch_c.reshape(SAMPLES, image_dev, WIDTH)
    branch_n = branch_n.reshape(SAMPLES, image_dev, WIDTH)
    branch_s = branch_s.reshape(SAMPLES, image_dev, WIDTH)
    velocity_c = head_out(branch_c, image_states, gate, scale, final_head)
    velocity_n = head_out(branch_n, image_states, gate, scale, final_head)
    target = velocity_n - (velocity_c - velocity_n)

    def student(branch):
        velocity_s = head_out(branch, image_states, gate, scale, final_head)
        return jnp.sum((velocity_s - target) ** 2) / SAMPLES

    loss_part, pull = jax.vjp(student, branch_s)
    (cotangent,) = pull(jnp.ones_like(loss_part))
    cotangent_samples = cotangent.astype(jnp.bfloat16)
    cotangent_rows = cotangent_samples.reshape(token_rows, WIDTH)
    columns = attention[0]
    return lax.psum_scatter(
        lax.dot_general(
            columns, cotangent_rows, (((0,), (0,)), ((), ())), preferred_element_type=jnp.float32
        ),
        "seq",
        scatter_dimension=0,
        tiled=True,
    )


def solution(mesh):
    return jax.shard_map(
        shards,
        mesh=mesh,
        in_specs=(
            P(None, "grp", None, "seq", None),
            P(None, None, "grp", None, "seq", None),
            P(None, "grp", None),
            P("grp"),
            P("grp", "seq", None),
            P("seq", None),
            P(("grp", "seq"), None),
            P(),
            P(),
        ),
        out_specs=P(("grp", "seq"), None),
        check_vma=False,
    )
```

profile of v0, /device:TPU:0, one launch (start us, length us, event | category | flops | bytes accessed | tf_op | source)
XLA Modules:
  0.0 544.9 jit_solution(13315047425198892459)
XLA Ops:
  7.3 2.2 copy.27
  9.5 2.0 copy.28
  11.4 7.4 %all-to-all-start.1 = ((bf16[4,64,32,128]{3,2,0,1:T(8,128)(2,1)}), bf16[4,64,32,128]{3,2,0,1:T(8,128)(2,1)}, u32[]{:S(2)}, u32[]{:S(2)}) async-start(bf16[4,64,32,128]{3,2,0,1:T(8,128)(2,1)} %copy.28), calls=%async_computation.1 | async-start | bytes 4194304 | tf_op jit(solution)/shard_map/all_to_all | solution.py:79
  18.9 2.4 copy.23
  21.3 2.0 copy.24
  23.3 49.5 %all-to-all-done.1 = bf16[4,64,32,128]{3,2,0,1:T(8,128)(2,1)} async-done(((bf16[4,64,32,128]{3,2,0,1:T(8,128)(2,1)}), bf16[4,64,32,128]{3,2,0,1:T(8,128)(2,1)}, u32[]{:S(2)}, u32[]{:S(2)}) %all-to-all-start.1) | async-done | bytes 2097184 | tf_op jit(solution)/shard_map/all_to_all | solution.py:79
  72.8 33.3 %all-to-all-start = ((bf16[3,64,56,128]{3,2,0,1:T(8,128)(2,1)}), bf16[3,64,56,128]{3,2,0,1:T(8,128)(2,1)}, u32[]{:S(2)}, u32[]{:S(2)}) async-start(bf16[3,64,56,128]{3,2,0,1:T(8,128)(2,1)} %copy.24), calls=%async_computation | async-start | bytes 5505024 | tf_op jit(solution)/shard_map/all_to_all | solution.py:78
  107.1 3.4 copy.30
  110.6 72.9 %all-to-all-done = bf16[3,64,56,128]{3,2,0,1:T(8,128)(2,1)} async-done(((bf16[3,64,56,128]{3,2,0,1:T(8,128)(2,1)}), bf16[3,64,56,128]{3,2,0,1:T(8,128)(2,1)}, u32[]{:S(2)}, u32[]{:S(2)}) %all-to-all-start) | async-done | bytes 2752544 | tf_op jit(solution)/shard_map/all_to_all | solution.py:78
  183.5 4.0 copy.26
  187.4 113.6 %while.23 = (s32[]{:T(128)}, bf16[4,2,896,128]{3,1,0,2:T(2,128)(2,1)}, s32[4]{0:T(128)S(1)}, bf16[3,4,896,128]{3,2,1,0:T(8,128)(2,1)}, pred[2,4,512]{2,1,0:T(4,1...) while((s32[]{:T(128)}, ...), condition=%wide.region_9.10_spmd, body=%wide.region_0.9_spmd.sunk | while | flops 447742848 | bytes 26686016 | solution.py:117
  190.0 1.8 constant_dynamic-slice_fusion.10
  191.8 2.0 dynamic-slice_bitcast_fusion.3
  193.9 19.6 %while.24 = (s32[]{:T(128)}, bf16[2,2,448,128]{3,2,1,0:T(8,128)(2,1)}, bf16[2,448,128]{2,1,0:T(8,128)(2,1)S(1)}, bf16[896,128]{1,0:T(8,128)(2,1)}, pred[1,1,512]...) while((s32[]{:T(128)}, ...), condition=%wide.region_8.8_spmd, body=%wide.region_1.7_spmd.sunk | while | flops 447742848 | bytes 22390328 | solution.py:114
  193.9 1.4 multiply_reduce_fusion.6
  195.9 2.1 fusion.139
  198.6 1.1 fusion.138
  203.7 1.4 multiply_reduce_fusion.6
  205.7 2.1 fusion.139
  208.4 1.1 fusion.138
  214.6 1.3 copy_dynamic-update-slice_fusion.2
  218.4 1.8 constant_dynamic-slice_fusion.10
  220.3 2.0 dynamic-slice_bitcast_fusion.3
  222.3 19.6 %while.24 = (s32[]{:T(128)}, bf16[2,2,448,128]{3,2,1,0:T(8,128)(2,1)}, bf16[2,448,128]{2,1,0:T(8,128)(2,1)S(1)}, bf16[896,128]{1,0:T(8,128)(2,1)}, pred[1,1,512]...) while((s32[]{:T(128)}, ...), condition=%wide.region_8.8_spmd, body=%wide.region_1.7_spmd.sunk | while | flops 447742848 | bytes 22390328 | solution.py:114
  222.3 1.4 multiply_reduce_fusion.6
  224.3 2.1 fusion.139
  227.0 1.1 fusion.138
  232.1 1.4 multiply_reduce_fusion.6
  234.1 2.1 fusion.139
  236.8 1.1 fusion.138
  243.0 1.3 copy_dynamic-update-slice_fusion.2
  246.8 1.8 constant_dynamic-slice_fusion.10
  248.7 2.0 dynamic-slice_bitcast_fusion.3
  250.7 19.6 %while.24 = (s32[]{:T(128)}, bf16[2,2,448,128]{3,2,1,0:T(8,128)(2,1)}, bf16[2,448,128]{2,1,0:T(8,128)(2,1)S(1)}, bf16[896,128]{1,0:T(8,128)(2,1)}, pred[1,1,512]...) while((s32[]{:T(128)}, ...), condition=%wide.region_8.8_spmd, body=%wide.region_1.7_spmd.sunk | while | flops 447742848 | bytes 22390328 | solution.py:114
  250.7 1.4 multiply_reduce_fusion.6
  252.7 2.1 fusion.139
  255.5 1.1 fusion.138
  260.5 1.4 multiply_reduce_fusion.6
  262.6 2.1 fusion.139
  265.3 1.1 fusion.138
  271.4 1.3 copy_dynamic-update-slice_fusion.2
  275.2 1.8 constant_dynamic-slice_fusion.10
  277.1 2.0 dynamic-slice_bitcast_fusion.3
  279.1 19.6 %while.24 = (s32[]{:T(128)}, bf16[2,2,448,128]{3,2,1,0:T(8,128)(2,1)}, bf16[2,448,128]{2,1,0:T(8,128)(2,1)S(1)}, bf16[896,128]{1,0:T(8,128)(2,1)}, pred[1,1,512]...) while((s32[]{:T(128)}, ...), condition=%wide.region_8.8_spmd, body=%wide.region_1.7_spmd.sunk | while | flops 447742848 | bytes 22390328 | solution.py:114
  279.1 1.4 multiply_reduce_fusion.6
  281.1 2.1 fusion.139
  283.9 1.1 fusion.138
  288.9 1.4 multiply_reduce_fusion.6
  291.0 2.1 fusion.139
  293.7 1.1 fusion.138
  299.8 1.3 copy_dynamic-update-slice_fusion.2
  301.1 27.2 %all-to-all-start.2 = ((bf16[2,4,896,128]{3,0,1,2:T(2,128)(2,1)}), bf16[2,4,896,128]{3,0,1,2:T(2,128)(2,1)}, u32[]{:S(2)}, u32[]{:S(2)}) async-start(bf16[2,4,896,128]{3,0,1,2:T(2,128)(2,1)} %bitcast.168), calls=%async_computation.2 | async-start | bytes 3670016 | tf_op jit(solution)/shard_map/all_to_all | solution.py:120
  329.4 35.5 %all-to-all-done.2 = bf16[2,4,896,128]{3,0,1,2:T(2,128)(2,1)} async-done(((bf16[2,4,896,128]{3,0,1,2:T(2,128)(2,1)}), bf16[2,4,896,128]{3,0,1,2:T(2,128)(2,1)}, u32[]{:S(2)}, u32[]{:S(2)}) %all-to-all-start.2) | async-done | bytes 1835040 | tf_op jit(solution)/shard_map/all_to_all | solution.py:120
  364.9 2.7 copy.44
  367.5 1.3 fusion.105
  368.8 1.3 dot_general.66
  370.1 2.2 dot_general.69
  372.4 4.9 multiply_reduce_fusion.4
  377.3 5.0 multiply_reduce_fusion.3
  382.7 2.8 multiply_reduce_fusion.2
  386.4 3.4 multiply_reduce_fusion.1
  389.8 1.8 fusion.65
  391.6 6.4 %fusion.70 = f32[2048,1536]{1,0:T(8,128)} fusion(bf16[224,1536]{1,0:T(8,128)(2,1)S(1)} %bitcast.167, bf16[28,8,16,128]{3,2,1,0:T(8,128)(2,1)S(1)} %bitcast.164), kind=kOutput, calls=%fused_computation.90 | convolution fusion | flops 1409286144 | bytes 14188544 | tf_op jit(solution)/shard_map/dot_general | solution.py:154
  398.0 140.3 %reduce-scatter.2.cloned.1.call-done = f32[128,1536]{1,0:T(8,128)} async-done(((f32[2048,1536]{1,0:T(8,128)}), f32[128,1536]{1,0:T(8,128)}) %reduce-scatter.2.cloned.1.call-update) | async-done | bytes 786448 | tf_op jit(solution)/shard_map/reduce_scatter | solution.py:153
  (265 shorter events, 51.0 us)
Async XLA Ops:
  6.5 322.1 %copy-start = (bf16[256,3072]{1,0:T(8,128)(2,1)S(1)}, bf16[256,3072]{1,0:T(8,128)(2,1)}, u32[]{:S(2)}) copy-start(bf16[256,3072]{1,0:T(8,128)(2,1)} %param.20) | copy-start | bytes 4718596
  6.5 365.8 %all-gather.3.cloned.1.call-start = ((), (), s32[]{:S(2)}) async-start(), calls=%async_computation.4 | async-start | bytes 6684672 | tf_op jit(solution)/shard_map/all_gather | solution.py:131
  11.4 61.4 %all-to-all-start.1 = ((bf16[4,64,32,128]{3,2,0,1:T(8,128)(2,1)}), bf16[4,64,32,128]{3,2,0,1:T(8,128)(2,1)}, u32[]{:S(2)}, u32[]{:S(2)}) async-start(bf16[4,64,32,128]{3,2,0,1:T(8,128)(2,1)} %copy.28), calls=%async_computation.1 | async-start | bytes 4194304 | tf_op jit(solution)/shard_map/all_to_all | solution.py:79
  23.3 83.6 %copy-start.15 = (s32[2,4,512]{2,1,0:T(4,128)S(1)}, s32[2,4,512]{2,1,0:T(4,128)}, u32[]{:S(2)}) copy-start(s32[2,4,512]{2,1,0:T(4,128)} %param.15) | copy-start | bytes 49156
  72.8 110.7 %all-to-all-start = ((bf16[3,64,56,128]{3,2,0,1:T(8,128)(2,1)}), bf16[3,64,56,128]{3,2,0,1:T(8,128)(2,1)}, u32[]{:S(2)}, u32[]{:S(2)}) async-start(bf16[3,64,56,128]{3,2,0,1:T(8,128)(2,1)} %copy.24), calls=%async_computation | async-start | bytes 5505024 | tf_op jit(solution)/shard_map/all_to_all | solution.py:78
  106.1 271.1 %all-gather.5.cloned.1.call-start = ((), (), s32[]{:S(2)}) async-start(), calls=%async_computation.5 | async-start | bytes 6684672 | tf_op jit(solution)/shard_map/all_gather | solution.py:130
  187.4 2.5 copy-start.17
  187.4 6.4 %copy-start.11 = (pred[2,4,512]{2,1,0:T(4,128)(4,1)}, pred[2,4,512]{2,1,0:T(4,128)(4,1)S(1)}, u32[]{:S(2)}) copy-start(pred[2,4,512]{2,1,0:T(4,128)(4,1)S(1)} %get-tuple-element.467) | copy-start | bytes 12292 | tf_op jit(solution)/shard_map/while
  198.6 1.2 copy-start.1
  199.8 1.2 copy-start.2
  200.9 0.9 copy-start.8
  201.0 1.2 copy-start.7
  201.8 1.0 copy-start.3
  208.4 1.2 copy-start.1
  209.6 1.2 copy-start.2
  210.8 1.2 copy-start.7
  211.7 1.0 copy-start.3
  213.5 2.4 copy-start.12
  213.5 2.4 copy-start.18
  215.9 2.5 copy-start.17
  215.9 6.4 %copy-start.11 = (pred[2,4,512]{2,1,0:T(4,128)(4,1)}, pred[2,4,512]{2,1,0:T(4,128)(4,1)S(1)}, u32[]{:S(2)}) copy-start(pred[2,4,512]{2,1,0:T(4,128)(4,1)S(1)} %get-tuple-element.467) | copy-start | bytes 12292 | tf_op jit(solution)/shard_map/while
  227.0 1.2 copy-start.1
  228.2 1.2 copy-start.2
  229.4 1.2 copy-start.7
  230.3 1.0 copy-start.3
  236.8 1.2 copy-start.1
  238.0 1.2 copy-start.2
  239.2 1.2 copy-start.7
  240.1 1.0 copy-start.3
  241.9 2.4 copy-start.12
  241.9 2.4 copy-start.18
  244.3 2.5 copy-start.17
  244.3 6.4 %copy-start.11 = (pred[2,4,512]{2,1,0:T(4,128)(4,1)}, pred[2,4,512]{2,1,0:T(4,128)(4,1)S(1)}, u32[]{:S(2)}) copy-start(pred[2,4,512]{2,1,0:T(4,128)(4,1)S(1)} %get-tuple-element.467) | copy-start | bytes 12292 | tf_op jit(solution)/shard_map/while
  255.5 1.2 copy-start.1
  256.6 1.2 copy-start.2
  257.8 1.2 copy-start.7
  258.7 1.0 copy-start.3
  265.3 1.2 copy-start.1
  266.4 1.2 copy-start.2
  267.6 1.2 copy-start.7
  268.5 1.0 copy-start.3
  270.3 2.4 copy-start.12
  270.3 2.4 copy-start.18
  272.7 2.5 copy-start.17
  272.7 6.4 %copy-start.11 = (pred[2,4,512]{2,1,0:T(4,128)(4,1)}, pred[2,4,512]{2,1,0:T(4,128)(4,1)S(1)}, u32[]{:S(2)}) copy-start(pred[2,4,512]{2,1,0:T(4,128)(4,1)S(1)} %get-tuple-element.467) | copy-start | bytes 12292 | tf_op jit(solution)/shard_map/while
  283.9 1.2 copy-start.1
  285.0 1.2 copy-start.2
  286.2 1.2 copy-start.7
  287.1 1.0 copy-start.3
  293.7 1.2 copy-start.1
  294.9 1.2 copy-start.2
  296.0 1.2 copy-start.7
  296.9 1.0 copy-start.3
  298.7 2.4 copy-start.12
  298.7 2.4 copy-start.18
  301.1 27.4 %copy-start.16 = (s32[4]{0:T(128)S(1)}, s32[4]{0:T(128)}, u32[]{:S(2)}) copy-start(s32[4]{0:T(128)} %param.16) | copy-start | bytes 52
  301.1 63.8 %all-to-all-start.2 = ((bf16[2,4,896,128]{3,0,1,2:T(2,128)(2,1)}), bf16[2,4,896,128]{3,0,1,2:T(2,128)(2,1)}, u32[]{:S(2)}, u32[]{:S(2)}) async-start(bf16[2,4,896,128]{3,0,1,2:T(2,128)(2,1)} %bitcast.168), calls=%async_computation.2 | async-start | bytes 3670016 | tf_op jit(solution)/shard_map/all_to_all | solution.py:120
  328.2 210.1 %reduce-scatter.2.cloned.1.call-start = ((), (), s32[]{:S(2)}) async-start(), calls=%async_computation.6 | async-start | bytes 13369344 | tf_op jit(solution)/shard_map/reduce_scatter | solution.py:153
  368.8 3.6 copy-start.5
  377.3 5.1 copy-start.10
  377.3 5.3 copy-start.13
  377.3 5.4 copy-start.14
  382.7 2.9 copy-start.9
  389.8 1.8 copy-start.6
  (15 other events, 12.5 us)
Sparse Core Ops, SparseCore 0:
  9.6 98.0 all-gather.2
  110.0 94.7 all-gather.4
  398.2 140.1 reduce-scatter.1
where the time goes:
time: 547 us; the launch traced here: 545 us
  waiting for transfers between devices  300 us (55%)
  matrix products  71 us (13%)
  starting transfers between devices  68.2 us (12%)
  local copies, waits for them, and re-layouts  63.1 us (12%)
  other arithmetic  20.9 us (4%)
  between operations  13.3 us (2%)
  loops' own time  8.68 us (2%)
    reduce_scatter x1, waiting for transfers between devices, shards(): lax.psum_scatter(lax.dot_general(columns, cotangent_rows, (((0,), (0,)),...  140 us
    all_to_all x1, waiting for transfers between devices, shards(): lax.all_to_all(image_local, 'seq', split_axis=1, concat_axis=2, tiled=True)  72.9 us
    all_to_all x1, waiting for transfers between devices, shards(): lax.all_to_all(text_local, 'seq', split_axis=1, concat_axis=2, tiled=True)  49.5 us
    all_to_all x1, waiting for transfers between devices, shards(): lax.all_to_all(both_passes, 'seq', split_axis=2, concat_axis=1, tiled=True)  35.5 us
    all_to_all x1, starting transfers between devices, shards(): lax.all_to_all(image_local, 'seq', split_axis=1, concat_axis=2, tiled=True)  33.3 us
    all_to_all x1, starting transfers between devices, shards(): lax.all_to_all(both_passes, 'seq', split_axis=2, concat_axis=1, tiled=True)  27.2 us
    dot_general x16, matrix products, text_finish(): jnp.dot(queries, text_keys.T, preferred_element_type=jnp.float32) * factor  25.9 us
    while x128, local copies, waits for them, and re-layouts  12.1 us
  transfers between devices with their start and end apart: 6, of which 4 were waited for; matrix products, arithmetic and copies ran while one was open for 22% of the time, Pallas kernels for 0%

commit v1 on v0

v1 whole, which is shorter than its diff:
```python
import functools
import math

import jax
import jax.numpy as jnp
from jax import lax
from jax.experimental import pallas as pl
from jax.experimental.pallas import tpu as pltpu
from jax.sharding import PartitionSpec as P

SAMPLES = 4
HEADS = 16
HEAD_DIM = 128
WIDTH = 1536
TIME_DIM = 256
LOG2E = math.log2(math.e)


def attention_kernel(image_dev, text_dev, block_rows, x_ref, live_ref, out_ref, q_s, k_s, v_s, tk_s, tv_s):
    sources = x_ref.shape[0]
    image_all = sources * image_dev
    text_all = sources * text_dev
    block = pl.program_id(1)

    @pl.when(block == 0)
    def _():
        def rows(start, count):
            piece = x_ref[:, 0, start:start + count, :].astype(jnp.float32)
            return piece.reshape(sources * count, HEAD_DIM).astype(jnp.bfloat16)

        ones_image = jnp.ones((image_all, HEAD_DIM), jnp.bfloat16)
        ones_text = jnp.ones((text_all, HEAD_DIM), jnp.bfloat16)
        for p in range(2):
            tk_s[p] = rows(2 * p * text_dev, text_dev)
            tv_s[p, :, :HEAD_DIM] = rows((2 * p + 1) * text_dev, text_dev)
            tv_s[p, :, HEAD_DIM:] = ones_text
        base = 4 * text_dev
        q_s[...] = rows(base, image_dev)
        k_s[...] = rows(base + image_dev, image_dev)
        v_s[:, :HEAD_DIM] = rows(base + 2 * image_dev, image_dev)
        v_s[:, HEAD_DIM:] = ones_image

    factor = HEAD_DIM ** (-0.5) * LOG2E
    contract = (((1,), (1,)), ((), ()))
    start = pl.multiple_of(block * block_rows, 16)
    queries = q_s[pl.ds(start, block_rows), :]
    scores = lax.dot_general(queries, k_s[...], contract, preferred_element_type=jnp.float32)
    image_max = jnp.max(scores, axis=1, keepdims=True) * factor
    weights = jnp.exp2(scores * factor - image_max).astype(jnp.bfloat16)
    image_out = jnp.dot(weights, v_s[...], preferred_element_type=jnp.float32)
    for p in range(2):
        text = lax.dot_general(queries, tk_s[p], contract, preferred_element_type=jnp.float32)
        text = jnp.where(live_ref[0, p:p + 1, :] != 0, text * factor, -jnp.inf)
        pass_max = jnp.maximum(image_max, jnp.max(text, axis=1, keepdims=True))
        ratio = jnp.exp2(image_max - pass_max)
        text_weights = jnp.exp2(text - pass_max).astype(jnp.bfloat16)
        both = ratio * image_out + jnp.dot(text_weights, tv_s[p], preferred_element_type=jnp.float32)
        result = both[:, :HEAD_DIM] / both[:, HEAD_DIM:]
        out_ref[:, 0, p] = result.reshape(block_rows // image_dev, image_dev, HEAD_DIM).astype(out_ref.dtype)


def attend(gathered, live, image_dev, text_dev):
    sources, owned = gathered.shape[:2]
    rows = gathered.shape[2]
    image_all, text_all = sources * image_dev, sources * text_dev
    per_block = 4
    blocks = sources // per_block
    block_rows = per_block * image_dev
    scores_flops = 2 * image_all * (image_all + 2 * text_all) * HEAD_DIM
    return pl.pallas_call(
        functools.partial(attention_kernel, image_dev, text_dev, block_rows),
        grid=(owned, blocks),
        in_specs=[
            pl.BlockSpec((sources, 1, rows, HEAD_DIM), lambda j, i: (0, j, 0, 0)),
            pl.BlockSpec((1, 2, text_all), lambda j, i: (j, 0, 0)),
        ],
        out_specs=pl.BlockSpec((per_block, 1, 2, image_dev, HEAD_DIM), lambda j, i: (i, j, 0, 0, 0)),
        out_shape=jax.ShapeDtypeStruct((sources, owned, 2, image_dev, HEAD_DIM), jnp.bfloat16),
        scratch_shapes=[
            pltpu.VMEM((image_all, HEAD_DIM), jnp.bfloat16),
            pltpu.VMEM((image_all, HEAD_DIM), jnp.bfloat16),
            pltpu.VMEM((image_all, 2 * HEAD_DIM), jnp.bfloat16),
            pltpu.VMEM((2, text_all, HEAD_DIM), jnp.bfloat16),
            pltpu.VMEM((2, text_all, 2 * HEAD_DIM), jnp.bfloat16),
        ],
        compiler_params=pltpu.CompilerParams(
            dimension_semantics=("arbitrary", "arbitrary"), vmem_limit_bytes=48 << 20
        ),
        cost_estimate=pl.CostEstimate(
            flops=2 * owned * scores_flops,
            bytes_accessed=2 * gathered.size + 4 * owned * image_all * HEAD_DIM,
            transcendentals=owned * image_all * (image_all + 2 * text_all),
        ),
        name="attention",
    )(gathered, live)


def head_out(branch, states, gate, scale, final_head):
    mixed = states.astype(jnp.float32) + gate[:, None, :] * branch
    normed = (
        mixed
        * lax.rsqrt(jnp.mean(mixed * mixed, axis=-1, keepdims=True) + 1e-06)
        * (1.0 + scale[:, None, :])
    )
    normed = normed.astype(jnp.bfloat16)
    return jnp.einsum("bic,cd->bid", normed, final_head, preferred_element_type=jnp.float32)


def shards(
    image_qkv,
    text_kv,
    prompt_ids,
    timesteps,
    image_states,
    frozen_out,
    trainee_out,
    time_mod,
    final_head,
):
    group_size = lax.axis_size("seq")
    position = lax.axis_index("seq")
    image_dev = image_qkv.shape[3]
    text_dev = text_kv.shape[4]
    owned = SAMPLES * HEADS // group_size
    token_rows = SAMPLES * image_dev
    image_items = image_qkv.transpose(2, 1, 0, 3, 4).reshape(group_size, owned, 3 * image_dev, HEAD_DIM)
    text_items = text_kv.transpose(3, 2, 0, 1, 4, 5).reshape(group_size, owned, 4 * text_dev, HEAD_DIM)
    packed = jnp.concatenate([text_items, image_items], axis=2)
    gathered = lax.all_to_all(packed, "seq", split_axis=0, concat_axis=0, tiled=True)
    sample_of = (position * owned + jnp.arange(owned, dtype=jnp.int32)) % SAMPLES
    live = jnp.take(prompt_ids, sample_of, axis=1).transpose(1, 0, 2)
    live = (live != 0).astype(jnp.int32)
    both = attend(gathered, live, image_dev, text_dev)
    returned = lax.all_to_all(both, "seq", split_axis=0, concat_axis=0, tiled=True)
    attention = returned.reshape(HEADS, SAMPLES, 2, image_dev, HEAD_DIM).transpose(2, 1, 3, 0, 4)
    attention = attention.reshape(2, token_rows, HEADS * HEAD_DIM)
    half_dim = TIME_DIM // 2
    freqs = jnp.exp(-math.log(10000.0) * jnp.arange(half_dim, dtype=jnp.float32) / half_dim)
    angles = timesteps.astype(jnp.float32)[:, None] * freqs[None, :]
    embedding = jnp.concatenate([jnp.cos(angles), jnp.sin(angles)], 1)
    modulation = jnp.dot(embedding, time_mod.astype(jnp.float32), precision=lax.Precision.HIGHEST)
    gate = modulation[:, :WIDTH]
    scale = modulation[:, WIDTH:]
    piece_frozen = lax.all_gather(frozen_out, "seq", axis=0, tiled=True)
    piece_trainee = lax.all_gather(trainee_out, "seq", axis=0, tiled=True)
    columns_c = attention[0]
    columns_n = attention[1]
    branch_c = jnp.dot(columns_c, piece_frozen, preferred_element_type=jnp.float32)
    branch_n = jnp.dot(columns_n, piece_frozen, preferred_element_type=jnp.float32)
    branch_s = jnp.dot(columns_c, piece_trainee, preferred_element_type=jnp.float32)
    branch_c = branch_c.reshape(SAMPLES, image_dev, WIDTH)
    branch_n = branch_n.reshape(SAMPLES, image_dev, WIDTH)
    branch_s = branch_s.reshape(SAMPLES, image_dev, WIDTH)
    velocity_c = head_out(branch_c, image_states, gate, scale, final_head)
    velocity_n = head_out(branch_n, image_states, gate, scale, final_head)
    target = velocity_n - (velocity_c - velocity_n)

    def student(branch):
        velocity_s = head_out(branch, image_states, gate, scale, final_head)
        return jnp.sum((velocity_s - target) ** 2) / SAMPLES

    loss_part, pull = jax.vjp(student, branch_s)
    (cotangent,) = pull(jnp.ones_like(loss_part))
    cotangent_rows = cotangent.astype(jnp.bfloat16).reshape(token_rows, WIDTH)
    partial = lax.dot_general(
        columns_c, cotangent_rows, (((0,), (0,)), ((), ())), preferred_element_type=jnp.float32
    ).astype(jnp.bfloat16)
    total = lax.psum_scatter(partial, "seq", scatter_dimension=0, tiled=True)
    return total.astype(jnp.float32)


def solution(mesh):
    return jax.shard_map(
        shards,
        mesh=mesh,
        in_specs=(
            P(None, "grp", None, "seq", None),
            P(None, None, "grp", None, "seq", None),
            P(None, "grp", None),
            P("grp"),
            P("grp", "seq", None),
            P("seq", None),
            P(("grp", "seq"), None),
            P(),
            P(),
        ),
        out_specs=P(("grp", "seq"), None),
        check_vma=False,
    )
```

time: 547 us -> 376 us (0.69)
  local copies, waits for them, and re-layouts: 63.1 us -> 10.7 us
  matrix products: 71 us -> 22.2 us
  waiting for transfers between devices: 300 us -> 259 us
  starting transfers between devices: 68.2 us -> 43 us
  Pallas kernels: 0 us -> 20.9 us
  other arithmetic: 20.9 us -> 6.61 us
  loops' own time: 8.68 us -> 0 us
    dot_general x50 -> x1, matrix products: 53.3 us -> 4.54 us  [shards(): lax.dot_general(columns_c, cotangent_rows, (((0,), (0,)), ((), ())), pref...]
    reduce_scatter x1, waiting for transfers between devices: 140 us -> 91.6 us  [shards(): total = lax.psum_scatter(partial, 'seq', scatter_dimension=0, tiled=True)]
    all_to_all x3 -> x2, starting transfers between devices: 67.9 us -> 42.7 us  [the longest x1 35.2 us: shards(): lax.all_to_all(both, 'seq', split_axis=0, concat_axis=0, tiled=True)]
    pallas_call x0 -> x1, Pallas kernels: none -> 20.9 us  [attend(): pl.pallas_call(functools.partial(attention_kernel, image_dev, text_dev, b...]
    while x128 -> x0, local copies, waits for them, and re-layouts: 12.1 us -> none
    all_to_all x3 -> x0, local copies, waits for them, and re-layouts: 10.1 us -> none  [the longest x1 3.97 us: shards(): lax.all_to_all(image_local, 'seq', split_axis=1, concat_axis=2, tiled=True)]
    dynamic_slice x12 -> x0, local copies, waits for them, and re-layouts: 9.79 us -> none  [the longest x4 7.4 us: per_block(): text_heads[3, item_index]]
    another operation x20 -> x0, other arithmetic: 9.54 us -> none
  transfers between devices with their start and end apart: 6 -> 5, of which waited for: 4 -> 3; matrix products, arithmetic and copies ran while one was open for 22% -> 5% of each run, Pallas kernels for 0% -> 6%
where the time goes in v1:
time: 376 us; the launch traced here: 375 us
  waiting for transfers between devices  259 us (69%)
  starting transfers between devices  43 us (11%)
  matrix products  22.2 us (6%)
  Pallas kernels  20.9 us (6%)
  between operations  13.3 us (4%)
  local copies, waits for them, and re-layouts  10.7 us (3%)
  other arithmetic  6.61 us (2%)
    all_to_all x1, waiting for transfers between devices, shards(): lax.all_to_all(packed, 'seq', split_axis=0, concat_axis=0, tiled=True)  126 us
    reduce_scatter x1, waiting for transfers between devices, shards(): total = lax.psum_scatter(partial, 'seq', scatter_dimension=0, tiled=True)  91.6 us
    all_to_all x1, waiting for transfers between devices, shards(): lax.all_to_all(both, 'seq', split_axis=0, concat_axis=0, tiled=True)  39.7 us
    all_to_all x1, starting transfers between devices, shards(): lax.all_to_all(both, 'seq', split_axis=0, concat_axis=0, tiled=True)  35.2 us
    pallas_call x1, Pallas kernels, attend(): pl.pallas_call(functools.partial(attention_kernel, image_dev, text_dev, b...  20.9 us
    all_to_all x1, starting transfers between devices, shards(): lax.all_to_all(packed, 'seq', split_axis=0, concat_axis=0, tiled=True)  7.56 us
  transfers between devices with their start and end apart: 5, of which 3 were waited for; matrix products, arithmetic and copies ran while one was open for 5% of the time, Pallas kernels for 6%

profile of v1, /device:TPU:0, one launch (start us, length us, event | category | flops | bytes accessed | tf_op | source)
XLA Modules:
  0.0 375.4 jit_solution(16916648188682381010)
XLA Ops:
  6.5 0.0 copy-start
  6.5 0.0 all-gather.3.cloned.1.call-start
  6.5 0.7 all-gather.3.cloned.1.call-update
  7.3 0.0 copy-start.5
  7.3 2.4 copy.13
  9.7 0.0 copy-done.5
  9.7 0.6 copy.12
  10.3 2.6 pad_maximum_fusion
  12.8 0.0 copy-start.6
  12.8 7.6 %all-to-all-start = ((bf16[16,4,296,128]{3,2,1,0:T(8,128)(2,1)}), bf16[16,4,296,128]{3,2,1,0:T(8,128)(2,1)}, u32[]{:S(2)}, u32[]{:S(2)}) async-start(bf16[16,4,296,128]{3,2,1,0:T(8,128)(2,1)} %pad_maximum_fusion), calls=%async_computation | async-start | bytes 9699328 | tf_op jit(solution)/shard_map/all_to_all | solution.py:129
  20.4 0.0 all-gather.5.cloned.1.call-start
  20.5 0.7 all-gather.5.cloned.1.call-update
  21.2 0.0 copy-done.6
  21.2 0.6 gather_fusion
  21.8 0.1 compare_convert_fusion.live_ref
  21.9 125.8 %all-to-all-done.x_ref = bf16[16,4,296,128]{3,2,1,0:T(8,128)(2,1)} async-done(((bf16[16,4,296,128]{3,2,1,0:T(8,128)(2,1)}), bf16[16,4,296,128]{3,2,1,0:T(8,128)(2,1)}, u32[]{:S(2)}, u32[]{:S(2)}) %all-to-all-start) | async-done | bytes 4849696 | tf_op jit(solution)/shard_map/all_to_all | solution.py:129
  147.7 20.9 %attention.1 = bf16[16,4,2,56,128]{4,3,2,1,0:T(8,128)(2,1)} custom-call(bf16[16,4,296,128]{3,2,1,0:T(8,128)(2,1)} %all-to-all-done.x_ref, s32[4,2,512]{2,1,0:T(2,128)S(1)} %compare_convert_fusion.live_ref), custom_call_target="tpu_custom_call" | custom-call | flops 3523215360 | bytes 6684672 | tf_op jit(solution)/shard_map/attention/pallas_call | solution.py:70
  168.6 0.0 copy-start.10
  168.6 35.2 %all-to-all-start.1 = ((bf16[16,4,2,56,128]{4,3,2,1,0:T(8,128)(2,1)}), bf16[16,4,2,56,128]{4,3,2,1,0:T(8,128)(2,1)S(1)}, u32[]{:S(2)}, u32[]{:S(2)}) async-start(bf16[16,4,2,56,128]{4,3,2,1,0:T(8,128)(2,1)} %attention.1), calls=%async_computation.1 | async-start | bytes 3670016 | tf_op jit(solution)/shard_map/all_to_all | solution.py:134
  203.8 0.2 reduce-scatter.2.cloned.1.call-start
  204.0 0.0 copy-done.10
  204.1 0.1 multiply_cosine_fusion
  204.2 0.0 copy-done
  204.2 0.7 fusion.48
  204.9 39.7 %all-to-all-done.1 = bf16[16,4,2,56,128]{4,3,2,1,0:T(8,128)(2,1)S(1)} async-done(((bf16[16,4,2,56,128]{4,3,2,1,0:T(8,128)(2,1)}), bf16[16,4,2,56,128]{4,3,2,1,0:T(8,128)(2,1)S(1)}, u32[]{:S(2)}, u32[]{:S(2)}) %all-to-all-start.1) | async-done | bytes 1835040 | tf_op jit(solution)/shard_map/all_to_all | solution.py:134
  244.7 1.1 fusion.58
  245.7 0.4 copy.15
  246.1 0.0 copy-start.1
  246.1 0.0 copy-start.3
  246.1 1.3 dot_general.32
  247.4 0.5 copy-done.3
  247.9 1.3 copy.17
  249.3 0.0 copy-done.1
  249.3 2.2 dot_general.35
  251.5 0.0 all-gather.3.cloned.1.call-done
  251.5 4.9 %multiply_reduce_fusion.3 = (f32[4,56]{1,0:T(4,128)S(1)}, f32[4,56,1536]{2,1,0:T(8,128)S(1)}) fusion(bf16[4,56,2048]{2,1,0:T(8,128)(2,1)} %dot_general.32, bf16[2048,1536]{1,0:T(8,128)(2,1)} %all-gather.3.cloned.1.call-done, f32[4,1536]{1,0:T(4,128)S(1)} %get-tuple-element.8, bf16[4,56,1536]{2,1,0:T(8,128)(2,1)} %param.13), kind=kOutput, calls=%fused_computation.27 | convolution fusion | flops 1411006208 | bytes 9298816 | tf_op jit(solution)/shard_map/dot_general | solution.py:150
  256.4 0.0 all-gather.5.cloned.1.call-done
  256.4 0.0 copy-start.7
  256.4 0.0 copy-start.8
  256.4 0.0 copy-start.9
  256.5 5.0 %multiply_reduce_fusion.2 = (f32[4,56]{1,0:T(4,128)S(1)}, f32[4,56,1536]{2,1,0:T(8,128)S(1)}) fusion(bf16[4,56,2048]{2,1,0:T(8,128)(2,1)} %dot_general.35, bf16[2048,1536]{1,0:T(8,128)(2,1)} %all-gather.5.cloned.1.call-done, f32[4,1536]{1,0:T(4,128)S(1)} %get-tuple-element.8, bf16[4,56,1536]{2,1,0:T(8,128)(2,1)} %param.13), kind=kOutput, calls=%fused_computation.25 | convolution fusion | flops 1411006208 | bytes 9298816 | tf_op jit(solution)/shard_map/dot_general | solution.py:149
  261.5 0.0 copy-done.7
  261.5 0.3 copy-done.8
  261.8 0.1 copy-done.9
  261.9 0.0 copy-start.4
  261.9 2.8 multiply_reduce_fusion.1
  264.6 0.0 copy-done.4
  264.6 0.4 fusion.33
  265.0 0.4 fusion.34
  265.5 3.4 multiply_reduce_fusion
  268.9 0.0 copy-start.2
  268.9 1.8 fusion.27
  270.7 0.0 copy-done.2
  270.7 4.5 %convolution_convert_fusion = bf16[2048,1536]{1,0:T(8,128)(2,1)} fusion(bf16[224,1536]{1,0:T(8,128)(2,1)S(1)} %bitcast.65, bf16[28,8,16,128]{3,2,1,0:T(8,128)(2,1)S(1)} %bitcast.61), kind=kOutput, calls=%fused_computation.1 | convolution fusion | flops 1412431872 | bytes 7897088 | tf_op jit(solution)/shard_map/dot_general | solution.py:165
  275.2 0.0 reduce-scatter.2.cloned.1.call-update
  275.3 91.6 %reduce-scatter.2.cloned.1.call-done = bf16[128,1536]{1,0:T(8,128)(2,1)} async-done(((bf16[2048,1536]{1,0:T(8,128)(2,1)}), bf16[128,1536]{1,0:T(8,128)(2,1)}) %reduce-scatter.2.cloned.1.call-update) | async-done | bytes 393232 | tf_op jit(solution)/shard_map/reduce_scatter | solution.py:168
  366.9 2.0 convert_element_type.49
  (10 shorter events, 0.1 us)
Async XLA Ops:
  6.5 197.7 %copy-start = (bf16[256,3072]{1,0:T(8,128)(2,1)S(1)}, bf16[256,3072]{1,0:T(8,128)(2,1)}, u32[]{:S(2)}) copy-start(bf16[256,3072]{1,0:T(8,128)(2,1)} %param.16) | copy-start | bytes 4718596
  6.5 244.9 %all-gather.3.cloned.1.call-start = ((), (), s32[]{:S(2)}) async-start(), calls=%async_computation.3 | async-start | bytes 6684672 | tf_op jit(solution)/shard_map/all_gather | solution.py:145
  7.3 2.4 copy-start.5
  12.8 8.4 %copy-start.6 = (s32[2,4,512]{2,1,0:T(4,128)S(1)}, s32[2,4,512]{2,1,0:T(4,128)}, u32[]{:S(2)}) copy-start(s32[2,4,512]{2,1,0:T(4,128)} %param.11) | copy-start | bytes 49156
  12.8 134.9 %all-to-all-start = ((bf16[16,4,296,128]{3,2,1,0:T(8,128)(2,1)}), bf16[16,4,296,128]{3,2,1,0:T(8,128)(2,1)}, u32[]{:S(2)}, u32[]{:S(2)}) async-start(bf16[16,4,296,128]{3,2,1,0:T(8,128)(2,1)} %pad_maximum_fusion), calls=%async_computation | async-start | bytes 9699328 | tf_op jit(solution)/shard_map/all_to_all | solution.py:129
  20.4 236.0 %all-gather.5.cloned.1.call-start = ((), (), s32[]{:S(2)}) async-start(), calls=%async_computation.4 | async-start | bytes 6684672 | tf_op jit(solution)/shard_map/all_gather | solution.py:144
  168.6 35.4 %copy-start.10 = (s32[4]{0:T(128)S(1)}, s32[4]{0:T(128)}, u32[]{:S(2)}) copy-start(s32[4]{0:T(128)} %param.12) | copy-start | bytes 52
  168.6 76.0 %all-to-all-start.1 = ((bf16[16,4,2,56,128]{4,3,2,1,0:T(8,128)(2,1)}), bf16[16,4,2,56,128]{4,3,2,1,0:T(8,128)(2,1)S(1)}, u32[]{:S(2)}, u32[]{:S(2)}) async-start(bf16[16,4,2,56,128]{4,3,2,1,0:T(8,128)(2,1)} %attention.1), calls=%async_computation.1 | async-start | bytes 3670016 | tf_op jit(solution)/shard_map/all_to_all | solution.py:134
  203.8 163.1 %reduce-scatter.2.cloned.1.call-start = ((), (), s32[]{:S(2)}) async-start(), calls=%async_computation.5 | async-start | bytes 6684672 | tf_op jit(solution)/shard_map/reduce_scatter | solution.py:168
  246.1 3.2 copy-start.1
  246.1 1.8 copy-start.3
  256.4 5.1 %copy-start.7 = (bf16[4,56,2048]{2,1,0:T(8,128)(2,1)S(1)}, bf16[4,56,2048]{2,1,0:T(8,128)(2,1)}, u32[]{:S(2)}) copy-start(bf16[4,56,2048]{2,1,0:T(8,128)(2,1)} %dot_general.32) | copy-start | bytes 2752516
  256.4 5.3 %copy-start.8 = (bf16[2048,1536]{1,0:T(8,128)(2,1)S(1)}, bf16[2048,1536]{1,0:T(8,128)(2,1)}, u32[]{:S(2)}) copy-start(bf16[2048,1536]{1,0:T(8,128)(2,1)} %all-gather.5.cloned.1.call-done) | copy-start | bytes 18874372
  256.4 5.4 %copy-start.9 = (bf16[4,56,1536]{2,1,0:T(8,128)(2,1)S(1)}, bf16[4,56,1536]{2,1,0:T(8,128)(2,1)}, u32[]{:S(2)}) copy-start(bf16[4,56,1536]{2,1,0:T(8,128)(2,1)} %param.13) | copy-start | bytes 2064388
  261.9 2.8 copy-start.4
  268.9 1.8 copy-start.2
Sparse Core Ops, SparseCore 0:
  9.6 133.4 all-gather.2
  145.4 81.8 all-gather.4
  275.4 91.4 reduce-scatter.1

commit v2 on v1

--- a/solution.py
+++ b/solution.py
@@ -13,6 +13,7 @@
 HEAD_DIM = 128
 WIDTH = 1536
 TIME_DIM = 256
+CHUNKS = 2
 LOG2E = math.log2(math.e)
 
 
@@ -95,15 +96,102 @@
     )(gathered, live)
 
 
-def head_out(branch, states, gate, scale, final_head):
-    mixed = states.astype(jnp.float32) + gate[:, None, :] * branch
-    normed = (
-        mixed
-        * lax.rsqrt(jnp.mean(mixed * mixed, axis=-1, keepdims=True) + 1e-06)
-        * (1.0 + scale[:, None, :])
-    )
-    normed = normed.astype(jnp.bfloat16)
-    return jnp.einsum("bic,cd->bid", normed, final_head, preferred_element_type=jnp.float32)
+def head_kernel(
+    samples, image_dev, back_ref, frozen_ref, trainee_ref, states_ref, gate_ref, scale_ref, head_ref,
+    cot_ref, att_ref, both_s, mixed_s, square_s,
+):
+    step = pl.program_id(0)
+    rows = samples * image_dev
+    width = frozen_ref.shape[1]
+
+    @pl.when(step == 0)
+    def _():
+        for h in range(HEADS):
+            for p in range(2):
+                piece = back_ref[h, :, p].astype(jnp.float32).reshape(rows, HEAD_DIM)
+                both_s[p * rows:(p + 1) * rows, h * HEAD_DIM:(h + 1) * HEAD_DIM] = piece.astype(jnp.bfloat16)
+        square_s[...] = jnp.zeros_like(square_s)
+
+    def spread(values):
+        return jnp.concatenate(
+            [jnp.broadcast_to(values[b:b + 1, :], (image_dev, values.shape[1])) for b in range(samples)], axis=0
+        )
+
+    columns = pl.ds(pl.multiple_of(step * width, 128), width)
+    states = states_ref[:, :, columns].astype(jnp.float32).reshape(rows, width)
+    gate = spread(gate_ref[:, columns])
+    frozen = jnp.dot(both_s[...], frozen_ref[...], preferred_element_type=jnp.float32)
+    trainee = jnp.dot(both_s[:rows, :], trainee_ref[...], preferred_element_type=jnp.float32)
+    for k, branch in enumerate((frozen[:rows], frozen[rows:], trainee)):
+        mixed = states + gate * branch
+        mixed_s[k, :, columns] = mixed
+        square = mixed * mixed
+        total = square[:, :128]
+        for c in range(1, width // 128):
+            total = total + square[:, c * 128:(c + 1) * 128]
+        square_s[k] += total
+
+    @pl.when(step == pl.num_programs(0) - 1)
+    def _():
+        lift = 1.0 + spread(scale_ref[...])
+        velocities = []
+        for k in range(3):
+            mean = jnp.sum(square_s[k], axis=1, keepdims=True) * (1.0 / WIDTH)
+            root = lax.rsqrt(mean + 1e-06)
+            normed = (mixed_s[k] * root * lift).astype(jnp.bfloat16)
+            velocities.append(jnp.dot(normed, head_ref[...], preferred_element_type=jnp.float32))
+        velocity_c, velocity_n, velocity_s = velocities
+        target = velocity_n - (velocity_c - velocity_n)
+        pull = (velocity_s - target) * (2.0 / SAMPLES)
+        high = pull.astype(jnp.bfloat16)
+        low = (pull - high.astype(jnp.float32)).astype(jnp.bfloat16)
+        contract = (((1,), (1,)), ((), ()))
+        inner = lax.dot_general(high, head_ref[...], contract, preferred_element_type=jnp.float32)
+        inner += lax.dot_general(low, head_ref[...], contract, preferred_element_type=jnp.float32)
+        inner = inner * lift
+        mixed = mixed_s[2]
+        along = jnp.sum(inner * mixed, axis=1, keepdims=True) * (1.0 / WIDTH)
+        cot = root * inner - mixed * (root * root * root * along)
+        cot_ref[...] = (cot * spread(gate_ref[...])).astype(cot_ref.dtype)
+        att_ref[...] = both_s[:rows, :]
+
+
+def project(back, frozen, trainee, states, gate, scale, final_head):
+    samples, image_dev = states.shape[:2]
+    rows = samples * image_dev
+    inner = frozen.shape[0]
+    width = 256
+    whole = lambda shape: pl.BlockSpec(shape, lambda n: (0,) * len(shape))
+    return pl.pallas_call(
+        functools.partial(head_kernel, samples, image_dev),
+        grid=(WIDTH // width,),
+        in_specs=[
+            whole(back.shape),
+            pl.BlockSpec((inner, width), lambda n: (0, n)),
+            pl.BlockSpec((inner, width), lambda n: (0, n)),
+            whole(states.shape),
+            whole(gate.shape),
+            whole(scale.shape),
+            whole(final_head.shape),
+        ],
+        out_specs=[whole((rows, WIDTH)), whole((rows, inner))],
+        out_shape=[
+            jax.ShapeDtypeStruct((rows, WIDTH), jnp.bfloat16),
+            jax.ShapeDtypeStruct((rows, inner), jnp.bfloat16),
+        ],
+        scratch_shapes=[
+            pltpu.VMEM((2 * rows, inner), jnp.bfloat16),
+            pltpu.VMEM((3, rows, WIDTH), jnp.float32),
+            pltpu.VMEM((3, rows, 128), jnp.float32),
+        ],
+        compiler_params=pltpu.CompilerParams(dimension_semantics=("arbitrary",), vmem_limit_bytes=40 << 20),
+        cost_estimate=pl.CostEstimate(
+            flops=6 * rows * inner * WIDTH,
+            bytes_accessed=4 * inner * WIDTH + 4 * rows * inner,
+            transcendentals=3 * rows,
+        ),
+        name="project",
+    )(back, frozen, trainee, states, gate, scale, final_head)
 
 
 def shards(
@@ -122,18 +210,11 @@
     image_dev = image_qkv.shape[3]
     text_dev = text_kv.shape[4]
     owned = SAMPLES * HEADS // group_size
-    token_rows = SAMPLES * image_dev
     image_items = image_qkv.transpose(2, 1, 0, 3, 4).reshape(group_size, owned, 3 * image_dev, HEAD_DIM)
     text_items = text_kv.transpose(3, 2, 0, 1, 4, 5).reshape(group_size, owned, 4 * text_dev, HEAD_DIM)
-    packed = jnp.concatenate([text_items, image_items], axis=2)
-    gathered = lax.all_to_all(packed, "seq", split_axis=0, concat_axis=0, tiled=True)
     sample_of = (position * owned + jnp.arange(owned, dtype=jnp.int32)) % SAMPLES
     live = jnp.take(prompt_ids, sample_of, axis=1).transpose(1, 0, 2)
     live = (live != 0).astype(jnp.int32)
-    both = attend(gathered, live, image_dev, text_dev)
-    returned = lax.all_to_all(both, "seq", split_axis=0, concat_axis=0, tiled=True)
-    attention = returned.reshape(HEADS, SAMPLES, 2, image_dev, HEAD_DIM).transpose(2, 1, 3, 0, 4)
-    attention = attention.reshape(2, token_rows, HEADS * HEAD_DIM)
     half_dim = TIME_DIM // 2
     freqs = jnp.exp(-math.log(10000.0) * jnp.arange(half_dim, dtype=jnp.float32) / half_dim)
     angles = timesteps.astype(jnp.float32)[:, None] * freqs[None, :]
@@ -141,29 +222,31 @@
     modulation = jnp.dot(embedding, time_mod.astype(jnp.float32), precision=lax.Precision.HIGHEST)
     gate = modulation[:, :WIDTH]
     scale = modulation[:, WIDTH:]
-    piece_frozen = lax.all_gather(frozen_out, "seq", axis=0, tiled=True)
-    piece_trainee = lax.all_gather(trainee_out, "seq", axis=0, tiled=True)
-    columns_c = attention[0]
-    columns_n = attention[1]
-    branch_c = jnp.dot(columns_c, piece_frozen, preferred_element_type=jnp.float32)
-    branch_n = jnp.dot(columns_n, piece_frozen, preferred_element_type=jnp.float32)
-    branch_s = jnp.dot(columns_c, piece_trainee, preferred_element_type=jnp.float32)
-    branch_c = branch_c.reshape(SAMPLES, image_dev, WIDTH)
-    branch_n = branch_n.reshape(SAMPLES, image_dev, WIDTH)
-    branch_s = branch_s.reshape(SAMPLES, image_dev, WIDTH)
-    velocity_c = head_out(branch_c, image_states, gate, scale, final_head)
-    velocity_n = head_out(branch_n, image_states, gate, scale, final_head)
-    target = velocity_n - (velocity_c - velocity_n)
-
-    def student(branch):
-        velocity_s = head_out(branch, image_states, gate, scale, final_head)
-        return jnp.sum((velocity_s - target) ** 2) / SAMPLES
-
-    loss_part, pull = jax.vjp(student, branch_s)
-    (cotangent,) = pull(jnp.ones_like(loss_part))
-    cotangent_rows = cotangent.astype(jnp.bfloat16).reshape(token_rows, WIDTH)
+    chunks = CHUNKS if owned == SAMPLES else 1
+    items = owned // chunks
+    samples = SAMPLES // chunks
+    exchange = functools.partial(lax.all_to_all, axis_name="seq", split_axis=0, concat_axis=0, tiled=True)
+    gathered = []
+    for c in range(chunks):
+        own = slice(c * items, (c + 1) * items)
+        gathered.append(exchange(jnp.concatenate([text_items[:, own], image_items[:, own]], axis=2)))
+    all_frozen = lax.all_gather(frozen_out, "seq", axis=0, tiled=True)
+    all_trainee = lax.all_gather(trainee_out, "seq", axis=0, tiled=True)
+    cotangents, columns = [], []
+    for c in range(chunks):
+        both = attend(gathered[c], live[c * items:(c + 1) * items], image_dev, text_dev)
+        back = exchange(both).reshape(HEADS, samples, 2, image_dev, HEAD_DIM)
+        part = slice(c * samples, (c + 1) * samples)
+        cot, att = project(
+            back, all_frozen, all_trainee, image_states[part], gate[part], scale[part], final_head
+        )
+        cotangents.append(cot)
+        columns.append(att)
     partial = lax.dot_general(
-        columns_c, cotangent_rows, (((0,), (0,)), ((), ())), preferred_element_type=jnp.float32
+        jnp.concatenate(columns),
+        jnp.concatenate(cotangents),
+        (((0,), (0,)), ((), ())),
+        preferred_element_type=jnp.float32,
     ).astype(jnp.bfloat16)
     total = lax.psum_scatter(partial, "seq", scatter_dimension=0, tiled=True)
     return total.astype(jnp.float32)

time: 376 us -> 377 us (level)
  waiting for transfers between devices: 259 us -> 239 us
  matrix products: 22.2 us -> 5.19 us
  Pallas kernels: 20.9 us -> 37.4 us
  starting transfers between devices: 43 us -> 54 us
  local copies, waits for them, and re-layouts: 10.7 us -> 19.9 us
    dot_general x7 -> x1, matrix products: 21.4 us -> 4.47 us  [shards(): lax.dot_general(jnp.concatenate(columns), jnp.concatenate(cotangents), ((...]
    pallas_call x0 -> x2, Pallas kernels: none -> 15.4 us  [project(): pl.pallas_call(functools.partial(head_kernel, samples, image_dev), grid=(...]
    all_to_all x2 -> x4, waiting for transfers between devices: 166 us -> 150 us  [the longest x2 138 us: shards(): exchange(jnp.concatenate([text_items[:, own], image_items[:, own]], axis=2))]
    unnamed x22 -> x33, local copies, waits for them, and re-layouts: 0.9 us -> 12.9 us
    all_to_all x2 -> x4, starting transfers between devices: 42.7 us -> 54 us  [the longest x2 28.4 us: shards(): back = exchange(both).reshape(HEADS, samples, 2, image_dev, HEAD_DIM)]
    reduce_scatter x1, waiting for transfers between devices: 91.6 us -> 87.3 us  [shards(): total = lax.psum_scatter(partial, 'seq', scatter_dimension=0, tiled=True)]
    pallas_call x1 -> x2, Pallas kernels: 20.9 us -> 22 us  [attend(): pl.pallas_call(functools.partial(attention_kernel, image_dev, text_dev, b...]
  transfers between devices with their start and end apart: 5 -> 7, of which waited for: 3 -> 5; matrix products, arithmetic and copies ran while one was open for 5% -> 4% of each run, Pallas kernels for 6% -> 8%
where the time goes in v2:
time: 377 us; the launch traced here: 375 us
  waiting for transfers between devices  239 us (63%)
  starting transfers between devices  54 us (14%)
  Pallas kernels  37.4 us (10%)
  local copies, waits for them, and re-layouts  19.9 us (5%)
  between operations  13.3 us (4%)
  other arithmetic  6.59 us (2%)
  matrix products  5.19 us (1%)
    all_to_all x2, waiting for transfers between devices, shards(): exchange(jnp.concatenate([text_items[:, own], image_items[:, own]], axis=2))  138 us
    reduce_scatter x1, waiting for transfers between devices, shards(): total = lax.psum_scatter(partial, 'seq', scatter_dimension=0, tiled=True)  87.3 us
    all_to_all x2, starting transfers between devices, shards(): back = exchange(both).reshape(HEADS, samples, 2, image_dev, HEAD_DIM)  28.4 us
    all_to_all x2, starting transfers between devices, shards(): exchange(jnp.concatenate([text_items[:, own], image_items[:, own]], axis=2))  25.6 us
    pallas_call x2, Pallas kernels, attend(): pl.pallas_call(functools.partial(attention_kernel, image_dev, text_dev, b...  22 us
    pallas_call x2, Pallas kernels, project(): pl.pallas_call(functools.partial(head_kernel, samples, image_dev), grid=(...  15.4 us
    unnamed x33, local copies, waits for them, and re-layouts  12.9 us
    all_to_all x2, waiting for transfers between devices, shards(): back = exchange(both).reshape(HEADS, samples, 2, image_dev, HEAD_DIM)  12.3 us
  transfers between devices with their start and end apart: 7, of which 5 were waited for; matrix products, arithmetic and copies ran while one was open for 4% of the time, Pallas kernels for 8%

profile of v2, /device:TPU:0, one launch (start us, length us, event | category | flops | bytes accessed | tf_op | source)
XLA Modules:
  0.0 375.5 jit_solution(3454541861836429124)
XLA Ops:
  6.5 0.0 copy-start
  6.5 0.0 all-gather.3.cloned.1.call-start
  6.5 0.7 all-gather.3.cloned.1.call-update
  7.3 0.0 copy-start.12
  7.3 2.4 copy.15
  9.7 0.0 copy-done.12
  9.7 0.7 copy.14
  10.3 1.1 fusion.16
  11.5 0.2 fusion.15
  11.7 1.6 pad_maximum_fusion
  13.2 7.4 %all-to-all-start = ((bf16[16,2,296,128]{3,2,1,0:T(8,128)(2,1)}), bf16[16,2,296,128]{3,2,1,0:T(8,128)(2,1)}, u32[]{:S(2)}, u32[]{:S(2)}) async-start(bf16[16,2,296,128]{3,2,1,0:T(8,128)(2,1)} %pad_maximum_fusion), calls=%async_computation | async-start | bytes 4849664 | tf_op jit(solution)/shard_map/all_to_all | solution.py:232
  20.7 0.0 all-gather.5.cloned.1.call-start
  20.7 0.7 all-gather.5.cloned.1.call-update
  21.4 2.8 pad_maximum_fusion.1
  24.2 0.0 copy-start.13
  24.3 75.3 %all-to-all-done.x_ref = bf16[16,2,296,128]{3,2,1,0:T(8,128)(2,1)} async-done(((bf16[16,2,296,128]{3,2,1,0:T(8,128)(2,1)}), bf16[16,2,296,128]{3,2,1,0:T(8,128)(2,1)}, u32[]{:S(2)}, u32[]{:S(2)}) %all-to-all-start) | async-done | bytes 2424864 | tf_op jit(solution)/shard_map/all_to_all | solution.py:232
  99.5 18.2 %all-to-all-start.2 = ((bf16[16,2,296,128]{3,2,1,0:T(8,128)(2,1)}), bf16[16,2,296,128]{3,2,1,0:T(8,128)(2,1)}, u32[]{:S(2)}, u32[]{:S(2)}) async-start(bf16[16,2,296,128]{3,2,1,0:T(8,128)(2,1)} %pad_maximum_fusion.1), calls=%async_computation.2 | async-start | bytes 4849664 | tf_op jit(solution)/shard_map/all_to_all | solution.py:232
  117.7 0.0 copy-done.13
  117.8 0.6 gather_fusion
  118.4 0.1 compare_convert_fusion
  118.5 0.0 copy-start.15
  118.5 0.0 copy-start.14
  118.5 11.4 %attention.2 = bf16[16,2,2,56,128]{4,3,2,1,0:T(8,128)(2,1)} custom-call(bf16[16,2,296,128]{3,2,1,0:T(8,128)(2,1)} %all-to-all-done.x_ref, s32[2,2,512]{2,1,0:T(2,128)S(1)} %get-tuple-element.23.live_ref), custom_call_target="tpu_custom_call" | custom-call | flops 1761607680 | bytes 3342336 | tf_op jit(solution)/shard_map/attention/pallas_call | solution.py:71
  129.9 62.8 %all-to-all-done.2.x_ref = bf16[16,2,296,128]{3,2,1,0:T(8,128)(2,1)} async-done(((bf16[16,2,296,128]{3,2,1,0:T(8,128)(2,1)}), bf16[16,2,296,128]{3,2,1,0:T(8,128)(2,1)}, u32[]{:S(2)}, u32[]{:S(2)}) %all-to-all-start.2) | async-done | bytes 2424864 | tf_op jit(solution)/shard_map/all_to_all | solution.py:232
  192.7 22.2 %all-to-all-start.1 = ((bf16[16,2,2,56,128]{4,3,2,1,0:T(8,128)(2,1)}), bf16[16,2,2,56,128]{4,3,2,1,0:T(8,128)(2,1)S(1)}, u32[]{:S(2)}, u32[]{:S(2)}) async-start(bf16[16,2,2,56,128]{4,3,2,1,0:T(8,128)(2,1)} %attention.2), calls=%async_computation.1 | async-start | bytes 1835008 | tf_op jit(solution)/shard_map/all_to_all | solution.py:238
  214.9 0.0 copy-done.15
  214.9 0.0 copy-done.14
  214.9 0.9 copy.17.head_ref
  215.8 10.6 %attention.3 = bf16[16,2,2,56,128]{4,3,2,1,0:T(8,128)(2,1)S(1)} custom-call(bf16[16,2,296,128]{3,2,1,0:T(8,128)(2,1)} %all-to-all-done.2.x_ref, s32[2,2,512]{2,1,0:T(2,128)S(1)} %get-tuple-element.24.live_ref), custom_call_target="tpu_custom_call" | custom-call | flops 1761607680 | bytes 3342336 | tf_op jit(solution)/shard_map/attention/pallas_call | solution.py:71
  226.4 0.0 copy-start.7
  226.4 0.9 copy-done.7
  227.4 8.4 %all-to-all-done.1.back_ref = bf16[16,2,2,56,128]{4,3,2,1,0:T(8,128)(2,1)S(1)} async-done(((bf16[16,2,2,56,128]{4,3,2,1,0:T(8,128)(2,1)}), bf16[16,2,2,56,128]{4,3,2,1,0:T(8,128)(2,1)S(1)}, u32[]{:S(2)}, u32[]{:S(2)}) %all-to-all-start.1) | async-done | bytes 917536 | tf_op jit(solution)/shard_map/all_to_all | solution.py:238
  235.7 6.2 %all-to-all-start.3 = ((bf16[16,2,2,56,128]{4,3,2,1,0:T(8,128)(2,1)}), bf16[16,2,2,56,128]{4,3,2,1,0:T(8,128)(2,1)S(1)}, u32[]{:S(2)}, u32[]{:S(2)}) async-start(bf16[16,2,2,56,128]{4,3,2,1,0:T(8,128)(2,1)} %copy-done.7), calls=%async_computation.3 | async-start | bytes 1835008 | tf_op jit(solution)/shard_map/all_to_all | solution.py:238
  241.9 0.0 reduce-scatter.2.cloned.1.call-start
  242.0 0.1 multiply_cosine_fusion
  242.1 0.0 copy-done
  242.1 0.7 fusion.6
  242.8 2.0 fusion.17
  244.8 0.0 all-gather.3.cloned.1.call-done.frozen_ref
  244.8 0.0 all-gather.5.cloned.1.call-done.trainee_ref
  244.8 0.0 copy-start.1
  244.8 2.8 copy-done.1
  247.6 0.0 copy-start.3
  247.6 1.0 copy-done.3
  248.6 0.0 copy-start.6
  248.6 1.0 copy-done.6
  249.6 7.7 %project.2 = (bf16[112,1536]{1,0:T(8,128)(2,1)S(1)}, bf16[112,2048]{1,0:T(8,128)(2,1)S(1)}) custom-call(bf16[16,2,2,56,128]{4,3,2,1,0:T(8,128)(2,1)S(1)} %all-to-all-done.1.back_ref, bf16[2048,1536]{1,0:T(8,128)(2,1)S(1)} %copy-done.1, bf16[2048,1536]{1,0:T(8,128)(2,1)} %all-gather.5.cloned.1.call-done.trainee_ref, bf16[2,56,1536]{2,1,0:T(8,128)(2,1)S(1)} %copy-done.6, ...), custom_call_target="tpu_custom_call" | custom-call | flops 2113929216 | bytes 13500416 | tf_op jit(solution)/shard_map/project/pallas_call | solution.py:165
  257.3 0.0 copy-start.8
  257.3 0.8 copy-done.8
  258.1 0.0 copy-start.10
  258.1 0.7 copy-done.10
  258.8 3.9 %all-to-all-done.3.back_ref = bf16[16,2,2,56,128]{4,3,2,1,0:T(8,128)(2,1)S(1)} async-done(((bf16[16,2,2,56,128]{4,3,2,1,0:T(8,128)(2,1)}), bf16[16,2,2,56,128]{4,3,2,1,0:T(8,128)(2,1)S(1)}, u32[]{:S(2)}, u32[]{:S(2)}) %all-to-all-start.3) | async-done | bytes 917536 | tf_op jit(solution)/shard_map/all_to_all | solution.py:238
  262.7 0.0 copy-start.2
  262.7 2.8 copy-done.2
  265.5 0.0 copy-start.4
  265.5 1.0 copy-done.4
  266.5 1.0 copy-done.5
  267.5 7.7 %project.3 = (bf16[112,1536]{1,0:T(8,128)(2,1)S(1)}, bf16[112,2048]{1,0:T(8,128)(2,1)S(1)}) custom-call(bf16[16,2,2,56,128]{4,3,2,1,0:T(8,128)(2,1)S(1)} %all-to-all-done.3.back_ref, bf16[2048,1536]{1,0:T(8,128)(2,1)S(1)} %copy-done.2, bf16[2048,1536]{1,0:T(8,128)(2,1)} %all-gather.5.cloned.1.call-done.trainee_ref, bf16[2,56,1536]{2,1,0:T(8,128)(2,1)S(1)} %copy-done.5, ...), custom_call_target="tpu_custom_call" | custom-call | flops 2113929216 | bytes 13500416 | tf_op jit(solution)/shard_map/project/pallas_call | solution.py:165
  275.2 0.0 copy-done.9
  275.2 0.0 copy-done.11
  275.2 4.5 %convolution_convert_fusion = bf16[2048,1536]{1,0:T(8,128)(2,1)} fusion(bf16[112,2048]{1,0:T(8,128)(2,1)S(1)} %get-tuple-element.10, bf16[112,2048]{1,0:T(8,128)(2,1)S(1)} %copy-done.9, bf16[112,1536]{1,0:T(8,128)(2,1)S(1)} %get-tuple-element.12, bf16[112,1536]{1,0:T(8,128)(2,1)S(1)} %copy-done.11), kind=kOutput, calls=%fused_computation.1 | convolution fusion | flops 1415643136 | bytes 7897088 | tf_op jit(solution)/shard_map/dot_general | solution.py:245
  279.7 0.0 reduce-scatter.2.cloned.1.call-update
  279.7 87.3 %reduce-scatter.2.cloned.1.call-done = bf16[128,1536]{1,0:T(8,128)(2,1)} async-done(((bf16[2048,1536]{1,0:T(8,128)(2,1)}), bf16[128,1536]{1,0:T(8,128)(2,1)}) %reduce-scatter.2.cloned.1.call-update) | async-done | bytes 393232 | tf_op jit(solution)/shard_map/reduce_scatter | solution.py:251
  367.0 2.0 convert_element_type.20
  (10 shorter events, 0.1 us)
Async XLA Ops:
  6.5 235.5 %copy-start = (bf16[256,3072]{1,0:T(8,128)(2,1)S(1)}, bf16[256,3072]{1,0:T(8,128)(2,1)}, u32[]{:S(2)}) copy-start(bf16[256,3072]{1,0:T(8,128)(2,1)} %param.16) | copy-start | bytes 4718596
  6.5 238.3 %all-gather.3.cloned.1.call-start = ((), (), s32[]{:S(2)}) async-start(), calls=%async_computation.5 | async-start | bytes 6684672 | tf_op jit(solution)/shard_map/all_gather | solution.py:233
  7.3 2.4 copy-start.12
  13.2 86.3 %all-to-all-start = ((bf16[16,2,296,128]{3,2,1,0:T(8,128)(2,1)}), bf16[16,2,296,128]{3,2,1,0:T(8,128)(2,1)}, u32[]{:S(2)}, u32[]{:S(2)}) async-start(bf16[16,2,296,128]{3,2,1,0:T(8,128)(2,1)} %pad_maximum_fusion), calls=%async_computation | async-start | bytes 4849664 | tf_op jit(solution)/shard_map/all_to_all | solution.py:232
  20.7 224.1 %all-gather.5.cloned.1.call-start = ((), (), s32[]{:S(2)}) async-start(), calls=%async_computation.6 | async-start | bytes 6684672 | tf_op jit(solution)/shard_map/all_gather | solution.py:234
  24.2 93.5 %copy-start.13 = (s32[2,4,512]{2,1,0:T(4,128)S(1)}, s32[2,4,512]{2,1,0:T(4,128)}, u32[]{:S(2)}) copy-start(s32[2,4,512]{2,1,0:T(4,128)} %param.11) | copy-start | bytes 49156
  99.5 93.2 %all-to-all-start.2 = ((bf16[16,2,296,128]{3,2,1,0:T(8,128)(2,1)}), bf16[16,2,296,128]{3,2,1,0:T(8,128)(2,1)}, u32[]{:S(2)}, u32[]{:S(2)}) async-start(bf16[16,2,296,128]{3,2,1,0:T(8,128)(2,1)} %pad_maximum_fusion.1), calls=%async_computation.2 | async-start | bytes 4849664 | tf_op jit(solution)/shard_map/all_to_all | solution.py:232
  118.5 96.4 %copy-start.15 = (s32[4]{0:T(128)S(1)}, s32[4]{0:T(128)}, u32[]{:S(2)}) copy-start(s32[4]{0:T(128)} %param.12) | copy-start | bytes 52
  118.5 96.4 %copy-start.14 = (bf16[1536,64]{0,1:T(8,128)(2,1)S(1)}, bf16[1536,64]{0,1:T(8,128)(2,1)}, u32[]{:S(2)}) copy-start(bf16[1536,64]{0,1:T(8,128)(2,1)} %param.17) | copy-start | bytes 589828
  192.7 43.0 %all-to-all-start.1 = ((bf16[16,2,2,56,128]{4,3,2,1,0:T(8,128)(2,1)}), bf16[16,2,2,56,128]{4,3,2,1,0:T(8,128)(2,1)S(1)}, u32[]{:S(2)}, u32[]{:S(2)}) async-start(bf16[16,2,2,56,128]{4,3,2,1,0:T(8,128)(2,1)} %attention.2), calls=%async_computation.1 | async-start | bytes 1835008 | tf_op jit(solution)/shard_map/all_to_all | solution.py:238
  226.4 0.9 copy-start.7
  235.7 27.0 %all-to-all-start.3 = ((bf16[16,2,2,56,128]{4,3,2,1,0:T(8,128)(2,1)}), bf16[16,2,2,56,128]{4,3,2,1,0:T(8,128)(2,1)S(1)}, u32[]{:S(2)}, u32[]{:S(2)}) async-start(bf16[16,2,2,56,128]{4,3,2,1,0:T(8,128)(2,1)} %copy-done.7), calls=%async_computation.3 | async-start | bytes 1835008 | tf_op jit(solution)/shard_map/all_to_all | solution.py:238
  241.9 125.1 %reduce-scatter.2.cloned.1.call-start = ((), (), s32[]{:S(2)}) async-start(), calls=%async_computation.7 | async-start | bytes 6684672 | tf_op jit(solution)/shard_map/reduce_scatter | solution.py:251
  244.8 2.8 copy-start.1
  247.6 1.0 copy-start.3
  248.6 1.0 copy-start.6
  257.3 0.8 copy-start.8
  258.1 0.7 copy-start.10
  262.7 2.8 copy-start.2
  265.5 1.0 copy-start.4
  266.5 1.0 copy-start.5
  267.5 7.7 %copy-start.9 = (bf16[112,2048]{1,0:T(8,128)(2,1)S(1)}, bf16[112,2048]{1,0:T(8,128)(2,1)}, u32[]{:S(2)}) copy-start(bf16[112,2048]{1,0:T(8,128)(2,1)} %copy-done.8) | copy-start | bytes 1376260
  267.5 7.8 %copy-start.11 = (bf16[112,1536]{1,0:T(8,128)(2,1)S(1)}, bf16[112,1536]{1,0:T(8,128)(2,1)}, u32[]{:S(2)}) copy-start(bf16[112,1536]{1,0:T(8,128)(2,1)} %copy-done.10) | copy-start | bytes 1032196
Sparse Core Ops, SparseCore 0:
  9.6 100.6 all-gather.2
  112.6 95.4 all-gather.4
  279.9 87.1 reduce-scatter.1

commit v3 on v2

--- a/solution.py
+++ b/solution.py
@@ -13,7 +13,6 @@
 HEAD_DIM = 128
 WIDTH = 1536
 TIME_DIM = 256
-CHUNKS = 2
 LOG2E = math.log2(math.e)
 
 
@@ -153,7 +152,8 @@
         along = jnp.sum(inner * mixed, axis=1, keepdims=True) * (1.0 / WIDTH)
         cot = root * inner - mixed * (root * root * root * along)
         cot_ref[...] = (cot * spread(gate_ref[...])).astype(cot_ref.dtype)
-        att_ref[...] = both_s[:rows, :]
+        for h in range(HEADS):
+            att_ref[h] = both_s[:rows, h * HEAD_DIM:(h + 1) * HEAD_DIM]
 
 
 def project(back, frozen, trainee, states, gate, scale, final_head):
@@ -174,17 +174,17 @@
             whole(scale.shape),
             whole(final_head.shape),
         ],
-        out_specs=[whole((rows, WIDTH)), whole((rows, inner))],
+        out_specs=[whole((rows, WIDTH)), whole((HEADS, rows, HEAD_DIM))],
         out_shape=[
             jax.ShapeDtypeStruct((rows, WIDTH), jnp.bfloat16),
-            jax.ShapeDtypeStruct((rows, inner), jnp.bfloat16),
+            jax.ShapeDtypeStruct((HEADS, rows, HEAD_DIM), jnp.bfloat16),
         ],
         scratch_shapes=[
             pltpu.VMEM((2 * rows, inner), jnp.bfloat16),
             pltpu.VMEM((3, rows, WIDTH), jnp.float32),
             pltpu.VMEM((3, rows, 128), jnp.float32),
         ],
-        compiler_params=pltpu.CompilerParams(dimension_semantics=("arbitrary",), vmem_limit_bytes=40 << 20),
+        compiler_params=pltpu.CompilerParams(dimension_semantics=("arbitrary",), vmem_limit_bytes=60 << 20),
         cost_estimate=pl.CostEstimate(
             flops=6 * rows * inner * WIDTH,
             bytes_accessed=4 * inner * WIDTH + 4 * rows * inner,
@@ -192,6 +192,91 @@
         ),
         name="project",
     )(back, frozen, trainee, states, gate, scale, final_head)
+
+
+def product_kernel(mine, peer, att_ref, att_peer_ref, cot_ref, cot_peer_ref, *out_refs):
+    half = WIDTH // 2
+    slots = out_refs[0].shape[0]
+    for part, out_ref in enumerate(out_refs):
+        picked = range(part * slots, (part + 1) * slots)
+        own = jnp.concatenate([att_ref[mine[i]] for i in picked], axis=1)
+        other = jnp.concatenate([att_peer_ref[peer[i]] for i in picked], axis=1)
+        columns = slice(part * half, (part + 1) * half)
+        contract = (((0,), (0,)), ((), ()))
+        total = lax.dot_general(
+            jnp.concatenate([own, other], axis=0),
+            jnp.concatenate([cot_ref[:, columns], cot_peer_ref[:, columns]], axis=0),
+            contract,
+            preferred_element_type=jnp.float32,
+        )
+        out_ref[...] = total.reshape(out_ref.shape).astype(out_ref.dtype)
+
+
+def product(blocks, core, att, att_peer, cot, cot_peer):
+    slots = blocks.shape[0] // 2
+    rows = cot.shape[0]
+    half = WIDTH // 2
+    out = jax.ShapeDtypeStruct((slots, HEAD_DIM, half), jnp.bfloat16)
+    return pl.pallas_call(
+        product_kernel,
+        in_specs=[pl.BlockSpec(memory_space=pltpu.SMEM)] * 2 + [pl.BlockSpec(memory_space=pltpu.VMEM)] * 4,
+        out_specs=[pl.BlockSpec(memory_space=pltpu.VMEM)] * 2,
+        out_shape=[out, out],
+        compiler_params=pltpu.CompilerParams(vmem_limit_bytes=32 << 20),
+        cost_estimate=pl.CostEstimate(
+            flops=8 * slots * rows * HEAD_DIM * half,
+            bytes_accessed=4 * rows * (WIDTH + 2 * slots * HEAD_DIM) + 4 * slots * HEAD_DIM * half,
+            transcendentals=0,
+        ),
+        name="product",
+    )(2 * blocks + core, blocks, att, att_peer, cot, cot_peer)
+
+
+def reduce_by_halving(att, cot, position, group_size):
+    levels = group_size.bit_length() - 1
+    chips = group_size // 2
+    bit = [(position >> k) & 1 for k in range(levels)]
+
+    def swap(x, k):
+        return lax.ppermute(x, "seq", [(s, s ^ (1 << k)) for s in range(group_size)])
+
+    by_core = att.reshape(chips, 2, *att.shape[1:])
+    cot_peer = swap(cot, 0)
+    att_peer = swap(lax.dynamic_index_in_dim(by_core, 1 - bit[0], 1, keepdims=False), 0)
+    orders = (tuple(range(1, levels)), tuple(range(2, levels)) + (1,))
+
+    def chip_blocks(keep):
+        tables = []
+        for order in orders:
+            k = order[0] - 1
+            ids = [m for m in range(chips) if not (m >> k) & 1]
+            wanted = bit[order[0]] if keep else 1 - bit[order[0]]
+            tables.append(jnp.array(ids, jnp.int32) + (wanted << k))
+        return jnp.concatenate(tables)
+
+    factors = (bit[0], att, att_peer, cot, cot_peer)
+    sent = product(chip_blocks(False), *factors)
+    kept = product(chip_blocks(True), *factors)
+    state = []
+    for part, order in enumerate(orders):
+        left = sorted(order[1:], reverse=True)
+        shape = (2,) * len(left) + (HEAD_DIM, WIDTH // 2)
+        state.append((kept[part].reshape(shape), swap(sent[part], order[0]).reshape(shape), left))
+    for level in range(1, levels - 1):
+        following = []
+        for (keep, got, left), order in zip(state, orders):
+            k = order[level]
+            axis = left.index(k)
+
+            def half(x, which):
+                return lax.dynamic_index_in_dim(x, which, axis, keepdims=False).astype(jnp.float32)
+
+            def joined(which):
+                return (half(keep, which) + half(got, which)).astype(jnp.bfloat16)
+
+            following.append((joined(bit[k]), swap(joined(1 - bit[k]), k), [n for n in left if n != k]))
+        state = following
+    return jnp.concatenate([keep.astype(jnp.float32) + got.astype(jnp.float32) for keep, got, _ in state], axis=1)
 
 
 def shards(
@@ -222,34 +307,18 @@
     modulation = jnp.dot(embedding, time_mod.astype(jnp.float32), precision=lax.Precision.HIGHEST)
     gate = modulation[:, :WIDTH]
     scale = modulation[:, WIDTH:]
-    chunks = CHUNKS if owned == SAMPLES else 1
-    items = owned // chunks
-    samples = SAMPLES // chunks
     exchange = functools.partial(lax.all_to_all, axis_name="seq", split_axis=0, concat_axis=0, tiled=True)
-    gathered = []
-    for c in range(chunks):
-        own = slice(c * items, (c + 1) * items)
-        gathered.append(exchange(jnp.concatenate([text_items[:, own], image_items[:, own]], axis=2)))
+    gathered = exchange(jnp.concatenate([text_items, image_items], axis=2))
     all_frozen = lax.all_gather(frozen_out, "seq", axis=0, tiled=True)
     all_trainee = lax.all_gather(trainee_out, "seq", axis=0, tiled=True)
-    cotangents, columns = [], []
-    for c in range(chunks):
-        both = attend(gathered[c], live[c * items:(c + 1) * items], image_dev, text_dev)
-        back = exchange(both).reshape(HEADS, samples, 2, image_dev, HEAD_DIM)
-        part = slice(c * samples, (c + 1) * samples)
-        cot, att = project(
-            back, all_frozen, all_trainee, image_states[part], gate[part], scale[part], final_head
-        )
-        cotangents.append(cot)
-        columns.append(att)
-    partial = lax.dot_general(
-        jnp.concatenate(columns),
-        jnp.concatenate(cotangents),
-        (((0,), (0,)), ((), ())),
-        preferred_element_type=jnp.float32,
-    ).astype(jnp.bfloat16)
-    total = lax.psum_scatter(partial, "seq", scatter_dimension=0, tiled=True)
-    return total.astype(jnp.float32)
+    both = attend(gathered, live, image_dev, text_dev)
+    back = exchange(both).reshape(HEADS, SAMPLES, 2, image_dev, HEAD_DIM)
+    cot, att = project(back, all_frozen, all_trainee, image_states, gate, scale, final_head)
+    if group_size == HEADS:
+        return reduce_by_halving(att, cot, position, group_size)
+    partial = jnp.einsum("hrd,rc->hdc", att, cot, preferred_element_type=jnp.float32)
+    partial = partial.reshape(HEADS * HEAD_DIM, WIDTH).astype(jnp.bfloat16)
+    return lax.psum_scatter(partial, "seq", scatter_dimension=0, tiled=True).astype(jnp.float32)
 
 
 def solution(mesh):

time: 377 us -> 342 us (0.907)
  waiting for transfers between devices: 239 us -> 202 us
  starting transfers between devices: 54 us -> 63.1 us
  local copies, waits for them, and re-layouts: 19.9 us -> 15.4 us
  matrix products: 5.19 us -> 0.72 us
    reduce_scatter x1 -> x0, waiting for transfers between devices: 87.3 us -> none  [shards(): total = lax.psum_scatter(partial, 'seq', scatter_dimension=0, tiled=True)]
    ppermute x0 -> x8, waiting for transfers between devices: none -> 36.9 us  [swap(): return lax.ppermute(x, 'seq', [(s, s ^ 1 << k) for s in range(group_size)])]
    ppermute x0 -> x8, starting transfers between devices: none -> 20.3 us  [swap(): return lax.ppermute(x, 'seq', [(s, s ^ 1 << k) for s in range(group_size)])]
    all_gather x1, waiting for transfers between devices: 0.01 us -> 20.1 us  [shards(): all_trainee = lax.all_gather(trainee_out, 'seq', axis=0, tiled=True)]
    all_to_all x4 -> x2, starting transfers between devices: 54 us -> 42.7 us  [the longest x1 35.2 us: shards(): back = exchange(both).reshape(HEADS, SAMPLES, 2, image_dev, HEAD_DIM)]
    all_to_all x4 -> x2, waiting for transfers between devices: 150 us -> 143 us  [the longest x1 126 us: shards(): gathered = exchange(jnp.concatenate([text_items, image_items], axis=2))]
    pallas_call x0 -> x2, Pallas kernels: none -> 5.05 us  [product(): pl.pallas_call(product_kernel, in_specs=[pl.BlockSpec(memory_space=pltpu....]
    dot_general x1 -> x0, matrix products: 4.47 us -> none  [shards(): lax.dot_general(jnp.concatenate(columns), jnp.concatenate(cotangents), ((...]
  transfers between devices with their start and end apart: 7 -> 12, of which waited for: 5 -> 9; matrix products, arithmetic and copies ran while one was open for 4% -> 5% of each run, Pallas kernels for 8% -> 7%
where the time goes in v3:
time: 342 us
  waiting for transfers between devices  202 us (59%)
  starting transfers between devices  63.1 us (18%)
  Pallas kernels  39 us (11%)
  local copies, waits for them, and re-layouts  15.4 us (5%)
  between operations  13.6 us (4%)
  other arithmetic  8.27 us (2%)
    all_to_all x1, waiting for transfers between devices, shards(): gathered = exchange(jnp.concatenate([text_items, image_items], axis=2))  126 us
    ppermute x8, waiting for transfers between devices, swap(): return lax.ppermute(x, 'seq', [(s, s ^ 1 << k) for s in range(group_size)])  36.9 us
    all_to_all x1, starting transfers between devices, shards(): back = exchange(both).reshape(HEADS, SAMPLES, 2, image_dev, HEAD_DIM)  35.2 us
    pallas_call x1, Pallas kernels, attend(): pl.pallas_call(functools.partial(attention_kernel, image_dev, text_dev, b...  20.9 us
    ppermute x8, starting transfers between devices, swap(): return lax.ppermute(x, 'seq', [(s, s ^ 1 << k) for s in range(group_size)])  20.3 us
    all_gather x1, waiting for transfers between devices, shards(): all_trainee = lax.all_gather(trainee_out, 'seq', axis=0, tiled=True)  20.1 us
    all_to_all x1, waiting for transfers between devices, shards(): back = exchange(both).reshape(HEADS, SAMPLES, 2, image_dev, HEAD_DIM)  17.4 us
    pallas_call x1, Pallas kernels, project(): pl.pallas_call(functools.partial(head_kernel, samples, image_dev), grid=(...  13 us
  transfers between devices with their start and end apart: 12, of which 9 were waited for; matrix products, arithmetic and copies ran while one was open for 5% of the time, Pallas kernels for 7%

profile of v3, /device:TPU:0, one launch (start us, length us, event | category | flops | bytes accessed | tf_op | source)
XLA Modules:
  0.0 341.7 jit_solution(2032369136455502402)
XLA Ops:
  6.5 0.0 copy-start
  6.5 0.0 all-gather.3.cloned.1.call-start
  6.5 0.7 all-gather.3.cloned.1.call-update
  7.3 0.0 copy-start.10
  7.3 2.4 copy.19
  9.7 0.0 copy-done.10
  9.7 0.6 copy.18
  10.3 2.6 pad_maximum_fusion
  12.8 0.0 copy-start.12
  12.8 7.6 %all-to-all-start = ((bf16[16,4,296,128]{3,2,1,0:T(8,128)(2,1)}), bf16[16,4,296,128]{3,2,1,0:T(8,128)(2,1)}, u32[]{:S(2)}, u32[]{:S(2)}) async-start(bf16[16,4,296,128]{3,2,1,0:T(8,128)(2,1)} %pad_maximum_fusion), calls=%async_computation | async-start | bytes 9699328 | tf_op jit(solution)/shard_map/all_to_all | solution.py:311
  20.4 0.0 all-gather.5.cloned.1.call-start
  20.4 0.7 all-gather.5.cloned.1.call-update
  21.2 0.0 copy-done.12
  21.2 0.6 gather_fusion
  21.8 0.1 compare_convert_fusion.live_ref
  21.9 125.8 %all-to-all-done.x_ref = bf16[16,4,296,128]{3,2,1,0:T(8,128)(2,1)} async-done(((bf16[16,4,296,128]{3,2,1,0:T(8,128)(2,1)}), bf16[16,4,296,128]{3,2,1,0:T(8,128)(2,1)}, u32[]{:S(2)}, u32[]{:S(2)}) %all-to-all-start) | async-done | bytes 4849696 | tf_op jit(solution)/shard_map/all_to_all | solution.py:311
  147.7 20.9 %attention.1 = bf16[16,4,2,56,128]{4,3,2,1,0:T(8,128)(2,1)} custom-call(bf16[16,4,296,128]{3,2,1,0:T(8,128)(2,1)} %all-to-all-done.x_ref, s32[4,2,512]{2,1,0:T(2,128)S(1)} %compare_convert_fusion.live_ref), custom_call_target="tpu_custom_call" | custom-call | flops 3523215360 | bytes 6684672 | tf_op jit(solution)/shard_map/attention/pallas_call | solution.py:70
  168.7 35.2 %all-to-all-start.1 = ((bf16[16,4,2,56,128]{4,3,2,1,0:T(8,128)(2,1)}), bf16[16,4,2,56,128]{4,3,2,1,0:T(8,128)(2,1)S(1)}, u32[]{:S(2)}, u32[]{:S(2)}) async-start(bf16[16,4,2,56,128]{4,3,2,1,0:T(8,128)(2,1)} %attention.1), calls=%async_computation.1 | async-start | bytes 3670016 | tf_op jit(solution)/shard_map/all_to_all | solution.py:315
  203.8 0.0 copy-done.14
  203.9 1.9 copy.21.head_ref
  205.7 0.1 multiply_cosine_fusion
  205.8 0.0 copy-done
  205.8 0.7 fusion.10
  206.6 0.6 fusion.20
  207.2 20.1 %all-gather.5.cloned.1.call-done.trainee_ref = bf16[2048,1536]{1,0:T(8,128)(2,1)} async-done(((bf16[128,1536]{1,0:T(8,128)(2,1)}), bf16[2048,1536]{1,0:T(8,128)(2,1)}) %all-gather.5.cloned.1.call-update) | async-done | bytes 6291472 | tf_op jit(solution)/shard_map/all_gather | solution.py:313
  227.3 17.4 %all-to-all-done.1.back_ref = bf16[16,4,2,56,128]{4,3,2,1,0:T(8,128)(2,1)S(1)} async-done(((bf16[16,4,2,56,128]{4,3,2,1,0:T(8,128)(2,1)}), bf16[16,4,2,56,128]{4,3,2,1,0:T(8,128)(2,1)S(1)}, u32[]{:S(2)}, u32[]{:S(2)}) %all-to-all-start.1) | async-done | bytes 1835040 | tf_op jit(solution)/shard_map/all_to_all | solution.py:315
  244.7 1.2 copy-done.11
  245.9 13.0 %project.1 = (bf16[224,1536]{1,0:T(8,128)(2,1)}, bf16[16,224,128]{2,1,0:T(8,128)(2,1)}) custom-call(bf16[16,4,2,56,128]{4,3,2,1,0:T(8,128)(2,1)} %copy-done.11, bf16[2048,1536]{1,0:T(8,128)(2,1)} %all-gather.3.cloned.1.call-done.frozen_ref, bf16[2048,1536]{1,0:T(8,128)(2,1)} %all-gather.5.cloned.1.call-done.trainee_ref, bf16[4,56,1536]{2,1,0:T(8,128)(2,1)} %states_ref.1, ...), custom_call_target="tpu_custom_call" | custom-call | flops 4227858432 | bytes 14417920 | tf_op jit(solution)/shard_map/project/pallas_call | solution.py:165
  258.9 0.1 collective-permute-start.1
  259.0 1.9 dynamic-slice_bitcast_fusion
  260.9 0.3 collective-permute-start
  261.2 0.0 copy-done.13
  261.3 0.1 multiply_add_fusion
  261.3 1.7 collective-permute-done.att_peer_ref
  263.1 0.0 collective-permute-done.1.cot_peer_ref
  263.1 0.9 copy-done.5
  263.9 1.2 copy-done.1
  265.1 1.1 copy-done.3
  266.2 1.1 copy-done.6
  267.3 3.0 product.3
  270.3 3.9 %collective-permute-start.2 = (bf16[4,128,768]{2,1,0:T(8,128)(2,1)}, bf16[4,128,768]{2,1,0:T(8,128)(2,1)}, u32[]{:S(2)}, u32[]{:S(2)}) collective-permute-start(bf16[4,128,768]{2,1,0:T(8,128)(2,1)} %get-tuple-element.14), channel_id=1, source_target_pairs={{0,2},{1,3},{2,0},{3,1},{4,6},{5,7},{6,4},{7,5},{8,10},{9,11},{10,... | collective-permute-start | bytes 2359304 | tf_op jit(solution)/shard_map/ppermute | solution.py:241
  274.2 5.5 %collective-permute-start.5 = (bf16[4,128,768]{2,1,0:T(8,128)(2,1)}, bf16[4,128,768]{2,1,0:T(8,128)(2,1)}, u32[]{:S(2)}, u32[]{:S(2)}) collective-permute-start(bf16[4,128,768]{2,1,0:T(8,128)(2,1)} %get-tuple-element.16), channel_id=1, source_target_pairs={{0,4},{1,5},{2,6},{3,7},{4,0},{5,1},{6,2},{7,3},{8,12},{9,13},{10,... | collective-permute-start | bytes 2359304 | tf_op jit(solution)/shard_map/ppermute | solution.py:241
  279.7 0.0 copy-done.2
  279.7 0.0 copy-done.4
  279.7 1.1 copy-done.7
  280.8 2.0 product.2
  282.8 0.0 copy-start.8
  282.8 0.9 copy-done.8
  283.7 8.8 %collective-permute-done.2 = bf16[4,128,768]{2,1,0:T(8,128)(2,1)} collective-permute-done((bf16[4,128,768]{2,1,0:T(8,128)(2,1)}, bf16[4,128,768]{2,1,0:T(8,128)(2,1)}, u32[]{:S(2)}, u32[]{:S(2)}) %collective-permute-start.2) | collective-permute-done | bytes 786464 | tf_op jit(solution)/shard_map/ppermute | solution.py:241
  292.5 2.1 add_convert_fusion.3
  294.7 5.5 %collective-permute-start.3 = (bf16[2,128,768]{2,1,0:T(8,128)(2,1)}, bf16[2,128,768]{2,1,0:T(8,128)(2,1)S(1)}, u32[]{:S(2)}, u32[]{:S(2)}) collective-permute-start(bf16[2,128,768]{2,1,0:T(8,128)(2,1)} %get-tuple-element.22), channel_id=1, source_target_pairs={{0,4},{1,5},{2,6},{3,7},{4,0},{5,1},{6,2},{7,3},{8,12},{9,13},{10,... | collective-permute-start | bytes 1179656 | tf_op jit(solution)/shard_map/ppermute | solution.py:241
  300.1 0.0 collective-permute-done.5
  300.2 0.0 copy-done.9
  300.2 2.0 add_convert_fusion.1
  302.2 1.4 collective-permute-start.6
  303.6 11.1 %collective-permute-done.3 = bf16[2,128,768]{2,1,0:T(8,128)(2,1)S(1)} collective-permute-done((bf16[2,128,768]{2,1,0:T(8,128)(2,1)}, bf16[2,128,768]{2,1,0:T(8,128)(2,1)S(1)}, u32[]{:S(2)}, u32[]{:S(2)}) %collective-permute-start.3) | collective-permute-done | bytes 393248 | tf_op jit(solution)/shard_map/ppermute | solution.py:241
  314.7 1.8 collective-permute-start.4
  316.5 11.4 %collective-permute-done.6 = bf16[2,128,768]{2,1,0:T(8,128)(2,1)S(1)} collective-permute-done((bf16[2,128,768]{2,1,0:T(8,128)(2,1)}, bf16[2,128,768]{2,1,0:T(8,128)(2,1)S(1)}, u32[]{:S(2)}, u32[]{:S(2)}) %collective-permute-start.6) | collective-permute-done | bytes 393248 | tf_op jit(solution)/shard_map/ppermute | solution.py:241
  328.0 1.8 collective-permute-start.7
  329.9 0.9 collective-permute-done.4
  330.8 0.1 convert_add_fusion.4
  330.9 2.9 collective-permute-done.7
  333.8 0.1 convert_add_fusion.1
  333.9 1.0 pad_maximum_fusion.1
  (22 shorter events, 0.2 us)
Async XLA Ops:
  6.5 199.3 %copy-start = (bf16[256,3072]{1,0:T(8,128)(2,1)S(1)}, bf16[256,3072]{1,0:T(8,128)(2,1)}, u32[]{:S(2)}) copy-start(bf16[256,3072]{1,0:T(8,128)(2,1)} %param.20) | copy-start | bytes 4718596
  6.5 200.7 %all-gather.3.cloned.1.call-start = ((), (), s32[]{:S(2)}) async-start(), calls=%async_computation.2 | async-start | bytes 6684672 | tf_op jit(solution)/shard_map/all_gather | solution.py:312
  7.3 2.4 copy-start.10
  12.8 8.4 %copy-start.12 = (s32[2,4,512]{2,1,0:T(4,128)S(1)}, s32[2,4,512]{2,1,0:T(4,128)}, u32[]{:S(2)}) copy-start(s32[2,4,512]{2,1,0:T(4,128)} %param.15) | copy-start | bytes 49156
  12.8 134.9 %all-to-all-start = ((bf16[16,4,296,128]{3,2,1,0:T(8,128)(2,1)}), bf16[16,4,296,128]{3,2,1,0:T(8,128)(2,1)}, u32[]{:S(2)}, u32[]{:S(2)}) async-start(bf16[16,4,296,128]{3,2,1,0:T(8,128)(2,1)} %pad_maximum_fusion), calls=%async_computation | async-start | bytes 9699328 | tf_op jit(solution)/shard_map/all_to_all | solution.py:311
  20.4 206.9 %all-gather.5.cloned.1.call-start = ((), (), s32[]{:S(2)}) async-start(), calls=%async_computation.3 | async-start | bytes 6684672 | tf_op jit(solution)/shard_map/all_gather | solution.py:313
  168.7 35.2 %copy-start.14 = (s32[4]{0:T(128)S(1)}, s32[4]{0:T(128)}, u32[]{:S(2)}) copy-start(s32[4]{0:T(128)} %param.16) | copy-start | bytes 52
  168.7 76.0 %all-to-all-start.1 = ((bf16[16,4,2,56,128]{4,3,2,1,0:T(8,128)(2,1)}), bf16[16,4,2,56,128]{4,3,2,1,0:T(8,128)(2,1)S(1)}, u32[]{:S(2)}, u32[]{:S(2)}) async-start(bf16[16,4,2,56,128]{4,3,2,1,0:T(8,128)(2,1)} %attention.1), calls=%async_computation.1 | async-start | bytes 3670016 | tf_op jit(solution)/shard_map/all_to_all | solution.py:315
  244.7 1.2 copy-start.11
  245.9 15.3 %copy-start.13 = (s32[4]{0:T(128)S(1)}, s32[4]{0:T(128)}, u32[]{:S(2)}) copy-start(s32[4]{0:T(128)} %constant.103.clone) | copy-start | bytes 52
  258.9 20.8 %copy-start.2 = (bf16[16,224,128]{2,1,0:T(8,128)(2,1)S(1)}, bf16[16,224,128]{2,1,0:T(8,128)(2,1)}, u32[]{:S(2)}) copy-start(bf16[16,224,128]{2,1,0:T(8,128)(2,1)} %get-tuple-element.11.att_ref) | copy-start | bytes 2752516
  258.9 4.2 %collective-permute-start.1 = (bf16[224,1536]{1,0:T(8,128)(2,1)}, bf16[224,1536]{1,0:T(8,128)(2,1)S(1)}, u32[]{:S(2)}, u32[]{:S(2)}) collective-permute-start(bf16[224,1536]{1,0:T(8,128)(2,1)} %get-tuple-element.12.cot_ref), channel_id=1, source_target_pairs={{0,1},{1,0},{2,3},{3,2},{4,5},{5,4},{6,7},{7,6},{8,9},{9,8},{10,11... | collective-permute-start | bytes 2064392 | tf_op jit(solution)/shard_map/ppermute | solution.py:241
  260.9 2.2 collective-permute-start
  263.1 0.9 copy-start.5
  263.9 1.2 copy-start.1
  265.1 1.1 copy-start.3
  266.2 1.1 copy-start.6
  267.3 12.4 %copy-start.4 = (bf16[224,1536]{1,0:T(8,128)(2,1)S(1)}, bf16[224,1536]{1,0:T(8,128)(2,1)}, u32[]{:S(2)}) copy-start(bf16[224,1536]{1,0:T(8,128)(2,1)} %get-tuple-element.12.cot_ref) | copy-start | bytes 2064388
  270.3 22.2 %collective-permute-start.2 = (bf16[4,128,768]{2,1,0:T(8,128)(2,1)}, bf16[4,128,768]{2,1,0:T(8,128)(2,1)}, u32[]{:S(2)}, u32[]{:S(2)}) collective-permute-start(bf16[4,128,768]{2,1,0:T(8,128)(2,1)} %get-tuple-element.14), channel_id=1, source_target_pairs={{0,2},{1,3},{2,0},{3,1},{4,6},{5,7},{6,4},{7,5},{8,10},{9,11},{10,... | collective-permute-start | bytes 2359304 | tf_op jit(solution)/shard_map/ppermute | solution.py:241
  274.2 26.0 %collective-permute-start.5 = (bf16[4,128,768]{2,1,0:T(8,128)(2,1)}, bf16[4,128,768]{2,1,0:T(8,128)(2,1)}, u32[]{:S(2)}, u32[]{:S(2)}) collective-permute-start(bf16[4,128,768]{2,1,0:T(8,128)(2,1)} %get-tuple-element.16), channel_id=1, source_target_pairs={{0,4},{1,5},{2,6},{3,7},{4,0},{5,1},{6,2},{7,3},{8,12},{9,13},{10,... | collective-permute-start | bytes 2359304 | tf_op jit(solution)/shard_map/ppermute | solution.py:241
  279.7 1.1 copy-start.7
  282.8 0.9 copy-start.8
  292.5 7.6 %copy-start.9 = (bf16[4,128,768]{2,1,0:T(8,128)(2,1)S(1)}, bf16[4,128,768]{2,1,0:T(8,128)(2,1)}, u32[]{:S(2)}) copy-start(bf16[4,128,768]{2,1,0:T(8,128)(2,1)} %copy-done.8) | copy-start | bytes 2359300
  294.7 20.0 %collective-permute-start.3 = (bf16[2,128,768]{2,1,0:T(8,128)(2,1)}, bf16[2,128,768]{2,1,0:T(8,128)(2,1)S(1)}, u32[]{:S(2)}, u32[]{:S(2)}) collective-permute-start(bf16[2,128,768]{2,1,0:T(8,128)(2,1)} %get-tuple-element.22), channel_id=1, source_target_pairs={{0,4},{1,5},{2,6},{3,7},{4,0},{5,1},{6,2},{7,3},{8,12},{9,13},{10,... | collective-permute-start | bytes 1179656 | tf_op jit(solution)/shard_map/ppermute | solution.py:241
  302.2 25.8 %collective-permute-start.6 = (bf16[2,128,768]{2,1,0:T(8,128)(2,1)}, bf16[2,128,768]{2,1,0:T(8,128)(2,1)S(1)}, u32[]{:S(2)}, u32[]{:S(2)}) collective-permute-start(bf16[2,128,768]{2,1,0:T(8,128)(2,1)} %get-tuple-element.24), channel_id=1, source_target_pairs={{0,8},{1,9},{2,10},{3,11},{4,12},{5,13},{6,14},{7,15},{8,0},{9,1},... | collective-permute-start | bytes 1179656 | tf_op jit(solution)/shard_map/ppermute | solution.py:241
  314.7 16.1 %collective-permute-start.4 = (bf16[128,768]{1,0:T(8,128)(2,1)S(1)}, bf16[128,768]{1,0:T(8,128)(2,1)S(1)}, u32[]{:S(2)}, u32[]{:S(2)}) collective-permute-start(bf16[128,768]{1,0:T(8,128)(2,1)S(1)} %fusion.7), channel_id=1, source_target_pairs={{0,8},{1,9},{2,10},{3,11},{4,12},{5,13},{6,14},{7,15},{8,0},{9,1},... | collective-permute-start | bytes 589832 | tf_op jit(solution)/shard_map/ppermute | solution.py:241
  328.0 5.7 %collective-permute-start.7 = (bf16[128,768]{1,0:T(8,128)(2,1)S(1)}, bf16[128,768]{1,0:T(8,128)(2,1)S(1)}, u32[]{:S(2)}, u32[]{:S(2)}) collective-permute-start(bf16[128,768]{1,0:T(8,128)(2,1)S(1)} %fusion.9), channel_id=1, source_target_pairs={{0,2},{1,3},{2,0},{3,1},{4,6},{5,7},{6,4},{7,5},{8,10},{9,11},{10,... | collective-permute-start | bytes 589832 | tf_op jit(solution)/shard_map/ppermute | solution.py:241
Sparse Core Ops, SparseCore 0:
  9.6 133.4 all-gather.2
  145.4 81.8 all-gather.4

commit v4 on v3

--- a/solution.py
+++ b/solution.py
@@ -13,6 +13,8 @@
 HEAD_DIM = 128
 WIDTH = 1536
 TIME_DIM = 256
+WAVES = 2
+VMEM_PRODUCT = 60 << 20
 LOG2E = math.log2(math.e)
 
 
@@ -96,8 +98,8 @@
 
 
 def head_kernel(
-    samples, image_dev, back_ref, frozen_ref, trainee_ref, states_ref, gate_ref, scale_ref, head_ref,
-    cot_ref, att_ref, both_s, mixed_s, square_s,
+    samples, image_dev, blocks_ref, back_ref, frozen_ref, frozen_other_ref, trainee_ref, states_ref, gate_ref,
+    scale_ref, head_ref, cot_ref, att_ref, both_s, mixed_s, square_s,
 ):
     step = pl.program_id(0)
     rows = samples * image_dev
@@ -116,10 +118,11 @@
             [jnp.broadcast_to(values[b:b + 1, :], (image_dev, values.shape[1])) for b in range(samples)], axis=0
         )
 
-    columns = pl.ds(pl.multiple_of(step * width, 128), width)
+    columns = pl.ds(pl.multiple_of(blocks_ref[step] * width, 128), width)
     states = states_ref[:, :, columns].astype(jnp.float32).reshape(rows, width)
     gate = spread(gate_ref[:, columns])
-    frozen = jnp.dot(both_s[...], frozen_ref[...], preferred_element_type=jnp.float32)
+    weights = jnp.where(step < pl.num_programs(0) // 2, frozen_ref[...], frozen_other_ref[...])
+    frozen = jnp.dot(both_s[...], weights, preferred_element_type=jnp.float32)
     trainee = jnp.dot(both_s[:rows, :], trainee_ref[...], preferred_element_type=jnp.float32)
     for k, branch in enumerate((frozen[:rows], frozen[rows:], trainee)):
         mixed = states + gate * branch
@@ -156,33 +159,39 @@
             att_ref[h] = both_s[:rows, h * HEAD_DIM:(h + 1) * HEAD_DIM]
 
 
-def project(back, frozen, trainee, states, gate, scale, final_head):
+def project(back, half, frozen, frozen_other, trainee, states, gate, scale, final_head):
     samples, image_dev = states.shape[:2]
     rows = samples * image_dev
-    inner = frozen.shape[0]
+    inner = trainee.shape[0]
     width = 256
-    whole = lambda shape: pl.BlockSpec(shape, lambda n: (0,) * len(shape))
+    steps = WIDTH // width
+    blocks = (jnp.arange(steps, dtype=jnp.int32) + half * (steps // 2)) % steps
+    whole = lambda shape: pl.BlockSpec(shape, lambda n, blocks: (0,) * len(shape))
     return pl.pallas_call(
         functools.partial(head_kernel, samples, image_dev),
-        grid=(WIDTH // width,),
-        in_specs=[
-            whole(back.shape),
-            pl.BlockSpec((inner, width), lambda n: (0, n)),
-            pl.BlockSpec((inner, width), lambda n: (0, n)),
-            whole(states.shape),
-            whole(gate.shape),
-            whole(scale.shape),
-            whole(final_head.shape),
-        ],
-        out_specs=[whole((rows, WIDTH)), whole((HEADS, rows, HEAD_DIM))],
+        grid_spec=pltpu.PrefetchScalarGridSpec(
+            num_scalar_prefetch=1,
+            grid=(steps,),
+            in_specs=[
+                whole(back.shape),
+                pl.BlockSpec((inner, width), lambda n, blocks: (0, jnp.minimum(n, steps // 2 - 1))),
+                pl.BlockSpec((inner, width), lambda n, blocks: (0, jnp.maximum(n - steps // 2, 0))),
+                pl.BlockSpec((inner, width), lambda n, blocks: (0, blocks[n])),
+                whole(states.shape),
+                whole(gate.shape),
+                whole(scale.shape),
+                whole(final_head.shape),
+            ],
+            out_specs=[whole((rows, WIDTH)), whole((HEADS, rows, HEAD_DIM))],
+            scratch_shapes=[
+                pltpu.VMEM((2 * rows, inner), jnp.bfloat16),
+                pltpu.VMEM((3, rows, WIDTH), jnp.float32),
+                pltpu.VMEM((3, rows, 128), jnp.float32),
+            ],
+        ),
         out_shape=[
             jax.ShapeDtypeStruct((rows, WIDTH), jnp.bfloat16),
             jax.ShapeDtypeStruct((HEADS, rows, HEAD_DIM), jnp.bfloat16),
-        ],
-        scratch_shapes=[
-            pltpu.VMEM((2 * rows, inner), jnp.bfloat16),
-            pltpu.VMEM((3, rows, WIDTH), jnp.float32),
-            pltpu.VMEM((3, rows, 128), jnp.float32),
         ],
         compiler_params=pltpu.CompilerParams(dimension_semantics=("arbitrary",), vmem_limit_bytes=60 << 20),
         cost_estimate=pl.CostEstimate(
@@ -191,41 +200,39 @@
             transcendentals=3 * rows,
         ),
         name="project",
-    )(back, frozen, trainee, states, gate, scale, final_head)
-
-
-def product_kernel(mine, peer, att_ref, att_peer_ref, cot_ref, cot_peer_ref, *out_refs):
-    half = WIDTH // 2
-    slots = out_refs[0].shape[0]
+    )(blocks, back, frozen, frozen_other, trainee, states, gate, scale, final_head)
+
+
+def product_kernel(first, mine, peer, att_ref, att_peer_ref, cot_ref, cot_peer_ref, *out_refs):
+    slots, _, width = out_refs[0].shape
     for part, out_ref in enumerate(out_refs):
         picked = range(part * slots, (part + 1) * slots)
         own = jnp.concatenate([att_ref[mine[i]] for i in picked], axis=1)
         other = jnp.concatenate([att_peer_ref[peer[i]] for i in picked], axis=1)
-        columns = slice(part * half, (part + 1) * half)
-        contract = (((0,), (0,)), ((), ()))
+        start = first + part * (WIDTH // 2)
+        columns = slice(start, start + width)
         total = lax.dot_general(
             jnp.concatenate([own, other], axis=0),
             jnp.concatenate([cot_ref[:, columns], cot_peer_ref[:, columns]], axis=0),
-            contract,
+            (((0,), (0,)), ((), ())),
             preferred_element_type=jnp.float32,
         )
         out_ref[...] = total.reshape(out_ref.shape).astype(out_ref.dtype)
 
 
-def product(blocks, core, att, att_peer, cot, cot_peer):
+def product(first, width, blocks, core, att, att_peer, cot, cot_peer):
     slots = blocks.shape[0] // 2
     rows = cot.shape[0]
-    half = WIDTH // 2
-    out = jax.ShapeDtypeStruct((slots, HEAD_DIM, half), jnp.bfloat16)
+    out = jax.ShapeDtypeStruct((slots, HEAD_DIM, width), jnp.bfloat16)
     return pl.pallas_call(
-        product_kernel,
-        in_specs=[pl.BlockSpec(memory_space=pltpu.SMEM)] * 2 + [pl.BlockSpec(memory_space=pltpu.VMEM)] * 4,
-        out_specs=[pl.BlockSpec(memory_space=pltpu.VMEM)] * 2,
+        functools.partial(product_kernel, first),
+        in_specs=[pl.BlockSpec(memory_space=pltpu.SMEM)] * 2 + [pl.BlockSpec()] * 4,
+        out_specs=[pl.BlockSpec()] * 2,
         out_shape=[out, out],
-        compiler_params=pltpu.CompilerParams(vmem_limit_bytes=32 << 20),
+        compiler_params=pltpu.CompilerParams(vmem_limit_bytes=VMEM_PRODUCT),
         cost_estimate=pl.CostEstimate(
-            flops=8 * slots * rows * HEAD_DIM * half,
-            bytes_accessed=4 * rows * (WIDTH + 2 * slots * HEAD_DIM) + 4 * slots * HEAD_DIM * half,
+            flops=8 * slots * rows * HEAD_DIM * width,
+            bytes_accessed=4 * rows * (WIDTH + 2 * slots * HEAD_DIM) + 4 * slots * HEAD_DIM * width,
             transcendentals=0,
         ),
         name="product",
@@ -235,6 +242,7 @@
 def reduce_by_halving(att, cot, position, group_size):
     levels = group_size.bit_length() - 1
     chips = group_size // 2
+    width = WIDTH // 2 // WAVES
     bit = [(position >> k) & 1 for k in range(levels)]
 
     def swap(x, k):
@@ -255,28 +263,39 @@
         return jnp.concatenate(tables)
 
     factors = (bit[0], att, att_peer, cot, cot_peer)
-    sent = product(chip_blocks(False), *factors)
-    kept = product(chip_blocks(True), *factors)
-    state = []
-    for part, order in enumerate(orders):
-        left = sorted(order[1:], reverse=True)
-        shape = (2,) * len(left) + (HEAD_DIM, WIDTH // 2)
-        state.append((kept[part].reshape(shape), swap(sent[part], order[0]).reshape(shape), left))
+    state = {}
+    arrived = {}
+    for wave in range(WAVES):
+        sent = product(wave * width, width, chip_blocks(False), *factors)
+        for part, order in enumerate(orders):
+            arrived[wave, part] = swap(sent[part], order[0])
+    for wave in range(WAVES):
+        kept = product(wave * width, width, chip_blocks(True), *factors)
+        for part, order in enumerate(orders):
+            left = sorted(order[1:], reverse=True)
+            shape = (2,) * len(left) + (HEAD_DIM, width)
+            state[wave, part] = (kept[part].reshape(shape), arrived[wave, part].reshape(shape), left)
     for level in range(1, levels - 1):
-        following = []
-        for (keep, got, left), order in zip(state, orders):
-            k = order[level]
-            axis = left.index(k)
-
-            def half(x, which):
-                return lax.dynamic_index_in_dim(x, which, axis, keepdims=False).astype(jnp.float32)
-
-            def joined(which):
-                return (half(keep, which) + half(got, which)).astype(jnp.bfloat16)
-
-            following.append((joined(bit[k]), swap(joined(1 - bit[k]), k), [n for n in left if n != k]))
-        state = following
-    return jnp.concatenate([keep.astype(jnp.float32) + got.astype(jnp.float32) for keep, got, _ in state], axis=1)
+        for wave in range(WAVES):
+            for part, order in enumerate(orders):
+                keep, got, left = state[wave, part]
+                k = order[level]
+                axis = left.index(k)
+
+                def half(x, which):
+                    return lax.dynamic_index_in_dim(x, which, axis, keepdims=False).astype(jnp.float32)
+
+                def joined(which):
+                    return (half(keep, which) + half(got, which)).astype(jnp.bfloat16)
+
+                rest = [n for n in left if n != k]
+                state[wave, part] = (joined(bit[k]), swap(joined(1 - bit[k]), k), rest)
+    total = []
+    for part in range(2):
+        for wave in range(WAVES):
+            keep, got, _ = state[wave, part]
+            total.append(keep.astype(jnp.float32) + got.astype(jnp.float32))
+    return jnp.concatenate(total, axis=1)
 
 
 def shards(
@@ -309,11 +328,17 @@
     scale = modulation[:, WIDTH:]
     exchange = functools.partial(lax.all_to_all, axis_name="seq", split_axis=0, concat_axis=0, tiled=True)
     gathered = exchange(jnp.concatenate([text_items, image_items], axis=2))
-    all_frozen = lax.all_gather(frozen_out, "seq", axis=0, tiled=True)
+    groups = lax.axis_size("grp")
+    half = lax.axis_index("grp") % 2
+    frozen = lax.all_gather(
+        lax.dynamic_slice_in_dim(frozen_out, half * (WIDTH // 2), WIDTH // 2, axis=1), "seq", axis=0, tiled=True
+    )
+    gathered, frozen, trainee_out = lax.optimization_barrier((gathered, frozen, trainee_out))
+    frozen_other = lax.ppermute(frozen, "grp", [(g, g ^ 1) for g in range(groups)])
     all_trainee = lax.all_gather(trainee_out, "seq", axis=0, tiled=True)
     both = attend(gathered, live, image_dev, text_dev)
     back = exchange(both).reshape(HEADS, SAMPLES, 2, image_dev, HEAD_DIM)
-    cot, att = project(back, all_frozen, all_trainee, image_states, gate, scale, final_head)
+    cot, att = project(back, half, frozen, frozen_other, all_trainee, image_states, gate, scale, final_head)
     if group_size == HEADS:
         return reduce_by_halving(att, cot, position, group_size)
     partial = jnp.einsum("hrd,rc->hdc", att, cot, preferred_element_type=jnp.float32)

time: 342 us -> 331 us (0.968)
  starting transfers between devices: 63.1 us -> 50.2 us
  Pallas kernels: 39 us -> 48 us
  local copies, waits for them, and re-layouts: 15.4 us -> 10.2 us
    all_to_all x1, waiting for transfers between devices: 126 us -> 7.84 us  [shards(): gathered = exchange(jnp.concatenate([text_items, image_items], axis=2))]
    all_gather x1, waiting for transfers between devices: 0.01 us -> 99.3 us  [shards(): lax.all_gather(lax.dynamic_slice_in_dim(frozen_out, half * (WIDTH // 2),...]
    ppermute x0 -> x1, waiting for transfers between devices: none -> 65.3 us  [shards(): lax.ppermute(frozen, 'grp', [(g, g ^ 1) for g in range(groups)])]
    all_gather x1, waiting for transfers between devices: 20.1 us -> 0.01 us  [shards(): all_trainee = lax.all_gather(trainee_out, 'seq', axis=0, tiled=True)]
    all_to_all x1, waiting for transfers between devices: 17.4 us -> 0.01 us  [shards(): back = exchange(both).reshape(HEADS, SAMPLES, 2, image_dev, HEAD_DIM)]
    all_to_all x1, starting transfers between devices: 35.2 us -> 22.5 us  [shards(): back = exchange(both).reshape(HEADS, SAMPLES, 2, image_dev, HEAD_DIM)]
    pallas_call x3 -> x5, Pallas kernels: 18.1 us -> 27.1 us  [the longest x1 14.1 us: project(): pl.pallas_call(functools.partial(head_kernel, samples, image_dev), grid_s...]
    ppermute x8 -> x14, waiting for transfers between devices: 36.9 us -> 28 us  [swap(): return lax.ppermute(x, 'seq', [(s, s ^ 1 << k) for s in range(group_size)])]
  transfers between devices with their start and end apart: 12 -> 19, of which waited for: 9 -> 11; matrix products, arithmetic and copies ran while one was open for 5% -> 3% of each run, Pallas kernels for 7% -> 9%
where the time goes in v4:
time: 331 us; the launch traced here: 330 us
  waiting for transfers between devices  201 us (61%)
  starting transfers between devices  50.2 us (15%)
  Pallas kernels  48 us (15%)
  between operations  13.6 us (4%)
  local copies, waits for them, and re-layouts  10.2 us (3%)
  other arithmetic  6.67 us (2%)
    all_gather x1, waiting for transfers between devices, shards(): lax.all_gather(lax.dynamic_slice_in_dim(frozen_out, half * (WIDTH // 2),...  99.3 us
    ppermute x1, waiting for transfers between devices, shards(): lax.ppermute(frozen, 'grp', [(g, g ^ 1) for g in range(groups)])  65.3 us
    ppermute x14, waiting for transfers between devices, swap(): return lax.ppermute(x, 'seq', [(s, s ^ 1 << k) for s in range(group_size)])  28 us
    all_to_all x1, starting transfers between devices, shards(): back = exchange(both).reshape(HEADS, SAMPLES, 2, image_dev, HEAD_DIM)  22.5 us
    pallas_call x1, Pallas kernels, attend(): pl.pallas_call(functools.partial(attention_kernel, image_dev, text_dev, b...  20.8 us
    ppermute x14, starting transfers between devices, swap(): return lax.ppermute(x, 'seq', [(s, s ^ 1 << k) for s in range(group_size)])  18.5 us
    pallas_call x1, Pallas kernels, project(): pl.pallas_call(functools.partial(head_kernel, samples, image_dev), grid_s...  14.1 us
    pallas_call x4, Pallas kernels, product(): pl.pallas_call(functools.partial(product_kernel, first), in_specs=[pl.Blo...  13 us
  transfers between devices with their start and end apart: 19, of which 11 were waited for; matrix products, arithmetic and copies ran while one was open for 3% of the time, Pallas kernels for 9%

profile of v4, /device:TPU:0, one launch (start us, length us, event | category | flops | bytes accessed | tf_op | source)
XLA Modules:
  0.0 329.9 jit_solution(13427579189958443053)
XLA Ops:
  6.5 2.4 copy.23
  8.9 0.1 copy-done.3
  9.1 0.6 copy.22
  9.7 2.6 pad_maximum_fusion
  12.3 7.6 %all-to-all-start = ((bf16[16,4,296,128]{3,2,1,0:T(8,128)(2,1)}), bf16[16,4,296,128]{3,2,1,0:T(8,128)(2,1)}, u32[]{:S(2)}, u32[]{:S(2)}) async-start(bf16[16,4,296,128]{3,2,1,0:T(8,128)(2,1)} %pad_maximum_fusion), calls=%async_computation | async-start | bytes 9699328 | tf_op jit(solution)/shard_map/all_to_all | solution.py:330
  19.8 0.0 all-gather.3.cloned.1.call-start
  19.9 0.7 constant_dynamic-slice_fusion
  20.6 0.0 all-gather.3.cloned.1.call-update
  20.6 0.0 all-gather.5.cloned.1.call-start
  20.7 99.3 %all-gather.3.cloned.1.call-done.frozen_ref = bf16[2048,768]{1,0:T(8,128)(2,1)} async-done(((bf16[128,768]{1,0:T(8,128)(2,1)}), bf16[2048,768]{1,0:T(8,128)(2,1)}) %all-gather.3.cloned.1.call-update) | async-done | bytes 3145744 | tf_op jit(solution)/shard_map/all_gather | solution.py:333
  120.0 7.8 %all-to-all-done.x_ref = bf16[16,4,296,128]{3,2,1,0:T(8,128)(2,1)} async-done(((bf16[16,4,296,128]{3,2,1,0:T(8,128)(2,1)}), bf16[16,4,296,128]{3,2,1,0:T(8,128)(2,1)}, u32[]{:S(2)}, u32[]{:S(2)}) %all-to-all-start) | async-done | bytes 4849696 | tf_op jit(solution)/shard_map/all_to_all | solution.py:330
  127.8 0.0 all-gather.5.cloned.1.call-update
  127.9 0.6 gather_fusion
  128.5 0.1 compare_convert_fusion.live_ref
  128.6 20.8 %attention.1 = bf16[16,4,2,56,128]{4,3,2,1,0:T(8,128)(2,1)} custom-call(bf16[16,4,296,128]{3,2,1,0:T(8,128)(2,1)} %all-to-all-done.x_ref, s32[4,2,512]{2,1,0:T(2,128)S(1)} %compare_convert_fusion.live_ref), custom_call_target="tpu_custom_call" | custom-call | flops 3523215360 | bytes 6684672 | tf_op jit(solution)/shard_map/attention/pallas_call | solution.py:72
  149.5 22.5 %all-to-all-start.1 = ((bf16[16,4,2,56,128]{4,3,2,1,0:T(8,128)(2,1)}), bf16[16,4,2,56,128]{4,3,2,1,0:T(8,128)(2,1)S(1)}, u32[]{:S(2)}, u32[]{:S(2)}) async-start(bf16[16,4,2,56,128]{4,3,2,1,0:T(8,128)(2,1)} %attention.1), calls=%async_computation.1 | async-start | bytes 3670016 | tf_op jit(solution)/shard_map/all_to_all | solution.py:340
  172.0 1.6 collective-permute-start
  173.5 1.8 copy.25.head_ref
  175.4 0.5 and_select_fusion.2.blocks_ref
  175.9 0.1 multiply_cosine_fusion
  176.0 0.7 fusion.20
  176.7 0.6 fusion.30
  177.3 65.3 %collective-permute-done.frozen_other_ref = bf16[2048,768]{1,0:T(8,128)(2,1)} collective-permute-done((bf16[2048,768]{1,0:T(8,128)(2,1)}, bf16[2048,768]{1,0:T(8,128)(2,1)}, u32[]{:S(2)}, u32[]{:S(2)}) %collective-permute-start) | collective-permute-done | bytes 3145760 | tf_op jit(solution)/shard_map/ppermute | solution.py:337
  242.7 0.0 all-to-all-done.1.back_ref
  242.7 1.2 copy-done.4
  243.9 14.1 %project.1 = (bf16[224,1536]{1,0:T(8,128)(2,1)}, bf16[16,224,128]{2,1,0:T(8,128)(2,1)}) custom-call(s32[6]{0:T(128)} %and_select_fusion.2.blocks_ref, bf16[16,4,2,56,128]{4,3,2,1,0:T(8,128)(2,1)} %copy-done.4, bf16[2048,768]{1,0:T(8,128)(2,1)} %all-gather.3.cloned.1.call-done.frozen_ref, bf16[2048,768]{1,0:T(8,128)(2,1)} %collective-permute-done.frozen_other_ref, ...), custom_call_target="tpu_custom_call" | custom-call | flops 4227858432 | bytes 14417920 | tf_op jit(solution)/shard_map/project/pallas_call | solution.py:170
  258.0 0.0 collective-permute-start.2
  258.0 1.0 dynamic-slice_bitcast_fusion
  259.1 0.6 collective-permute-start.1
  259.7 0.7 multiply_add_fusion
  260.4 0.7 collective-permute-done.1.att_peer_ref
  261.1 0.0 collective-permute-done.2.cot_peer_ref
  261.1 0.8 copy-done.2
  261.9 0.3 copy-done.1
  262.1 3.2 product.5
  265.4 1.7 collective-permute-start.3
  267.0 3.3 product.7
  270.3 0.4 collective-permute-start.6
  270.7 1.7 collective-permute-start.9
  272.3 0.4 collective-permute-start.12
  272.7 3.2 product.4
  275.9 3.3 product.6
  279.2 0.0 collective-permute-done.3
  279.2 0.1 add_convert_fusion.7
  279.3 1.7 collective-permute-start.4
  281.1 4.3 %collective-permute-done.6 = bf16[4,128,384]{2,1,0:T(8,128)(2,1)S(1)} collective-permute-done((bf16[4,128,384]{2,1,0:T(8,128)(2,1)}, bf16[4,128,384]{2,1,0:T(8,128)(2,1)S(1)}, u32[]{:S(2)}, u32[]{:S(2)}) %collective-permute-start.6) | collective-permute-done | bytes 393248 | tf_op jit(solution)/shard_map/ppermute | solution.py:249
  285.4 1.1 add_convert_fusion.5
  286.5 1.7 collective-permute-start.7
  288.2 0.0 collective-permute-done.9
  288.2 0.1 add_convert_fusion.3
  288.4 2.4 collective-permute-start.10
  290.8 6.8 %collective-permute-done.12 = bf16[4,128,384]{2,1,0:T(8,128)(2,1)S(1)} collective-permute-done((bf16[4,128,384]{2,1,0:T(8,128)(2,1)}, bf16[4,128,384]{2,1,0:T(8,128)(2,1)S(1)}, u32[]{:S(2)}, u32[]{:S(2)}) %collective-permute-start.12) | collective-permute-done | bytes 393248 | tf_op jit(solution)/shard_map/ppermute | solution.py:249
  297.6 0.1 add_convert_fusion.1
  297.7 1.7 collective-permute-start.13
  299.4 2.4 collective-permute-done.4
  301.9 1.6 collective-permute-start.5
  303.5 1.5 collective-permute-done.7
  305.0 1.6 collective-permute-start.8
  306.6 1.5 collective-permute-start.11
  308.2 9.1 %collective-permute-done.13 = bf16[2,128,384]{2,1,0:T(8,128)(2,1)S(1)} collective-permute-done((bf16[2,128,384]{2,1,0:T(8,128)(2,1)S(1)}, bf16[2,128,384]{2,1,0:T(8,128)(2,1)S(1)}, u32[]{:S(2)}, u32[]{:S(2)}) %collective-permute-start.13) | collective-permute-done | bytes 196640 | tf_op jit(solution)/shard_map/ppermute | solution.py:249
  317.3 1.5 collective-permute-start.14
  318.9 0.6 collective-permute-done.8
  319.6 2.4 collective-permute-done.14
  322.1 1.0 pad_maximum_fusion.1
  (40 shorter events, 0.4 us)
Async XLA Ops:
  6.5 169.5 %copy-start = (bf16[256,3072]{1,0:T(8,128)(2,1)S(1)}, bf16[256,3072]{1,0:T(8,128)(2,1)}, u32[]{:S(2)}) copy-start(bf16[256,3072]{1,0:T(8,128)(2,1)} %param.24) | copy-start | bytes 4718596
  6.5 2.5 copy-start.3
  12.3 7.6 %copy-start.9 = (bf16[128,1536]{1,0:T(8,128)(2,1)S(1)}, bf16[128,1536]{1,0:T(8,128)(2,1)}, u32[]{:S(2)}) copy-start(bf16[128,1536]{1,0:T(8,128)(2,1)} %param.22) | copy-start | bytes 1179652
  12.3 115.6 %copy-start.5 = (s32[2,4,512]{2,1,0:T(4,128)S(1)}, s32[2,4,512]{2,1,0:T(4,128)}, u32[]{:S(2)}) copy-start(s32[2,4,512]{2,1,0:T(4,128)} %param.19) | copy-start | bytes 49156
  12.3 115.6 %all-to-all-start = ((bf16[16,4,296,128]{3,2,1,0:T(8,128)(2,1)}), bf16[16,4,296,128]{3,2,1,0:T(8,128)(2,1)}, u32[]{:S(2)}, u32[]{:S(2)}) async-start(bf16[16,4,296,128]{3,2,1,0:T(8,128)(2,1)} %pad_maximum_fusion), calls=%async_computation | async-start | bytes 9699328 | tf_op jit(solution)/shard_map/all_to_all | solution.py:330
  19.8 100.2 %all-gather.3.cloned.1.call-start = ((), (), s32[]{:S(2)}) async-start(), calls=%async_computation.2 | async-start | bytes 3342336 | tf_op jit(solution)/shard_map/all_gather | solution.py:333
  20.6 222.1 %all-gather.5.cloned.1.call-start = ((), (), s32[]{:S(2)}) async-start(), calls=%async_computation.3 | async-start | bytes 6684672 | tf_op jit(solution)/shard_map/all_gather | solution.py:338
  149.5 24.1 %copy-start.11 = (s32[4]{0:T(128)S(1)}, s32[4]{0:T(128)}, u32[]{:S(2)}) copy-start(s32[4]{0:T(128)} %param.20) | copy-start | bytes 52
  149.5 93.2 %all-to-all-start.1 = ((bf16[16,4,2,56,128]{4,3,2,1,0:T(8,128)(2,1)}), bf16[16,4,2,56,128]{4,3,2,1,0:T(8,128)(2,1)S(1)}, u32[]{:S(2)}, u32[]{:S(2)}) async-start(bf16[16,4,2,56,128]{4,3,2,1,0:T(8,128)(2,1)} %attention.1), calls=%async_computation.1 | async-start | bytes 3670016 | tf_op jit(solution)/shard_map/all_to_all | solution.py:340
  172.0 70.7 %collective-permute-start = (bf16[2048,768]{1,0:T(8,128)(2,1)}, bf16[2048,768]{1,0:T(8,128)(2,1)}, u32[]{:S(2)}, u32[]{:S(2)}) collective-permute-start(bf16[2048,768]{1,0:T(8,128)(2,1)} %all-gather.3.cloned.1.call-done.frozen_ref), channel_id=1, source_target_pairs={{0,16},{16,0},{1,17},{17,1},{2,18},{18,2},{3,19},{19,3},{4,20},{20... | collective-permute-start | bytes 9437192 | tf_op jit(solution)/shard_map/ppermute | solution.py:337
  242.7 1.2 copy-start.4
  243.9 15.8 %copy-start.10 = (s32[4]{0:T(128)S(1)}, s32[4]{0:T(128)}, u32[]{:S(2)}) copy-start(s32[4]{0:T(128)} %constant.168.clone) | copy-start | bytes 52
  258.0 3.1 collective-permute-start.2
  259.1 2.0 collective-permute-start.1
  261.1 0.8 copy-start.2
  261.1 1.0 copy-start.1
  265.4 13.8 %collective-permute-start.3 = (bf16[4,128,384]{2,1,0:T(8,128)(2,1)}, bf16[4,128,384]{2,1,0:T(8,128)(2,1)S(1)}, u32[]{:S(2)}, u32[]{:S(2)}) collective-permute-start(bf16[4,128,384]{2,1,0:T(8,128)(2,1)} %get-tuple-element.24), channel_id=1, source_target_pairs={{0,2},{1,3},{2,0},{3,1},{4,6},{5,7},{6,4},{7,5},{8,10},{9,11},{10,... | collective-permute-start | bytes 1179656 | tf_op jit(solution)/shard_map/ppermute | solution.py:249
  270.3 15.1 %collective-permute-start.6 = (bf16[4,128,384]{2,1,0:T(8,128)(2,1)}, bf16[4,128,384]{2,1,0:T(8,128)(2,1)S(1)}, u32[]{:S(2)}, u32[]{:S(2)}) collective-permute-start(bf16[4,128,384]{2,1,0:T(8,128)(2,1)} %get-tuple-element.26), channel_id=1, source_target_pairs={{0,2},{1,3},{2,0},{3,1},{4,6},{5,7},{6,4},{7,5},{8,10},{9,11},{10,... | collective-permute-start | bytes 1179656 | tf_op jit(solution)/shard_map/ppermute | solution.py:249
  270.7 17.6 %collective-permute-start.9 = (bf16[4,128,384]{2,1,0:T(8,128)(2,1)}, bf16[4,128,384]{2,1,0:T(8,128)(2,1)S(1)}, u32[]{:S(2)}, u32[]{:S(2)}) collective-permute-start(bf16[4,128,384]{2,1,0:T(8,128)(2,1)} %get-tuple-element.28), channel_id=1, source_target_pairs={{0,4},{1,5},{2,6},{3,7},{4,0},{5,1},{6,2},{7,3},{8,12},{9,13},{10,... | collective-permute-start | bytes 1179656 | tf_op jit(solution)/shard_map/ppermute | solution.py:249
  272.3 25.3 %collective-permute-start.12 = (bf16[4,128,384]{2,1,0:T(8,128)(2,1)}, bf16[4,128,384]{2,1,0:T(8,128)(2,1)S(1)}, u32[]{:S(2)}, u32[]{:S(2)}) collective-permute-start(bf16[4,128,384]{2,1,0:T(8,128)(2,1)} %get-tuple-element.30), channel_id=1, source_target_pairs={{0,4},{1,5},{2,6},{3,7},{4,0},{5,1},{6,2},{7,3},{8,12},{9,13},{10,... | collective-permute-start | bytes 1179656 | tf_op jit(solution)/shard_map/ppermute | solution.py:249
  275.9 3.3 %copy-start.8 = (bf16[4,128,384]{2,1,0:T(8,128)(2,1)S(1)}, bf16[4,128,384]{2,1,0:T(8,128)(2,1)}, u32[]{:S(2)}) copy-start(bf16[4,128,384]{2,1,0:T(8,128)(2,1)} %get-tuple-element.23) | copy-start | bytes 1179652
  275.9 12.3 %copy-start.7 = (bf16[4,128,384]{2,1,0:T(8,128)(2,1)S(1)}, bf16[4,128,384]{2,1,0:T(8,128)(2,1)}, u32[]{:S(2)}) copy-start(bf16[4,128,384]{2,1,0:T(8,128)(2,1)} %get-tuple-element.27) | copy-start | bytes 1179652
  279.2 18.4 %copy-start.6 = (bf16[4,128,384]{2,1,0:T(8,128)(2,1)S(1)}, bf16[4,128,384]{2,1,0:T(8,128)(2,1)}, u32[]{:S(2)}) copy-start(bf16[4,128,384]{2,1,0:T(8,128)(2,1)} %get-tuple-element.29) | copy-start | bytes 1179652
  279.3 22.5 %collective-permute-start.4 = (bf16[2,128,384]{2,1,0:T(8,128)(2,1)S(1)}, bf16[2,128,384]{2,1,0:T(8,128)(2,1)S(1)}, u32[]{:S(2)}, u32[]{:S(2)}) collective-permute-start(bf16[2,128,384]{2,1,0:T(8,128)(2,1)S(1)} %get-tuple-element.36), channel_id=1, source_target_pairs={{0,4},{1,5},{2,6},{3,7},{4,0},{5,1},{6,2},{7,3},{8,12},{9,13},{10,... | collective-permute-start | bytes 589832 | tf_op jit(solution)/shard_map/ppermute | solution.py:249
  286.5 18.4 %collective-permute-start.7 = (bf16[2,128,384]{2,1,0:T(8,128)(2,1)S(1)}, bf16[2,128,384]{2,1,0:T(8,128)(2,1)S(1)}, u32[]{:S(2)}, u32[]{:S(2)}) collective-permute-start(bf16[2,128,384]{2,1,0:T(8,128)(2,1)S(1)} %get-tuple-element.38), channel_id=1, source_target_pairs={{0,4},{1,5},{2,6},{3,7},{4,0},{5,1},{6,2},{7,3},{8,12},{9,13},{10,... | collective-permute-start | bytes 589832 | tf_op jit(solution)/shard_map/ppermute | solution.py:249
  288.4 18.2 %collective-permute-start.10 = (bf16[2,128,384]{2,1,0:T(8,128)(2,1)S(1)}, bf16[2,128,384]{2,1,0:T(8,128)(2,1)S(1)}, u32[]{:S(2)}, u32[]{:S(2)}) collective-permute-start(bf16[2,128,384]{2,1,0:T(8,128)(2,1)S(1)} %get-tuple-element.40), channel_id=1, source_target_pairs={{0,8},{1,9},{2,10},{3,11},{4,12},{5,13},{6,14},{7,15},{8,0},{9,1},... | collective-permute-start | bytes 589832 | tf_op jit(solution)/shard_map/ppermute | solution.py:249
  297.7 19.6 %collective-permute-start.13 = (bf16[2,128,384]{2,1,0:T(8,128)(2,1)S(1)}, bf16[2,128,384]{2,1,0:T(8,128)(2,1)S(1)}, u32[]{:S(2)}, u32[]{:S(2)}) collective-permute-start(bf16[2,128,384]{2,1,0:T(8,128)(2,1)S(1)} %get-tuple-element.42), channel_id=1, source_target_pairs={{0,8},{1,9},{2,10},{3,11},{4,12},{5,13},{6,14},{7,15},{8,0},{9,1},... | collective-permute-start | bytes 589832 | tf_op jit(solution)/shard_map/ppermute | solution.py:249
  301.9 17.0 %collective-permute-start.5 = (bf16[128,384]{1,0:T(8,128)(2,1)S(1)}, bf16[128,384]{1,0:T(8,128)(2,1)S(1)}, u32[]{:S(2)}, u32[]{:S(2)}) collective-permute-start(bf16[128,384]{1,0:T(8,128)(2,1)S(1)} %fusion.13), channel_id=1, source_target_pairs={{0,8},{1,9},{2,10},{3,11},{4,12},{5,13},{6,14},{7,15},{8,0},{9,1},... | collective-permute-start | bytes 294920 | tf_op jit(solution)/shard_map/ppermute | solution.py:249
  305.0 14.5 %collective-permute-start.8 = (bf16[128,384]{1,0:T(8,128)(2,1)S(1)}, bf16[128,384]{1,0:T(8,128)(2,1)S(1)}, u32[]{:S(2)}, u32[]{:S(2)}) collective-permute-start(bf16[128,384]{1,0:T(8,128)(2,1)S(1)} %fusion.15), channel_id=1, source_target_pairs={{0,8},{1,9},{2,10},{3,11},{4,12},{5,13},{6,14},{7,15},{8,0},{9,1},... | collective-permute-start | bytes 294920 | tf_op jit(solution)/shard_map/ppermute | solution.py:249
  306.6 12.9 %collective-permute-start.11 = (bf16[128,384]{1,0:T(8,128)(2,1)S(1)}, bf16[128,384]{1,0:T(8,128)(2,1)S(1)}, u32[]{:S(2)}, u32[]{:S(2)}) collective-permute-start(bf16[128,384]{1,0:T(8,128)(2,1)S(1)} %fusion.17), channel_id=1, source_target_pairs={{0,2},{1,3},{2,0},{3,1},{4,6},{5,7},{6,4},{7,5},{8,10},{9,11},{10,... | collective-permute-start | bytes 294920 | tf_op jit(solution)/shard_map/ppermute | solution.py:249
  317.3 4.7 %collective-permute-start.14 = (bf16[128,384]{1,0:T(8,128)(2,1)S(1)}, bf16[128,384]{1,0:T(8,128)(2,1)S(1)}, u32[]{:S(2)}, u32[]{:S(2)}) collective-permute-start(bf16[128,384]{1,0:T(8,128)(2,1)S(1)} %fusion.19), channel_id=1, source_target_pairs={{0,2},{1,3},{2,0},{3,1},{4,6},{5,7},{6,4},{7,5},{8,10},{9,11},{10,... | collective-permute-start | bytes 294920 | tf_op jit(solution)/shard_map/ppermute | solution.py:249
Sparse Core Ops, SparseCore 0:
  22.9 97.0 all-gather.2
  128.0 108.3 all-gather.4

commit v5 on v4

--- a/solution.py
+++ b/solution.py
@@ -98,19 +98,23 @@
 
 
 def head_kernel(
-    samples, image_dev, blocks_ref, back_ref, frozen_ref, frozen_other_ref, trainee_ref, states_ref, gate_ref,
-    scale_ref, head_ref, cot_ref, att_ref, both_s, mixed_s, square_s,
+    samples, image_dev, pieces, heads, back_ref, states_ref, gate_ref, scale_ref, head_ref, *refs,
 ):
+    frozen_refs, trainee_refs = refs[:pieces], refs[pieces:2 * pieces]
+    cot_ref, att_ref, both_s, mixed_s, square_s = refs[2 * pieces:]
     step = pl.program_id(0)
     rows = samples * image_dev
-    width = frozen_ref.shape[1]
+    width = frozen_refs[0].shape[1]
 
     @pl.when(step == 0)
     def _():
-        for h in range(HEADS):
+        for k in range(HEADS):
+            h = heads[k]
             for p in range(2):
-                piece = back_ref[h, :, p].astype(jnp.float32).reshape(rows, HEAD_DIM)
-                both_s[p * rows:(p + 1) * rows, h * HEAD_DIM:(h + 1) * HEAD_DIM] = piece.astype(jnp.bfloat16)
+                piece = back_ref[h, :, p].astype(jnp.float32).reshape(rows, HEAD_DIM).astype(jnp.bfloat16)
+                both_s[p * rows:(p + 1) * rows, k * HEAD_DIM:(k + 1) * HEAD_DIM] = piece
+                if p == 0:
+                    att_ref[h] = piece
         square_s[...] = jnp.zeros_like(square_s)
 
     def spread(values):
@@ -118,12 +122,15 @@
             [jnp.broadcast_to(values[b:b + 1, :], (image_dev, values.shape[1])) for b in range(samples)], axis=0
         )
 
-    columns = pl.ds(pl.multiple_of(blocks_ref[step] * width, 128), width)
+    def times(count, weight_refs):
+        weights = jnp.concatenate([weight_ref[...] for weight_ref in weight_refs], axis=0)
+        return jnp.dot(both_s[:count, :], weights, preferred_element_type=jnp.float32)
+
+    columns = pl.ds(pl.multiple_of(step * width, 128), width)
     states = states_ref[:, :, columns].astype(jnp.float32).reshape(rows, width)
     gate = spread(gate_ref[:, columns])
-    weights = jnp.where(step < pl.num_programs(0) // 2, frozen_ref[...], frozen_other_ref[...])
-    frozen = jnp.dot(both_s[...], weights, preferred_element_type=jnp.float32)
-    trainee = jnp.dot(both_s[:rows, :], trainee_ref[...], preferred_element_type=jnp.float32)
+    frozen = times(2 * rows, frozen_refs)
+    trainee = times(rows, trainee_refs)
     for k, branch in enumerate((frozen[:rows], frozen[rows:], trainee)):
         mixed = states + gate * branch
         mixed_s[k, :, columns] = mixed
@@ -155,32 +162,34 @@
         along = jnp.sum(inner * mixed, axis=1, keepdims=True) * (1.0 / WIDTH)
         cot = root * inner - mixed * (root * root * root * along)
         cot_ref[...] = (cot * spread(gate_ref[...])).astype(cot_ref.dtype)
-        for h in range(HEADS):
-            att_ref[h] = both_s[:rows, h * HEAD_DIM:(h + 1) * HEAD_DIM]
-
-
-def project(back, half, frozen, frozen_other, trainee, states, gate, scale, final_head):
+
+
+def project(back, heads, weights, states, gate, scale, final_head):
     samples, image_dev = states.shape[:2]
     rows = samples * image_dev
-    inner = trainee.shape[0]
+    inner = HEADS * HEAD_DIM
     width = 256
     steps = WIDTH // width
-    blocks = (jnp.arange(steps, dtype=jnp.int32) + half * (steps // 2)) % steps
-    whole = lambda shape: pl.BlockSpec(shape, lambda n, blocks: (0,) * len(shape))
+    whole = lambda shape: pl.BlockSpec(shape, lambda n, heads: (0,) * len(shape))
+    pieces = len(weights)
+
+    def block_of(piece):
+        x, first = piece
+        return pl.BlockSpec((x.shape[0], width), lambda n, heads: (0, n + first // width))
+
     return pl.pallas_call(
-        functools.partial(head_kernel, samples, image_dev),
+        functools.partial(head_kernel, samples, image_dev, pieces),
         grid_spec=pltpu.PrefetchScalarGridSpec(
             num_scalar_prefetch=1,
             grid=(steps,),
             in_specs=[
                 whole(back.shape),
-                pl.BlockSpec((inner, width), lambda n, blocks: (0, jnp.minimum(n, steps // 2 - 1))),
-                pl.BlockSpec((inner, width), lambda n, blocks: (0, jnp.maximum(n - steps // 2, 0))),
-                pl.BlockSpec((inner, width), lambda n, blocks: (0, blocks[n])),
                 whole(states.shape),
                 whole(gate.shape),
                 whole(scale.shape),
                 whole(final_head.shape),
+                *[block_of(frozen) for frozen, _ in weights],
+                *[block_of(trainee) for _, trainee in weights],
             ],
             out_specs=[whole((rows, WIDTH)), whole((HEADS, rows, HEAD_DIM))],
             scratch_shapes=[
@@ -200,7 +209,40 @@
             transcendentals=3 * rows,
         ),
         name="project",
-    )(blocks, back, frozen, frozen_other, trainee, states, gate, scale, final_head)
+    )(heads, back, states, gate, scale, final_head, *[x for (x, _), _ in weights],
+      *[x for _, (x, _) in weights])
+
+
+class RowGather:
+    def __init__(self, block, group_size):
+        self.group_size = group_size
+        self.own = block
+
+    def swap(self, x, k):
+        return lax.ppermute(x, "seq", [(s, s ^ (1 << k)) for s in range(self.group_size)])
+
+    def near(self, value):
+        line, pair = self.swap(self.own, 2), self.swap(self.own, 1)
+        value, self.own, line, pair = lax.optimization_barrier((value, self.own, line, pair))
+        self.blocks = {0: self.own, 4: line, 2: pair, 6: self.swap(line, 1), 8: self.swap(self.own, 3)}
+        return value
+
+    def far(self, value):
+        value, self.blocks = lax.optimization_barrier((value, self.blocks))
+        line, pair = self.swap(self.blocks[8], 2), self.swap(self.blocks[8], 1)
+        self.blocks |= {12: line, 10: pair}
+        self.corner = (self.swap(line[:, :WIDTH], 1), self.swap(pair[:, WIDTH:], 2))
+        return value
+
+    def rows(self, position):
+        pieces = {n: ((x, 0), (x, WIDTH)) for n, x in self.blocks.items()}
+        pieces[14] = tuple((x, 0) for x in self.corner)
+        for offset, x in list(self.blocks.items()):
+            other = self.swap(x, 0)
+            pieces[offset + 1] = ((other, 0), (other, WIDTH))
+        pieces[15] = tuple((self.swap(x, 0), 0) for x in self.corner)
+        offsets = jnp.array(list(pieces), jnp.int32)
+        return list(pieces.values()), (position ^ offsets).astype(jnp.int32)
 
 
 def product_kernel(first, mine, peer, att_ref, att_peer_ref, cot_ref, cot_peer_ref, *out_refs):
@@ -328,17 +370,20 @@
     scale = modulation[:, WIDTH:]
     exchange = functools.partial(lax.all_to_all, axis_name="seq", split_axis=0, concat_axis=0, tiled=True)
     gathered = exchange(jnp.concatenate([text_items, image_items], axis=2))
-    groups = lax.axis_size("grp")
-    half = lax.axis_index("grp") % 2
-    frozen = lax.all_gather(
-        lax.dynamic_slice_in_dim(frozen_out, half * (WIDTH // 2), WIDTH // 2, axis=1), "seq", axis=0, tiled=True
-    )
-    gathered, frozen, trainee_out = lax.optimization_barrier((gathered, frozen, trainee_out))
-    frozen_other = lax.ppermute(frozen, "grp", [(g, g ^ 1) for g in range(groups)])
-    all_trainee = lax.all_gather(trainee_out, "seq", axis=0, tiled=True)
+    block = jnp.concatenate([frozen_out, trainee_out], axis=1)
+    rows = RowGather(block, group_size)
+    if group_size == HEADS:
+        gathered = rows.near(gathered)
     both = attend(gathered, live, image_dev, text_dev)
+    if group_size == HEADS:
+        both = rows.far(both)
+        weights, heads = rows.rows(position)
+    else:
+        everything = lax.all_gather(block, "seq", axis=0, tiled=True)
+        all_rows = [((everything, 0), (everything, WIDTH))]
+        weights, heads = all_rows, jnp.arange(HEADS, dtype=jnp.int32)
     back = exchange(both).reshape(HEADS, SAMPLES, 2, image_dev, HEAD_DIM)
-    cot, att = project(back, half, frozen, frozen_other, all_trainee, image_states, gate, scale, final_head)
+    cot, att = project(back, heads, weights, image_states, gate, scale, final_head)
     if group_size == HEADS:
         return reduce_by_halving(att, cot, position, group_size)
     partial = jnp.einsum("hrd,rc->hdc", att, cot, preferred_element_type=jnp.float32)

time: 331 us -> 313 us (0.946)
  between operations: 13.6 us -> 0.28 us
  waiting for transfers between devices: 201 us -> 194 us
  local copies, waits for them, and re-layouts: 10.2 us -> 13.9 us
    all_gather x2 -> x0, waiting for transfers between devices: 99.3 us -> none  [the longest x1 99.3 us: shards(): lax.all_gather(lax.dynamic_slice_in_dim(frozen_out, half * (WIDTH // 2),...]
    ppermute x1 -> x17, waiting for transfers between devices: 65.3 us -> 161 us  [swap(): lax.ppermute(x, 'seq', [(s, s ^ 1 << k) for s in range(self.group_size)])]
    ppermute x1 -> x17, starting transfers between devices: 1.55 us -> 22.4 us  [swap(): lax.ppermute(x, 'seq', [(s, s ^ 1 << k) for s in range(self.group_size)])]
    all_to_all x1, starting transfers between devices: 22.5 us -> 5.28 us  [shards(): back = exchange(both).reshape(HEADS, SAMPLES, 2, image_dev, HEAD_DIM)]
    all_to_all x1, waiting for transfers between devices: 7.84 us -> 0.01 us  [shards(): gathered = exchange(jnp.concatenate([text_items, image_items], axis=2))]
    ppermute x14, waiting for transfers between devices: 28 us -> 33.5 us  [swap(): return lax.ppermute(x, 'seq', [(s, s ^ 1 << k) for s in range(group_size)])]
    ppermute x14, starting transfers between devices: 18.5 us -> 13.1 us  [swap(): return lax.ppermute(x, 'seq', [(s, s ^ 1 << k) for s in range(group_size)])]
    slice x0 -> x2, local copies, waits for them, and re-layouts: none -> 3.54 us  [far(): self.corner = (self.swap(line[:, :WIDTH], 1), self.swap(pair[:, WIDTH:], 2))]
  transfers between devices with their start and end apart: 19 -> 33, of which waited for: 11 -> 16; matrix products, arithmetic and copies ran while one was open for 3% -> 4% of each run, Pallas kernels for 9% -> 10%
where the time goes in v5:
time: 313 us; the launch traced here: 312 us
  waiting for transfers between devices  194 us (62%)
  starting transfers between devices  48.4 us (15%)
  Pallas kernels  47.6 us (15%)
  local copies, waits for them, and re-layouts  13.9 us (4%)
  other arithmetic  6.76 us (2%)
    ppermute x17, waiting for transfers between devices, swap(): lax.ppermute(x, 'seq', [(s, s ^ 1 << k) for s in range(self.group_size)])  161 us
    ppermute x14, waiting for transfers between devices, swap(): return lax.ppermute(x, 'seq', [(s, s ^ 1 << k) for s in range(group_size)])  33.5 us
    ppermute x17, starting transfers between devices, swap(): lax.ppermute(x, 'seq', [(s, s ^ 1 << k) for s in range(self.group_size)])  22.4 us
    pallas_call x1, Pallas kernels, attend(): pl.pallas_call(functools.partial(attention_kernel, image_dev, text_dev, b...  20.9 us
    pallas_call x1, Pallas kernels, project(): pl.pallas_call(functools.partial(head_kernel, samples, image_dev, pieces)...  13.7 us
    ppermute x14, starting transfers between devices, swap(): return lax.ppermute(x, 'seq', [(s, s ^ 1 << k) for s in range(group_size)])  13.1 us
    pallas_call x4, Pallas kernels, product(): pl.pallas_call(functools.partial(product_kernel, first), in_specs=[pl.Blo...  13 us
    all_to_all x1, starting transfers between devices, shards(): gathered = exchange(jnp.concatenate([text_items, image_items], axis=2))  7.56 us
  transfers between devices with their start and end apart: 33, of which 16 were waited for; matrix products, arithmetic and copies ran while one was open for 4% of the time, Pallas kernels for 10%

profile of v5, /device:TPU:0, one launch (start us, length us, event | category | flops | bytes accessed | tf_op | source)
XLA Modules:
  0.0 311.6 jit_solution(15142769089699677745)
XLA Ops:
  0.0 2.4 copy.24
  2.5 0.6 copy.23
  3.1 2.6 pad_maximum_fusion
  5.7 7.6 %all-to-all-start = ((bf16[16,4,296,128]{3,2,1,0:T(8,128)(2,1)}), bf16[16,4,296,128]{3,2,1,0:T(8,128)(2,1)}, u32[]{:S(2)}, u32[]{:S(2)}) async-start(bf16[16,4,296,128]{3,2,1,0:T(8,128)(2,1)} %pad_maximum_fusion), calls=%async_computation | async-start | bytes 9699328 | tf_op jit(solution)/shard_map/all_to_all | solution.py:372
  13.4 1.9 collective-permute-start
  15.4 1.5 collective-permute-start.1
  16.8 94.4 %collective-permute-done.refs_2_.refs_18_ = bf16[128,3072]{1,0:T(8,128)(2,1)S(1)} collective-permute-done((bf16[128,3072]{1,0:T(8,128)(2,1)S(1)}, bf16[128,3072]{1,0:T(8,128)(2,1)S(1)}, u32[]{:S(2)}, u32[]{:S(2)}) %collective-permute-start) | collective-permute-done | bytes 786464 | tf_op jit(solution)/shard_map/ppermute | solution.py:222
  111.3 1.7 collective-permute-start.2
  113.0 9.9 %collective-permute-start.3 = (bf16[128,3072]{1,0:T(8,128)(2,1)S(1)}, bf16[128,3072]{1,0:T(8,128)(2,1)}, u32[]{:S(2)}, u32[]{:S(2)}) collective-permute-start(bf16[128,3072]{1,0:T(8,128)(2,1)S(1)} %constant_dynamic-update-slice_fusion.refs_0_.refs_16_), channel_id=1, source_target_pairs={{0,8},{1,9},{2,10},{3,11},{4,12},{5,13},{6,14},{7,15},{8,0},{9,1},... | collective-permute-start | bytes 2359304 | tf_op jit(solution)/shard_map/ppermute | solution.py:222
  122.9 0.6 gather_fusion
  123.6 20.9 %attention.1 = bf16[16,4,2,56,128]{4,3,2,1,0:T(8,128)(2,1)} custom-call(bf16[16,4,296,128]{3,2,1,0:T(8,128)(2,1)} %all-to-all-done.x_ref, s32[4,2,512]{2,1,0:T(2,128)S(1)} %compare_convert_fusion.live_ref), custom_call_target="tpu_custom_call" | custom-call | flops 3523215360 | bytes 6684672 | tf_op jit(solution)/shard_map/attention/pallas_call | solution.py:72
  144.5 12.7 %collective-permute-done.3.refs_4_.refs_20_ = bf16[128,3072]{1,0:T(8,128)(2,1)} collective-permute-done((bf16[128,3072]{1,0:T(8,128)(2,1)S(1)}, bf16[128,3072]{1,0:T(8,128)(2,1)}, u32[]{:S(2)}, u32[]{:S(2)}) %collective-permute-start.3) | collective-permute-done | bytes 786464 | tf_op jit(solution)/shard_map/ppermute | solution.py:222
  157.1 5.3 %all-to-all-start.1 = ((bf16[16,4,2,56,128]{4,3,2,1,0:T(8,128)(2,1)}), bf16[16,4,2,56,128]{4,3,2,1,0:T(8,128)(2,1)S(1)}, u32[]{:S(2)}, u32[]{:S(2)}) async-start(bf16[16,4,2,56,128]{4,3,2,1,0:T(8,128)(2,1)} %attention.1), calls=%async_computation.1 | async-start | bytes 3670016 | tf_op jit(solution)/shard_map/all_to_all | solution.py:385
  162.4 2.0 collective-permute-start.4
  164.4 1.5 collective-permute-start.5
  165.9 0.5 collective-permute-start.10
  166.4 45.7 %collective-permute-done.4.refs_5_.refs_21_ = bf16[128,3072]{1,0:T(8,128)(2,1)} collective-permute-done((bf16[128,3072]{1,0:T(8,128)(2,1)}, bf16[128,3072]{1,0:T(8,128)(2,1)}, u32[]{:S(2)}, u32[]{:S(2)}) %collective-permute-start.4) | collective-permute-done | bytes 786464 | tf_op jit(solution)/shard_map/ppermute | solution.py:222
  212.2 1.8 slice.20
  214.0 0.5 collective-permute-start.9
  214.5 1.8 slice.21
  216.3 1.5 collective-permute-start.6
  217.8 1.0 collective-permute-start.15
  218.8 0.5 collective-permute-start.13
  219.3 0.6 broadcast_xor_fusion.heads
  219.8 1.9 copy.26.head_ref
  221.7 0.7 fusion.20
  222.4 5.2 %collective-permute-done.6.refs_7_ = bf16[128,1536]{1,0:T(8,128)(2,1)} collective-permute-done((bf16[128,1536]{1,0:T(8,128)(2,1)}, bf16[128,1536]{1,0:T(8,128)(2,1)}, u32[]{:S(2)}, u32[]{:S(2)}) %collective-permute-start.6) | collective-permute-done | bytes 393248 | tf_op jit(solution)/shard_map/ppermute | solution.py:222
  227.6 1.2 collective-permute-done.15.refs_23_
  228.9 0.6 fusion.30
  229.6 1.2 collective-permute-done.16.refs_31_
  230.8 0.7 copy-done.14
  231.5 1.2 copy-done.2
  232.8 13.7 %project.1 = (bf16[224,1536]{1,0:T(8,128)(2,1)}, bf16[16,224,128]{2,1,0:T(8,128)(2,1)}) custom-call(s32[16]{0:T(128)} %broadcast_xor_fusion.heads, bf16[16,4,2,56,128]{4,3,2,1,0:T(8,128)(2,1)} %copy-done.2, bf16[4,56,1536]{2,1,0:T(8,128)(2,1)} %states_ref.1, f32[4,1536]{1,0:T(4,128)} %get-tuple-element.58.gate_ref, f32[4,1536]{1,0:T(4,128)} %get-tuple-element.57.scale_ref, ...), custom_call_target="tpu_custom_call" | custom-call | flops 4227858432 | bytes 14417920 | tf_op jit(solution)/shard_map/project/pallas_call | solution.py:180
  246.7 1.0 dynamic-slice_bitcast_fusion
  247.8 0.4 collective-permute-start.17
  248.2 0.7 multiply_add_fusion
  248.9 0.7 collective-permute-done.17.att_peer_ref
  249.7 0.8 copy-done.3
  250.4 0.2 copy-done.1
  250.7 3.2 %product.5 = (bf16[4,128,384]{2,1,0:T(8,128)(2,1)}, bf16[4,128,384]{2,1,0:T(8,128)(2,1)}) custom-call(s32[8]{0:T(128)} %get-tuple-element.47.mine, s32[8]{0:T(128)} %get-tuple-element.48.peer, bf16[16,224,128]{2,1,0:T(8,128)(2,1)} %get-tuple-element.35.att_ref, bf16[8,224,128]{2,1,0:T(8,128)(2,1)} %copy-done.3, bf16[224,1536]{1,0:T(8,128)(2,1)} %get-tuple-element.36.cot_ref, ...), custom_call_target="tpu_custom_call" | custom-call | flops 352321536 | bytes 3080192 | tf_op jit(solution)/shard_map/product/pallas_call | solution.py:269
  253.9 0.9 collective-permute-start.19
  254.8 3.2 %product.7 = (bf16[4,128,384]{2,1,0:T(8,128)(2,1)}, bf16[4,128,384]{2,1,0:T(8,128)(2,1)}) custom-call(s32[8]{0:T(128)} %get-tuple-element.47.mine, s32[8]{0:T(128)} %get-tuple-element.48.peer, bf16[16,224,128]{2,1,0:T(8,128)(2,1)} %get-tuple-element.35.att_ref, bf16[8,224,128]{2,1,0:T(8,128)(2,1)} %copy-done.3, bf16[224,1536]{1,0:T(8,128)(2,1)} %get-tuple-element.36.cot_ref, ...), custom_call_target="tpu_custom_call" | custom-call | flops 352321536 | bytes 3080192 | tf_op jit(solution)/shard_map/product/pallas_call | solution.py:269
  258.0 1.2 collective-permute-start.22
  259.2 1.0 collective-permute-start.25
  260.1 1.1 collective-permute-start.28
  261.2 3.2 %product.4 = (bf16[4,128,384]{2,1,0:T(8,128)(2,1)}, bf16[4,128,384]{2,1,0:T(8,128)(2,1)}) custom-call(s32[8]{0:T(128)} %get-tuple-element.63.mine, s32[8]{0:T(128)} %get-tuple-element.64.peer, bf16[16,224,128]{2,1,0:T(8,128)(2,1)} %get-tuple-element.35.att_ref, bf16[8,224,128]{2,1,0:T(8,128)(2,1)} %copy-done.3, bf16[224,1536]{1,0:T(8,128)(2,1)} %get-tuple-element.36.cot_ref, ...), custom_call_target="tpu_custom_call" | custom-call | flops 352321536 | bytes 3080192 | tf_op jit(solution)/shard_map/product/pallas_call | solution.py:269
  264.5 3.3 %product.6 = (bf16[4,128,384]{2,1,0:T(8,128)(2,1)}, bf16[4,128,384]{2,1,0:T(8,128)(2,1)}) custom-call(s32[8]{0:T(128)} %get-tuple-element.63.mine, s32[8]{0:T(128)} %get-tuple-element.64.peer, bf16[16,224,128]{2,1,0:T(8,128)(2,1)} %get-tuple-element.35.att_ref, bf16[8,224,128]{2,1,0:T(8,128)(2,1)} %copy-done.3, bf16[224,1536]{1,0:T(8,128)(2,1)} %get-tuple-element.36.cot_ref, ...), custom_call_target="tpu_custom_call" | custom-call | flops 352321536 | bytes 3080192 | tf_op jit(solution)/shard_map/product/pallas_call | solution.py:269
  267.9 1.0 collective-permute-start.20
  268.9 5.0 %collective-permute-done.22 = bf16[4,128,384]{2,1,0:T(8,128)(2,1)S(1)} collective-permute-done((bf16[4,128,384]{2,1,0:T(8,128)(2,1)}, bf16[4,128,384]{2,1,0:T(8,128)(2,1)S(1)}, u32[]{:S(2)}, u32[]{:S(2)}) %collective-permute-start.22) | collective-permute-done | bytes 393248 | tf_op jit(solution)/shard_map/ppermute | solution.py:291
  273.9 1.1 add_convert_fusion.5
  275.1 1.0 collective-permute-start.23
  276.2 2.0 collective-permute-start.26
  278.2 7.9 %collective-permute-done.28 = bf16[4,128,384]{2,1,0:T(8,128)(2,1)S(1)} collective-permute-done((bf16[4,128,384]{2,1,0:T(8,128)(2,1)}, bf16[4,128,384]{2,1,0:T(8,128)(2,1)S(1)}, u32[]{:S(2)}, u32[]{:S(2)}) %collective-permute-start.28) | collective-permute-done | bytes 393248 | tf_op jit(solution)/shard_map/ppermute | solution.py:291
  286.3 4.0 %collective-permute-done.20 = bf16[2,128,384]{2,1,0:T(8,128)(2,1)S(1)} collective-permute-done((bf16[2,128,384]{2,1,0:T(8,128)(2,1)S(1)}, bf16[2,128,384]{2,1,0:T(8,128)(2,1)S(1)}, u32[]{:S(2)}, u32[]{:S(2)}) %collective-permute-start.20) | collective-permute-done | bytes 196640 | tf_op jit(solution)/shard_map/ppermute | solution.py:291
  290.4 1.3 collective-permute-start.21
  291.7 1.8 collective-permute-done.23
  293.5 1.2 collective-permute-start.24
  294.7 0.9 collective-permute-start.27
  295.6 10.3 %collective-permute-done.29 = bf16[2,128,384]{2,1,0:T(8,128)(2,1)S(1)} collective-permute-done((bf16[2,128,384]{2,1,0:T(8,128)(2,1)S(1)}, bf16[2,128,384]{2,1,0:T(8,128)(2,1)S(1)}, u32[]{:S(2)}, u32[]{:S(2)}) %collective-permute-start.29) | collective-permute-done | bytes 196640 | tf_op jit(solution)/shard_map/ppermute | solution.py:291
  305.9 0.9 collective-permute-start.30
  306.9 0.2 collective-permute-done.21
  307.1 1.0 collective-permute-done.24
  308.2 2.4 collective-permute-done.30
  310.7 1.0 pad_maximum_fusion.1
  (81 shorter events, 1.5 us)
Async XLA Ops:
  0.0 221.7 %copy-start = (bf16[256,3072]{1,0:T(8,128)(2,1)S(1)}, bf16[256,3072]{1,0:T(8,128)(2,1)}, u32[]{:S(2)}) copy-start(bf16[256,3072]{1,0:T(8,128)(2,1)} %param.25) | copy-start | bytes 4718596
  0.0 2.5 copy-start.6
  5.7 7.6 %copy-start.8 = (bf16[128,1536]{1,0:T(8,128)(2,1)S(1)}, bf16[128,1536]{1,0:T(8,128)(2,1)}, u32[]{:S(2)}) copy-start(bf16[128,1536]{1,0:T(8,128)(2,1)} %param.23) | copy-start | bytes 1179652
  5.7 7.6 %copy-start.9 = (bf16[128,1536]{1,0:T(8,128)(2,1)S(1)}, bf16[128,1536]{1,0:T(8,128)(2,1)}, u32[]{:S(2)}) copy-start(bf16[128,1536]{1,0:T(8,128)(2,1)} %param.24) | copy-start | bytes 1179652
  5.7 117.1 %copy-start.7 = (s32[2,4,512]{2,1,0:T(4,128)S(1)}, s32[2,4,512]{2,1,0:T(4,128)}, u32[]{:S(2)}) copy-start(s32[2,4,512]{2,1,0:T(4,128)} %param.20) | copy-start | bytes 49156
  5.7 105.5 %all-to-all-start = ((bf16[16,4,296,128]{3,2,1,0:T(8,128)(2,1)}), bf16[16,4,296,128]{3,2,1,0:T(8,128)(2,1)}, u32[]{:S(2)}, u32[]{:S(2)}) async-start(bf16[16,4,296,128]{3,2,1,0:T(8,128)(2,1)} %pad_maximum_fusion), calls=%async_computation | async-start | bytes 9699328 | tf_op jit(solution)/shard_map/all_to_all | solution.py:372
  13.4 131.0 %copy-start.4 = (bf16[128,3072]{1,0:T(8,128)(2,1)}, bf16[128,3072]{1,0:T(8,128)(2,1)S(1)}, u32[]{:S(2)}) copy-start(bf16[128,3072]{1,0:T(8,128)(2,1)S(1)} %constant_dynamic-update-slice_fusion.refs_0_.refs_16_) | copy-start | bytes 2359300
  13.4 97.8 %collective-permute-start = (bf16[128,3072]{1,0:T(8,128)(2,1)S(1)}, bf16[128,3072]{1,0:T(8,128)(2,1)S(1)}, u32[]{:S(2)}, u32[]{:S(2)}) collective-permute-start(bf16[128,3072]{1,0:T(8,128)(2,1)S(1)} %constant_dynamic-update-slice_fusion.refs_0_.refs_16_), channel_id=1, source_target_pairs={{0,4},{1,5},{2,6},{3,7},{4,0},{5,1},{6,2},{7,3},{8,12},{9,13},{10,... | collective-permute-start | bytes 2359304 | tf_op jit(solution)/shard_map/ppermute | solution.py:222
  15.4 95.9 %collective-permute-start.1 = (bf16[128,3072]{1,0:T(8,128)(2,1)S(1)}, bf16[128,3072]{1,0:T(8,128)(2,1)}, u32[]{:S(2)}, u32[]{:S(2)}) collective-permute-start(bf16[128,3072]{1,0:T(8,128)(2,1)S(1)} %constant_dynamic-update-slice_fusion.refs_0_.refs_16_), channel_id=1, source_target_pairs={{0,2},{1,3},{2,0},{3,1},{4,6},{5,7},{6,4},{7,5},{8,10},{9,11},{10,... | collective-permute-start | bytes 2359304 | tf_op jit(solution)/shard_map/ppermute | solution.py:222
  111.2 33.2 %copy-start.5 = (bf16[128,3072]{1,0:T(8,128)(2,1)}, bf16[128,3072]{1,0:T(8,128)(2,1)S(1)}, u32[]{:S(2)}) copy-start(bf16[128,3072]{1,0:T(8,128)(2,1)S(1)} %collective-permute-done.refs_2_.refs_18_) | copy-start | bytes 2359300
  111.3 33.2 %collective-permute-start.2 = (bf16[128,3072]{1,0:T(8,128)(2,1)S(1)}, bf16[128,3072]{1,0:T(8,128)(2,1)}, u32[]{:S(2)}, u32[]{:S(2)}) collective-permute-start(bf16[128,3072]{1,0:T(8,128)(2,1)S(1)} %collective-permute-done.refs_2_.refs_18_), channel_id=1, source_target_pairs={{0,2},{1,3},{2,0},{3,1},{4,6},{5,7},{6,4},{7,5},{8,10},{9,11},{10,... | collective-permute-start | bytes 2359304 | tf_op jit(solution)/shard_map/ppermute | solution.py:222
  113.0 44.2 %collective-permute-start.3 = (bf16[128,3072]{1,0:T(8,128)(2,1)S(1)}, bf16[128,3072]{1,0:T(8,128)(2,1)}, u32[]{:S(2)}, u32[]{:S(2)}) collective-permute-start(bf16[128,3072]{1,0:T(8,128)(2,1)S(1)} %constant_dynamic-update-slice_fusion.refs_0_.refs_16_), channel_id=1, source_target_pairs={{0,8},{1,9},{2,10},{3,11},{4,12},{5,13},{6,14},{7,15},{8,0},{9,1},... | collective-permute-start | bytes 2359304 | tf_op jit(solution)/shard_map/ppermute | solution.py:222
  144.4 67.6 %copy-start.16 = (s32[4]{0:T(128)S(1)}, s32[4]{0:T(128)}, u32[]{:S(2)}) copy-start(s32[4]{0:T(128)} %param.21) | copy-start | bytes 52
  144.4 74.8 %copy-start.17 = (s32[16]{0:T(128)S(1)}, s32[16]{0:T(128)}, u32[]{:S(2)}) copy-start(s32[16]{0:T(128)} %constant.140.clone) | copy-start | bytes 196
  157.1 74.4 %all-to-all-start.1 = ((bf16[16,4,2,56,128]{4,3,2,1,0:T(8,128)(2,1)}), bf16[16,4,2,56,128]{4,3,2,1,0:T(8,128)(2,1)S(1)}, u32[]{:S(2)}, u32[]{:S(2)}) async-start(bf16[16,4,2,56,128]{4,3,2,1,0:T(8,128)(2,1)} %attention.1), calls=%async_computation.1 | async-start | bytes 3670016 | tf_op jit(solution)/shard_map/all_to_all | solution.py:385
  162.4 49.7 %collective-permute-start.4 = (bf16[128,3072]{1,0:T(8,128)(2,1)}, bf16[128,3072]{1,0:T(8,128)(2,1)}, u32[]{:S(2)}, u32[]{:S(2)}) collective-permute-start(bf16[128,3072]{1,0:T(8,128)(2,1)} %collective-permute-done.3.refs_4_.refs_20_), channel_id=1, source_target_pairs={{0,4},{1,5},{2,6},{3,7},{4,0},{5,1},{6,2},{7,3},{8,12},{9,13},{10,... | collective-permute-start | bytes 2359304 | tf_op jit(solution)/shard_map/ppermute | solution.py:222
  164.4 49.6 %collective-permute-start.5 = (bf16[128,3072]{1,0:T(8,128)(2,1)}, bf16[128,3072]{1,0:T(8,128)(2,1)}, u32[]{:S(2)}, u32[]{:S(2)}) collective-permute-start(bf16[128,3072]{1,0:T(8,128)(2,1)} %collective-permute-done.3.refs_4_.refs_20_), channel_id=1, source_target_pairs={{0,2},{1,3},{2,0},{3,1},{4,6},{5,7},{6,4},{7,5},{8,10},{9,11},{10,... | collective-permute-start | bytes 2359304 | tf_op jit(solution)/shard_map/ppermute | solution.py:222
  165.9 50.4 %collective-permute-start.11 = (bf16[128,3072]{1,0:T(8,128)(2,1)}, bf16[128,3072]{1,0:T(8,128)(2,1)}, u32[]{:S(2)}, u32[]{:S(2)}) collective-permute-start(bf16[128,3072]{1,0:T(8,128)(2,1)} %collective-permute-done.3.refs_4_.refs_20_), channel_id=1, source_target_pairs={{0,1},{1,0},{2,3},{3,2},{4,5},{5,4},{6,7},{7,6},{8,9},{9,8},{10,11... | collective-permute-start | bytes 2359304 | tf_op jit(solution)/shard_map/ppermute | solution.py:222
  165.9 51.9 %collective-permute-start.10 = (bf16[128,3072]{1,0:T(8,128)(2,1)}, bf16[128,3072]{1,0:T(8,128)(2,1)}, u32[]{:S(2)}, u32[]{:S(2)}) collective-permute-start(bf16[128,3072]{1,0:T(8,128)(2,1)} %collective-permute-done.2.refs_3_.refs_19_), channel_id=1, source_target_pairs={{0,1},{1,0},{2,3},{3,2},{4,5},{5,4},{6,7},{7,6},{8,9},{9,8},{10,11... | collective-permute-start | bytes 2359304 | tf_op jit(solution)/shard_map/ppermute | solution.py:222
  166.4 52.4 %collective-permute-start.7 = (bf16[128,3072]{1,0:T(8,128)(2,1)}, bf16[128,3072]{1,0:T(8,128)(2,1)}, u32[]{:S(2)}, u32[]{:S(2)}) collective-permute-start(bf16[128,3072]{1,0:T(8,128)(2,1)} %copy-done.4), channel_id=1, source_target_pairs={{0,1},{1,0},{2,3},{3,2},{4,5},{5,4},{6,7},{7,6},{8,9},{9,8},{10,11... | collective-permute-start | bytes 2359304 | tf_op jit(solution)/shard_map/ppermute | solution.py:222
  212.1 6.7 %collective-permute-start.8 = (bf16[128,3072]{1,0:T(8,128)(2,1)}, bf16[128,3072]{1,0:T(8,128)(2,1)}, u32[]{:S(2)}, u32[]{:S(2)}) collective-permute-start(bf16[128,3072]{1,0:T(8,128)(2,1)} %collective-permute-done.1.refs_1_.refs_17_), channel_id=1, source_target_pairs={{0,1},{1,0},{2,3},{3,2},{4,5},{5,4},{6,7},{7,6},{8,9},{9,8},{10,11... | collective-permute-start | bytes 2359304 | tf_op jit(solution)/shard_map/ppermute | solution.py:222
  214.0 15.5 %collective-permute-start.9 = (bf16[128,3072]{1,0:T(8,128)(2,1)}, bf16[128,3072]{1,0:T(8,128)(2,1)}, u32[]{:S(2)}, u32[]{:S(2)}) collective-permute-start(bf16[128,3072]{1,0:T(8,128)(2,1)} %copy-done.5), channel_id=1, source_target_pairs={{0,1},{1,0},{2,3},{3,2},{4,5},{5,4},{6,7},{7,6},{8,9},{9,8},{10,11... | collective-permute-start | bytes 2359304 | tf_op jit(solution)/shard_map/ppermute | solution.py:222
  216.3 11.3 %collective-permute-start.6 = (bf16[128,1536]{1,0:T(8,128)(2,1)}, bf16[128,1536]{1,0:T(8,128)(2,1)}, u32[]{:S(2)}, u32[]{:S(2)}) collective-permute-start(bf16[128,1536]{1,0:T(8,128)(2,1)} %slice.20), channel_id=1, source_target_pairs={{0,2},{1,3},{2,0},{3,1},{4,6},{5,7},{6,4},{7,5},{8,10},{9,11},{10,... | collective-permute-start | bytes 1179656 | tf_op jit(solution)/shard_map/ppermute | solution.py:222
  217.8 11.1 %collective-permute-start.15 = (bf16[128,1536]{1,0:T(8,128)(2,1)}, bf16[128,1536]{1,0:T(8,128)(2,1)}, u32[]{:S(2)}, u32[]{:S(2)}) collective-permute-start(bf16[128,1536]{1,0:T(8,128)(2,1)} %slice.21), channel_id=1, source_target_pairs={{0,4},{1,5},{2,6},{3,7},{4,0},{5,1},{6,2},{7,3},{8,12},{9,13},{10,... | collective-permute-start | bytes 1179656 | tf_op jit(solution)/shard_map/ppermute | solution.py:222
  218.8 12.0 %collective-permute-start.12 = (bf16[128,3072]{1,0:T(8,128)(2,1)}, bf16[128,3072]{1,0:T(8,128)(2,1)}, u32[]{:S(2)}, u32[]{:S(2)}) collective-permute-start(bf16[128,3072]{1,0:T(8,128)(2,1)} %collective-permute-done.4.refs_5_.refs_21_), channel_id=1, source_target_pairs={{0,1},{1,0},{2,3},{3,2},{4,5},{5,4},{6,7},{7,6},{8,9},{9,8},{10,11... | collective-permute-start | bytes 2359304 | tf_op jit(solution)/shard_map/ppermute | solution.py:222
  218.8 12.8 %collective-permute-start.13 = (bf16[128,3072]{1,0:T(8,128)(2,1)}, bf16[128,3072]{1,0:T(8,128)(2,1)}, u32[]{:S(2)}, u32[]{:S(2)}) collective-permute-start(bf16[128,3072]{1,0:T(8,128)(2,1)} %collective-permute-done.5.refs_6_.refs_22_), channel_id=1, source_target_pairs={{0,1},{1,0},{2,3},{3,2},{4,5},{5,4},{6,7},{7,6},{8,9},{9,8},{10,11... | collective-permute-start | bytes 2359304 | tf_op jit(solution)/shard_map/ppermute | solution.py:222
  227.6 1.9 collective-permute-start.14
  228.9 1.9 collective-permute-start.16
  229.6 1.2 copy-start.13
  230.8 0.7 copy-start.14
  231.5 1.3 copy-start.2
  232.8 15.4 %copy-start.15 = (s32[4]{0:T(128)S(1)}, s32[4]{0:T(128)}, u32[]{:S(2)}) copy-start(s32[4]{0:T(128)} %constant.142.clone) | copy-start | bytes 52
  246.5 3.1 %collective-permute-start.18 = (bf16[224,1536]{1,0:T(8,128)(2,1)}, bf16[224,1536]{1,0:T(8,128)(2,1)S(1)}, u32[]{:S(2)}, u32[]{:S(2)}) collective-permute-start(bf16[224,1536]{1,0:T(8,128)(2,1)} %get-tuple-element.36.cot_ref), channel_id=1, source_target_pairs={{0,1},{1,0},{2,3},{3,2},{4,5},{5,4},{6,7},{7,6},{8,9},{9,8},{10,11... | collective-permute-start | bytes 2064392 | tf_op jit(solution)/shard_map/ppermute | solution.py:291
  247.8 1.9 collective-permute-start.17
  249.7 0.8 copy-start.3
  249.7 1.0 copy-start.1
  253.9 13.9 %collective-permute-start.19 = (bf16[4,128,384]{2,1,0:T(8,128)(2,1)}, bf16[4,128,384]{2,1,0:T(8,128)(2,1)S(1)}, u32[]{:S(2)}, u32[]{:S(2)}) collective-permute-start(bf16[4,128,384]{2,1,0:T(8,128)(2,1)} %get-tuple-element.38), channel_id=1, source_target_pairs={{0,2},{1,3},{2,0},{3,1},{4,6},{5,7},{6,4},{7,5},{8,10},{9,11},{10,... | collective-permute-start | bytes 1179656 | tf_op jit(solution)/shard_map/ppermute | solution.py:291
  258.0 15.9 %collective-permute-start.22 = (bf16[4,128,384]{2,1,0:T(8,128)(2,1)}, bf16[4,128,384]{2,1,0:T(8,128)(2,1)S(1)}, u32[]{:S(2)}, u32[]{:S(2)}) collective-permute-start(bf16[4,128,384]{2,1,0:T(8,128)(2,1)} %get-tuple-element.40), channel_id=1, source_target_pairs={{0,2},{1,3},{2,0},{3,1},{4,6},{5,7},{6,4},{7,5},{8,10},{9,11},{10,... | collective-permute-start | bytes 1179656 | tf_op jit(solution)/shard_map/ppermute | solution.py:291
  259.2 16.9 %collective-permute-start.25 = (bf16[4,128,384]{2,1,0:T(8,128)(2,1)}, bf16[4,128,384]{2,1,0:T(8,128)(2,1)S(1)}, u32[]{:S(2)}, u32[]{:S(2)}) collective-permute-start(bf16[4,128,384]{2,1,0:T(8,128)(2,1)} %get-tuple-element.42), channel_id=1, source_target_pairs={{0,4},{1,5},{2,6},{3,7},{4,0},{5,1},{6,2},{7,3},{8,12},{9,13},{10,... | collective-permute-start | bytes 1179656 | tf_op jit(solution)/shard_map/ppermute | solution.py:291
  260.1 26.0 %collective-permute-start.28 = (bf16[4,128,384]{2,1,0:T(8,128)(2,1)}, bf16[4,128,384]{2,1,0:T(8,128)(2,1)S(1)}, u32[]{:S(2)}, u32[]{:S(2)}) collective-permute-start(bf16[4,128,384]{2,1,0:T(8,128)(2,1)} %get-tuple-element.44), channel_id=1, source_target_pairs={{0,4},{1,5},{2,6},{3,7},{4,0},{5,1},{6,2},{7,3},{8,12},{9,13},{10,... | collective-permute-start | bytes 1179656 | tf_op jit(solution)/shard_map/ppermute | solution.py:291
  264.5 3.3 %copy-start.12 = (bf16[4,128,384]{2,1,0:T(8,128)(2,1)S(1)}, bf16[4,128,384]{2,1,0:T(8,128)(2,1)}, u32[]{:S(2)}) copy-start(bf16[4,128,384]{2,1,0:T(8,128)(2,1)} %get-tuple-element.37) | copy-start | bytes 1179652
  264.5 11.6 %copy-start.11 = (bf16[4,128,384]{2,1,0:T(8,128)(2,1)S(1)}, bf16[4,128,384]{2,1,0:T(8,128)(2,1)}, u32[]{:S(2)}) copy-start(bf16[4,128,384]{2,1,0:T(8,128)(2,1)} %get-tuple-element.41) | copy-start | bytes 1179652
  267.8 18.4 %copy-start.10 = (bf16[4,128,384]{2,1,0:T(8,128)(2,1)S(1)}, bf16[4,128,384]{2,1,0:T(8,128)(2,1)}, u32[]{:S(2)}) copy-start(bf16[4,128,384]{2,1,0:T(8,128)(2,1)} %get-tuple-element.43) | copy-start | bytes 1179652
  267.9 22.5 %collective-permute-start.20 = (bf16[2,128,384]{2,1,0:T(8,128)(2,1)S(1)}, bf16[2,128,384]{2,1,0:T(8,128)(2,1)S(1)}, u32[]{:S(2)}, u32[]{:S(2)}) collective-permute-start(bf16[2,128,384]{2,1,0:T(8,128)(2,1)S(1)} %get-tuple-element.50), channel_id=1, source_target_pairs={{0,4},{1,5},{2,6},{3,7},{4,0},{5,1},{6,2},{7,3},{8,12},{9,13},{10,... | collective-permute-start | bytes 589832 | tf_op jit(solution)/shard_map/ppermute | solution.py:291
  275.1 18.4 %collective-permute-start.23 = (bf16[2,128,384]{2,1,0:T(8,128)(2,1)S(1)}, bf16[2,128,384]{2,1,0:T(8,128)(2,1)S(1)}, u32[]{:S(2)}, u32[]{:S(2)}) collective-permute-start(bf16[2,128,384]{2,1,0:T(8,128)(2,1)S(1)} %get-tuple-element.52), channel_id=1, source_target_pairs={{0,4},{1,5},{2,6},{3,7},{4,0},{5,1},{6,2},{7,3},{8,12},{9,13},{10,... | collective-permute-start | bytes 589832 | tf_op jit(solution)/shard_map/ppermute | solution.py:291
  276.2 18.5 %collective-permute-start.26 = (bf16[2,128,384]{2,1,0:T(8,128)(2,1)S(1)}, bf16[2,128,384]{2,1,0:T(8,128)(2,1)S(1)}, u32[]{:S(2)}, u32[]{:S(2)}) collective-permute-start(bf16[2,128,384]{2,1,0:T(8,128)(2,1)S(1)} %get-tuple-element.54), channel_id=1, source_target_pairs={{0,8},{1,9},{2,10},{3,11},{4,12},{5,13},{6,14},{7,15},{8,0},{9,1},... | collective-permute-start | bytes 589832 | tf_op jit(solution)/shard_map/ppermute | solution.py:291
  286.3 19.7 %collective-permute-start.29 = (bf16[2,128,384]{2,1,0:T(8,128)(2,1)S(1)}, bf16[2,128,384]{2,1,0:T(8,128)(2,1)S(1)}, u32[]{:S(2)}, u32[]{:S(2)}) collective-permute-start(bf16[2,128,384]{2,1,0:T(8,128)(2,1)S(1)} %get-tuple-element.56), channel_id=1, source_target_pairs={{0,8},{1,9},{2,10},{3,11},{4,12},{5,13},{6,14},{7,15},{8,0},{9,1},... | collective-permute-start | bytes 589832 | tf_op jit(solution)/shard_map/ppermute | solution.py:291
  290.4 16.7 %collective-permute-start.21 = (bf16[128,384]{1,0:T(8,128)(2,1)S(1)}, bf16[128,384]{1,0:T(8,128)(2,1)S(1)}, u32[]{:S(2)}, u32[]{:S(2)}) collective-permute-start(bf16[128,384]{1,0:T(8,128)(2,1)S(1)} %fusion.13), channel_id=1, source_target_pairs={{0,8},{1,9},{2,10},{3,11},{4,12},{5,13},{6,14},{7,15},{8,0},{9,1},... | collective-permute-start | bytes 294920 | tf_op jit(solution)/shard_map/ppermute | solution.py:291
  293.5 14.6 %collective-permute-start.24 = (bf16[128,384]{1,0:T(8,128)(2,1)S(1)}, bf16[128,384]{1,0:T(8,128)(2,1)S(1)}, u32[]{:S(2)}, u32[]{:S(2)}) collective-permute-start(bf16[128,384]{1,0:T(8,128)(2,1)S(1)} %fusion.15), channel_id=1, source_target_pairs={{0,8},{1,9},{2,10},{3,11},{4,12},{5,13},{6,14},{7,15},{8,0},{9,1},... | collective-permute-start | bytes 294920 | tf_op jit(solution)/shard_map/ppermute | solution.py:291
  294.7 13.4 %collective-permute-start.27 = (bf16[128,384]{1,0:T(8,128)(2,1)S(1)}, bf16[128,384]{1,0:T(8,128)(2,1)S(1)}, u32[]{:S(2)}, u32[]{:S(2)}) collective-permute-start(bf16[128,384]{1,0:T(8,128)(2,1)S(1)} %fusion.17), channel_id=1, source_target_pairs={{0,2},{1,3},{2,0},{3,1},{4,6},{5,7},{6,4},{7,5},{8,10},{9,11},{10,... | collective-permute-start | bytes 294920 | tf_op jit(solution)/shard_map/ppermute | solution.py:291
  305.9 4.7 %collective-permute-start.30 = (bf16[128,384]{1,0:T(8,128)(2,1)S(1)}, bf16[128,384]{1,0:T(8,128)(2,1)S(1)}, u32[]{:S(2)}, u32[]{:S(2)}) collective-permute-start(bf16[128,384]{1,0:T(8,128)(2,1)S(1)} %fusion.19), channel_id=1, source_target_pairs={{0,2},{1,3},{2,0},{3,1},{4,6},{5,7},{6,4},{7,5},{8,10},{9,11},{10,... | collective-permute-start | bytes 294920 | tf_op jit(solution)/shard_map/ppermute | solution.py:291

commit v6 on v5

--- a/solution.py
+++ b/solution.py
@@ -113,8 +113,6 @@
             for p in range(2):
                 piece = back_ref[h, :, p].astype(jnp.float32).reshape(rows, HEAD_DIM).astype(jnp.bfloat16)
                 both_s[p * rows:(p + 1) * rows, k * HEAD_DIM:(k + 1) * HEAD_DIM] = piece
-                if p == 0:
-                    att_ref[h] = piece
         square_s[...] = jnp.zeros_like(square_s)
 
     def spread(values):
@@ -126,6 +124,11 @@
         weights = jnp.concatenate([weight_ref[...] for weight_ref in weight_refs], axis=0)
         return jnp.dot(both_s[:count, :], weights, preferred_element_type=jnp.float32)
 
+    share = -(-HEADS // (WIDTH // width))
+    for i in range(share):
+        k = jnp.minimum(step * share + i, HEADS - 1)
+        piece = both_s[:rows, pl.ds(pl.multiple_of(k * HEAD_DIM, HEAD_DIM), HEAD_DIM)]
+        att_ref[heads[k]] = piece.T
     columns = pl.ds(pl.multiple_of(step * width, 128), width)
     states = states_ref[:, :, columns].astype(jnp.float32).reshape(rows, width)
     gate = spread(gate_ref[:, columns])
@@ -191,7 +194,7 @@
                 *[block_of(frozen) for frozen, _ in weights],
                 *[block_of(trainee) for _, trainee in weights],
             ],
-            out_specs=[whole((rows, WIDTH)), whole((HEADS, rows, HEAD_DIM))],
+            out_specs=[whole((rows, WIDTH)), whole((HEADS, HEAD_DIM, rows))],
             scratch_shapes=[
                 pltpu.VMEM((2 * rows, inner), jnp.bfloat16),
                 pltpu.VMEM((3, rows, WIDTH), jnp.float32),
@@ -200,7 +203,7 @@
         ),
         out_shape=[
             jax.ShapeDtypeStruct((rows, WIDTH), jnp.bfloat16),
-            jax.ShapeDtypeStruct((HEADS, rows, HEAD_DIM), jnp.bfloat16),
+            jax.ShapeDtypeStruct((HEADS, HEAD_DIM, rows), jnp.bfloat16),
         ],
         compiler_params=pltpu.CompilerParams(dimension_semantics=("arbitrary",), vmem_limit_bytes=60 << 20),
         cost_estimate=pl.CostEstimate(
@@ -214,67 +217,74 @@
 
 
 class RowGather:
-    def __init__(self, block, group_size):
+    def __init__(self, frozen, trainee, group_size):
         self.group_size = group_size
-        self.own = block
+        self.parts = (frozen, trainee)
+        self.own = jnp.concatenate([frozen, trainee], axis=1)
 
     def swap(self, x, k):
         return lax.ppermute(x, "seq", [(s, s ^ (1 << k)) for s in range(self.group_size)])
 
     def near(self, value):
         line, pair = self.swap(self.own, 2), self.swap(self.own, 1)
-        value, self.own, line, pair = lax.optimization_barrier((value, self.own, line, pair))
-        self.blocks = {0: self.own, 4: line, 2: pair, 6: self.swap(line, 1), 8: self.swap(self.own, 3)}
+        value, self.own, self.parts, line, pair = lax.optimization_barrier(
+            (value, self.own, self.parts, line, pair)
+        )
+        self.blocks = {0: self.own, 4: line, 2: pair, 6: self.swap(line, 1)}
+        self.across = [self.swap(x, 3) for x in self.parts]
         return value
 
     def far(self, value):
-        value, self.blocks = lax.optimization_barrier((value, self.blocks))
-        line, pair = self.swap(self.blocks[8], 2), self.swap(self.blocks[8], 1)
-        self.blocks |= {12: line, 10: pair}
-        self.corner = (self.swap(line[:, :WIDTH], 1), self.swap(pair[:, WIDTH:], 2))
+        value, self.across[0] = lax.optimization_barrier((value, self.across[0]))
+        line, pair = [self.swap(self.across[0], k) for k in (2, 1)]
+        value, self.blocks, self.across, line, pair = lax.optimization_barrier(
+            (value, self.blocks, self.across, line, pair)
+        )
+        corner = self.swap(line, 1)
+        line_t, pair_t = [self.swap(self.across[1], k) for k in (2, 1)]
+        self.split = {8: tuple(self.across), 12: (line, line_t), 10: (pair, pair_t),
+                      14: (corner, self.swap(pair_t, 2))}
         return value
 
     def rows(self, position):
         pieces = {n: ((x, 0), (x, WIDTH)) for n, x in self.blocks.items()}
-        pieces[14] = tuple((x, 0) for x in self.corner)
-        for offset, x in list(self.blocks.items()):
+        pieces |= {n: tuple((x, 0) for x in pair) for n, pair in self.split.items()}
+        for offset, x in self.blocks.items():
             other = self.swap(x, 0)
             pieces[offset + 1] = ((other, 0), (other, WIDTH))
-        pieces[15] = tuple((self.swap(x, 0), 0) for x in self.corner)
+        for offset, pair in self.split.items():
+            pieces[offset + 1] = tuple((self.swap(x, 0), 0) for x in pair)
         offsets = jnp.array(list(pieces), jnp.int32)
         return list(pieces.values()), (position ^ offsets).astype(jnp.int32)
 
 
-def product_kernel(first, mine, peer, att_ref, att_peer_ref, cot_ref, cot_peer_ref, *out_refs):
+def product_kernel(starts, mine, peer, att_ref, att_peer_ref, cot_ref, cot_peer_ref, *out_refs):
     slots, _, width = out_refs[0].shape
-    for part, out_ref in enumerate(out_refs):
+    for part in range(2):
         picked = range(part * slots, (part + 1) * slots)
-        own = jnp.concatenate([att_ref[mine[i]] for i in picked], axis=1)
-        other = jnp.concatenate([att_peer_ref[peer[i]] for i in picked], axis=1)
-        start = first + part * (WIDTH // 2)
-        columns = slice(start, start + width)
-        total = lax.dot_general(
-            jnp.concatenate([own, other], axis=0),
-            jnp.concatenate([cot_ref[:, columns], cot_peer_ref[:, columns]], axis=0),
-            (((0,), (0,)), ((), ())),
-            preferred_element_type=jnp.float32,
-        )
-        out_ref[...] = total.reshape(out_ref.shape).astype(out_ref.dtype)
-
-
-def product(first, width, blocks, core, att, att_peer, cot, cot_peer):
+        own = jnp.concatenate([att_ref[mine[i]] for i in picked], axis=0)
+        other = jnp.concatenate([att_peer_ref[peer[i]] for i in picked], axis=0)
+        for start, out_ref in zip(starts, out_refs[part::2]):
+            columns = slice(part * (WIDTH // 2) + start, part * (WIDTH // 2) + start + width)
+            total = jnp.dot(own, cot_ref[:, columns], preferred_element_type=jnp.float32)
+            total += jnp.dot(other, cot_peer_ref[:, columns], preferred_element_type=jnp.float32)
+            out_ref[...] = total.reshape(out_ref.shape).astype(out_ref.dtype)
+
+
+def product(starts, width, blocks, core, att, att_peer, cot, cot_peer):
     slots = blocks.shape[0] // 2
     rows = cot.shape[0]
     out = jax.ShapeDtypeStruct((slots, HEAD_DIM, width), jnp.bfloat16)
+    count = 2 * len(starts)
     return pl.pallas_call(
-        functools.partial(product_kernel, first),
+        functools.partial(product_kernel, starts),
         in_specs=[pl.BlockSpec(memory_space=pltpu.SMEM)] * 2 + [pl.BlockSpec()] * 4,
-        out_specs=[pl.BlockSpec()] * 2,
-        out_shape=[out, out],
+        out_specs=[pl.BlockSpec()] * count,
+        out_shape=[out] * count,
         compiler_params=pltpu.CompilerParams(vmem_limit_bytes=VMEM_PRODUCT),
         cost_estimate=pl.CostEstimate(
-            flops=8 * slots * rows * HEAD_DIM * width,
-            bytes_accessed=4 * rows * (WIDTH + 2 * slots * HEAD_DIM) + 4 * slots * HEAD_DIM * width,
+            flops=4 * count * slots * rows * HEAD_DIM * width,
+            bytes_accessed=4 * rows * (WIDTH + 2 * slots * HEAD_DIM) + 2 * count * slots * HEAD_DIM * width,
             transcendentals=0,
         ),
         name="product",
@@ -293,7 +303,7 @@
     by_core = att.reshape(chips, 2, *att.shape[1:])
     cot_peer = swap(cot, 0)
     att_peer = swap(lax.dynamic_index_in_dim(by_core, 1 - bit[0], 1, keepdims=False), 0)
-    orders = (tuple(range(1, levels)), tuple(range(2, levels)) + (1,))
+    orders = (tuple(range(1, levels)), (2, 1) + tuple(range(3, levels)))
 
     def chip_blocks(keep):
         tables = []
@@ -307,12 +317,15 @@
     factors = (bit[0], att, att_peer, cot, cot_peer)
     state = {}
     arrived = {}
+    waves = tuple(wave * width for wave in range(WAVES))
+    sent_all = product(waves, width, chip_blocks(False), *factors)
     for wave in range(WAVES):
-        sent = product(wave * width, width, chip_blocks(False), *factors)
+        sent = sent_all[2 * wave:2 * wave + 2]
         for part, order in enumerate(orders):
             arrived[wave, part] = swap(sent[part], order[0])
+    kept_all = product(waves, width, chip_blocks(True), *factors)
     for wave in range(WAVES):
-        kept = product(wave * width, width, chip_blocks(True), *factors)
+        kept = kept_all[2 * wave:2 * wave + 2]
         for part, order in enumerate(orders):
             left = sorted(order[1:], reverse=True)
             shape = (2,) * len(left) + (HEAD_DIM, width)
@@ -370,15 +383,15 @@
     scale = modulation[:, WIDTH:]
     exchange = functools.partial(lax.all_to_all, axis_name="seq", split_axis=0, concat_axis=0, tiled=True)
     gathered = exchange(jnp.concatenate([text_items, image_items], axis=2))
-    block = jnp.concatenate([frozen_out, trainee_out], axis=1)
-    rows = RowGather(block, group_size)
     if group_size == HEADS:
+        rows = RowGather(frozen_out, trainee_out, group_size)
         gathered = rows.near(gathered)
     both = attend(gathered, live, image_dev, text_dev)
     if group_size == HEADS:
         both = rows.far(both)
         weights, heads = rows.rows(position)
     else:
+        block = jnp.concatenate([frozen_out, trainee_out], axis=1)
         everything = lax.all_gather(block, "seq", axis=0, tiled=True)
         all_rows = [((everything, 0), (everything, WIDTH))]
         weights, heads = all_rows, jnp.arange(HEADS, dtype=jnp.int32)
@@ -386,7 +399,7 @@
     cot, att = project(back, heads, weights, image_states, gate, scale, final_head)
     if group_size == HEADS:
         return reduce_by_halving(att, cot, position, group_size)
-    partial = jnp.einsum("hrd,rc->hdc", att, cot, preferred_element_type=jnp.float32)
+    partial = jnp.einsum("hdr,rc->hdc", att, cot, preferred_element_type=jnp.float32)
     partial = partial.reshape(HEADS * HEAD_DIM, WIDTH).astype(jnp.bfloat16)
     return lax.psum_scatter(partial, "seq", scatter_dimension=0, tiled=True).astype(jnp.float32)
 

time: 313 us -> 302 us (0.965)
  waiting for transfers between devices: 194 us -> 181 us
  Pallas kernels: 47.6 us -> 42.4 us
  starting transfers between devices: 48.4 us -> 52.2 us
  other arithmetic: 6.76 us -> 10.1 us
    ppermute x14, waiting for transfers between devices: 33.5 us -> 24.1 us  [swap(): return lax.ppermute(x, 'seq', [(s, s ^ 1 << k) for s in range(group_size)])]
    pallas_call x4 -> x2, Pallas kernels: 13 us -> 7.66 us  [product(): pl.pallas_call(functools.partial(product_kernel, starts), in_specs=[pl.Bl...]
    ppermute x14, starting transfers between devices: 13.1 us -> 16.7 us  [swap(): return lax.ppermute(x, 'seq', [(s, s ^ 1 << k) for s in range(group_size)])]
    slice x2 -> x0, local copies, waits for them, and re-layouts: 3.54 us -> none  [far(): self.corner = (self.swap(line[:, :WIDTH], 1), self.swap(pair[:, WIDTH:], 2))]
    unnamed x38 -> x56, local copies, waits for them, and re-layouts: 5.07 us -> 8.61 us
    ppermute x17 -> x23, waiting for transfers between devices: 161 us -> 157 us  [swap(): lax.ppermute(x, 'seq', [(s, s ^ 1 << k) for s in range(self.group_size)])]
    ppermute x17 -> x23, starting transfers between devices: 22.4 us -> 23.3 us  [swap(): lax.ppermute(x, 'seq', [(s, s ^ 1 << k) for s in range(self.group_size)])]
  transfers between devices with their start and end apart: 33 -> 39, of which waited for: 16 -> 17; matrix products, arithmetic and copies ran while one was open for 4% -> 4% of each run, Pallas kernels for 10% -> 8%
where the time goes in v6:
time: 302 us
  waiting for transfers between devices  181 us (60%)
  starting transfers between devices  52.2 us (17%)
  Pallas kernels  42.4 us (14%)
  local copies, waits for them, and re-layouts  14.6 us (5%)
  other arithmetic  10.1 us (3%)
    ppermute x23, waiting for transfers between devices, swap(): lax.ppermute(x, 'seq', [(s, s ^ 1 << k) for s in range(self.group_size)])  157 us
    ppermute x14, waiting for transfers between devices, swap(): return lax.ppermute(x, 'seq', [(s, s ^ 1 << k) for s in range(group_size)])  24.1 us
    ppermute x23, starting transfers between devices, swap(): lax.ppermute(x, 'seq', [(s, s ^ 1 << k) for s in range(self.group_size)])  23.3 us
    pallas_call x1, Pallas kernels, attend(): pl.pallas_call(functools.partial(attention_kernel, image_dev, text_dev, b...  20.8 us
    ppermute x14, starting transfers between devices, swap(): return lax.ppermute(x, 'seq', [(s, s ^ 1 << k) for s in range(group_size)])  16.7 us
    pallas_call x1, Pallas kernels, project(): pl.pallas_call(functools.partial(head_kernel, samples, image_dev, pieces)...  13.9 us
    unnamed x56, local copies, waits for them, and re-layouts  8.61 us
    pallas_call x2, Pallas kernels, product(): pl.pallas_call(functools.partial(product_kernel, starts), in_specs=[pl.Bl...  7.66 us
  transfers between devices with their start and end apart: 39, of which 17 were waited for; matrix products, arithmetic and copies ran while one was open for 4% of the time, Pallas kernels for 8%

profile of v6, /device:TPU:0, one launch (start us, length us, event | category | flops | bytes accessed | tf_op | source)
XLA Modules:
  0.0 301.5 jit_solution(10556057872086513058)
XLA Ops:
  0.0 2.4 copy.20
  2.5 0.6 copy.19
  3.1 2.6 pad_maximum_fusion
  5.8 7.6 %all-to-all-start = ((bf16[16,4,296,128]{3,2,1,0:T(8,128)(2,1)}), bf16[16,4,296,128]{3,2,1,0:T(8,128)(2,1)}, u32[]{:S(2)}, u32[]{:S(2)}) async-start(bf16[16,4,296,128]{3,2,1,0:T(8,128)(2,1)} %pad_maximum_fusion), calls=%async_computation | async-start | bytes 9699328 | tf_op jit(solution)/shard_map/all_to_all | solution.py:385
  13.5 1.9 collective-permute-start
  15.4 1.5 collective-permute-start.1
  16.9 0.6 pad_clamp_fusion
  17.5 1.3 gather_fusion
  18.8 92.5 %collective-permute-done.refs_2_.refs_18_ = bf16[128,3072]{1,0:T(8,128)(2,1)S(1)} collective-permute-done((bf16[128,3072]{1,0:T(8,128)(2,1)S(1)}, bf16[128,3072]{1,0:T(8,128)(2,1)S(1)}, u32[]{:S(2)}, u32[]{:S(2)}) %collective-permute-start) | collective-permute-done | bytes 786464 | tf_op jit(solution)/shard_map/ppermute | solution.py:226
  111.3 11.6 %collective-permute-start.2 = (bf16[128,1536]{1,0:T(8,128)(2,1)S(1)}, bf16[128,1536]{1,0:T(8,128)(2,1)S(1)}, u32[]{:S(2)}, u32[]{:S(2)}) collective-permute-start(bf16[128,1536]{1,0:T(8,128)(2,1)S(1)} %copy-done.8), channel_id=1, source_target_pairs={{0,8},{1,9},{2,10},{3,11},{4,12},{5,13},{6,14},{7,15},{8,0},{9,1},... | collective-permute-start | bytes 1179656 | tf_op jit(solution)/shard_map/ppermute | solution.py:226
  122.9 0.8 compare_convert_fusion.live_ref
  123.8 20.8 %attention.1 = bf16[16,4,2,56,128]{4,3,2,1,0:T(8,128)(2,1)} custom-call(bf16[16,4,296,128]{3,2,1,0:T(8,128)(2,1)} %all-to-all-done.x_ref, s32[4,2,512]{2,1,0:T(2,128)S(1)} %compare_convert_fusion.live_ref), custom_call_target="tpu_custom_call" | custom-call | flops 3523215360 | bytes 6684672 | tf_op jit(solution)/shard_map/attention/pallas_call | solution.py:72
  144.6 3.6 %collective-permute-done.2.refs_4_ = bf16[128,1536]{1,0:T(8,128)(2,1)S(1)} collective-permute-done((bf16[128,1536]{1,0:T(8,128)(2,1)S(1)}, bf16[128,1536]{1,0:T(8,128)(2,1)S(1)}, u32[]{:S(2)}, u32[]{:S(2)}) %collective-permute-start.2) | collective-permute-done | bytes 393248 | tf_op jit(solution)/shard_map/ppermute | solution.py:226
  148.2 0.8 copy-done.11
  149.0 1.3 collective-permute-start.6
  150.2 6.4 %collective-permute-done.4.refs_20_ = bf16[128,1536]{1,0:T(8,128)(2,1)S(1)} collective-permute-done((bf16[128,1536]{1,0:T(8,128)(2,1)}, bf16[128,1536]{1,0:T(8,128)(2,1)S(1)}, u32[]{:S(2)}, u32[]{:S(2)}) %collective-permute-start.4) | collective-permute-done | bytes 393248 | tf_op jit(solution)/shard_map/ppermute | solution.py:226
  156.6 8.3 %collective-permute-done.5.refs_5_ = bf16[128,1536]{1,0:T(8,128)(2,1)S(1)} collective-permute-done((bf16[128,1536]{1,0:T(8,128)(2,1)S(1)}, bf16[128,1536]{1,0:T(8,128)(2,1)S(1)}, u32[]{:S(2)}, u32[]{:S(2)}) %collective-permute-start.5) | collective-permute-done | bytes 393248 | tf_op jit(solution)/shard_map/ppermute | solution.py:226
  164.9 0.8 copy-done.13
  165.7 0.8 copy-done.14
  166.5 4.7 %all-to-all-start.1 = ((bf16[16,4,2,56,128]{4,3,2,1,0:T(8,128)(2,1)}), bf16[16,4,2,56,128]{4,3,2,1,0:T(8,128)(2,1)S(1)}, u32[]{:S(2)}, u32[]{:S(2)}) async-start(bf16[16,4,2,56,128]{4,3,2,1,0:T(8,128)(2,1)} %attention.1), calls=%async_computation.1 | async-start | bytes 3670016 | tf_op jit(solution)/shard_map/all_to_all | solution.py:398
  171.1 2.0 collective-permute-start.17
  173.1 1.5 collective-permute-start.16
  174.6 0.6 collective-permute-start.7
  175.6 22.2 %collective-permute-done.17.refs_22_ = bf16[128,1536]{1,0:T(8,128)(2,1)S(1)} collective-permute-done((bf16[128,1536]{1,0:T(8,128)(2,1)}, bf16[128,1536]{1,0:T(8,128)(2,1)S(1)}, u32[]{:S(2)}, u32[]{:S(2)}) %collective-permute-start.17) | collective-permute-done | bytes 393248 | tf_op jit(solution)/shard_map/ppermute | solution.py:226
  197.9 14.4 %collective-permute-done.16.refs_21_ = bf16[128,1536]{1,0:T(8,128)(2,1)S(1)} collective-permute-done((bf16[128,1536]{1,0:T(8,128)(2,1)}, bf16[128,1536]{1,0:T(8,128)(2,1)S(1)}, u32[]{:S(2)}, u32[]{:S(2)}) %collective-permute-start.16) | collective-permute-done | bytes 393248 | tf_op jit(solution)/shard_map/ppermute | solution.py:226
  212.3 0.7 collective-permute-start.18
  213.2 0.5 copy-done.17
  213.7 0.8 copy-done.18
  215.4 8.4 %collective-permute-done.18.refs_23_ = bf16[128,1536]{1,0:T(8,128)(2,1)S(1)} collective-permute-done((bf16[128,1536]{1,0:T(8,128)(2,1)S(1)}, bf16[128,1536]{1,0:T(8,128)(2,1)S(1)}, u32[]{:S(2)}, u32[]{:S(2)}) %collective-permute-start.18) | collective-permute-done | bytes 393248 | tf_op jit(solution)/shard_map/ppermute | solution.py:226
  223.8 0.6 collective-permute-start.9
  225.1 0.6 broadcast_xor_fusion.heads
  225.7 1.9 copy.22.head_ref
  227.6 0.7 fusion.20
  228.4 0.6 fusion.30
  229.1 1.4 collective-permute-done.22.refs_31_
  230.4 1.2 copy-done.1
  231.7 13.9 %project.1 = (bf16[224,1536]{1,0:T(8,128)(2,1)}, bf16[16,128,224]{2,1,0:T(8,128)(2,1)}) custom-call(s32[16]{0:T(128)} %broadcast_xor_fusion.heads, bf16[16,4,2,56,128]{4,3,2,1,0:T(8,128)(2,1)} %copy-done.1, bf16[4,56,1536]{2,1,0:T(8,128)(2,1)} %states_ref.1, f32[4,1536]{1,0:T(4,128)} %get-tuple-element.72.gate_ref, f32[4,1536]{1,0:T(4,128)} %get-tuple-element.71.scale_ref, ...), custom_call_target="tpu_custom_call" | custom-call | flops 4227858432 | bytes 14417920 | tf_op jit(solution)/shard_map/project/pallas_call | solution.py:183
  245.7 1.1 dynamic-slice_bitcast_fusion
  247.3 0.7 multiply_add_fusion
  247.9 0.8 collective-permute-done.23.att_peer_ref
  248.8 0.8 copy-done.6
  249.8 3.8 %product.3 = (bf16[4,128,384]{2,1,0:T(8,128)(2,1)}, bf16[4,128,384]{2,1,0:T(8,128)(2,1)}, bf16[4,128,384]{2,1,0:T(8,128)(2,1)}, bf16[4,128,384]{2,1,0:T(8,128)(2,1)}) custom-call(s32[8]{0:T(128)} %get-tuple-element.61.mine, s32[8]{0:T(128)} %get-tuple-element.62.peer, bf16[16,128,224]{2,1,0:T(8,128)(2,1)} %get-tuple-element.49.att_ref, ...), custom_call_target="tpu_custom_call" | custom-call | flops 704643072 | bytes 3866624 | tf_op jit(solution)/shard_map/product/pallas_call | solution.py:279
  253.6 1.5 collective-permute-start.25
  255.7 0.6 collective-permute-start.31
  256.3 1.4 collective-permute-start.34
  257.7 3.8 %product.2 = (bf16[4,128,384]{2,1,0:T(8,128)(2,1)}, bf16[4,128,384]{2,1,0:T(8,128)(2,1)}, bf16[4,128,384]{2,1,0:T(8,128)(2,1)}, bf16[4,128,384]{2,1,0:T(8,128)(2,1)}) custom-call(s32[8]{0:T(128)} %get-tuple-element.77.mine, s32[8]{0:T(128)} %get-tuple-element.78.peer, bf16[16,128,224]{2,1,0:T(8,128)(2,1)} %get-tuple-element.49.att_ref, ...), custom_call_target="tpu_custom_call" | custom-call | flops 704643072 | bytes 3866624 | tf_op jit(solution)/shard_map/product/pallas_call | solution.py:279
  261.5 4.3 %collective-permute-done.25 = bf16[4,128,384]{2,1,0:T(8,128)(2,1)S(1)} collective-permute-done((bf16[4,128,384]{2,1,0:T(8,128)(2,1)}, bf16[4,128,384]{2,1,0:T(8,128)(2,1)S(1)}, u32[]{:S(2)}, u32[]{:S(2)}) %collective-permute-start.25) | collective-permute-done | bytes 393248 | tf_op jit(solution)/shard_map/ppermute | solution.py:301
  265.8 1.1 add_convert_fusion.7
  266.9 0.7 collective-permute-start.26
  267.6 6.1 %collective-permute-done.28 = bf16[4,128,384]{2,1,0:T(8,128)(2,1)S(1)} collective-permute-done((bf16[4,128,384]{2,1,0:T(8,128)(2,1)}, bf16[4,128,384]{2,1,0:T(8,128)(2,1)S(1)}, u32[]{:S(2)}, u32[]{:S(2)}) %collective-permute-start.28) | collective-permute-done | bytes 393248 | tf_op jit(solution)/shard_map/ppermute | solution.py:301
  273.7 1.1 add_convert_fusion.5
  274.8 0.8 collective-permute-start.29
  275.6 1.1 add_convert_fusion.3
  276.7 1.8 collective-permute-start.32
  279.0 1.5 collective-permute-done.26
  280.6 2.6 collective-permute-start.27
  283.2 1.5 collective-permute-done.29
  284.7 2.7 collective-permute-start.30
  287.8 2.7 collective-permute-start.36
  290.5 3.8 %collective-permute-done.27 = bf16[128,384]{1,0:T(8,128)(2,1)S(1)} collective-permute-done((bf16[128,384]{1,0:T(8,128)(2,1)S(1)}, bf16[128,384]{1,0:T(8,128)(2,1)S(1)}, u32[]{:S(2)}, u32[]{:S(2)}) %collective-permute-start.27) | collective-permute-done | bytes 98336 | tf_op jit(solution)/shard_map/ppermute | solution.py:301
  294.3 2.1 collective-permute-done.30
  296.4 2.1 collective-permute-done.33
  298.5 2.0 collective-permute-done.36
  300.5 1.0 pad_maximum_fusion.1
  (107 shorter events, 5.3 us)
Async XLA Ops:
  0.0 227.6 %copy-start = (bf16[256,3072]{1,0:T(8,128)(2,1)S(1)}, bf16[256,3072]{1,0:T(8,128)(2,1)}, u32[]{:S(2)}) copy-start(bf16[256,3072]{1,0:T(8,128)(2,1)} %param.21) | copy-start | bytes 4718596
  0.0 2.5 copy-start.5
  5.8 7.6 %copy-start.8 = (bf16[128,1536]{1,0:T(8,128)(2,1)S(1)}, bf16[128,1536]{1,0:T(8,128)(2,1)}, u32[]{:S(2)}) copy-start(bf16[128,1536]{1,0:T(8,128)(2,1)} %param.19) | copy-start | bytes 1179652
  5.8 7.6 %copy-start.9 = (bf16[128,1536]{1,0:T(8,128)(2,1)S(1)}, bf16[128,1536]{1,0:T(8,128)(2,1)}, u32[]{:S(2)}) copy-start(bf16[128,1536]{1,0:T(8,128)(2,1)} %param.20) | copy-start | bytes 1179652
  5.8 11.7 %copy-start.7 = (s32[2,4,512]{2,1,0:T(4,128)S(1)}, s32[2,4,512]{2,1,0:T(4,128)}, u32[]{:S(2)}) copy-start(s32[2,4,512]{2,1,0:T(4,128)} %param.16) | copy-start | bytes 49156
  5.8 105.5 %all-to-all-start = ((bf16[16,4,296,128]{3,2,1,0:T(8,128)(2,1)}), bf16[16,4,296,128]{3,2,1,0:T(8,128)(2,1)}, u32[]{:S(2)}, u32[]{:S(2)}) async-start(bf16[16,4,296,128]{3,2,1,0:T(8,128)(2,1)} %pad_maximum_fusion), calls=%async_computation | async-start | bytes 9699328 | tf_op jit(solution)/shard_map/all_to_all | solution.py:385
  13.4 131.2 %copy-start.2 = (bf16[128,3072]{1,0:T(8,128)(2,1)}, bf16[128,3072]{1,0:T(8,128)(2,1)S(1)}, u32[]{:S(2)}) copy-start(bf16[128,3072]{1,0:T(8,128)(2,1)S(1)} %constant_dynamic-update-slice_fusion.refs_0_.refs_16_) | copy-start | bytes 2359300
  13.5 97.8 %collective-permute-start = (bf16[128,3072]{1,0:T(8,128)(2,1)S(1)}, bf16[128,3072]{1,0:T(8,128)(2,1)S(1)}, u32[]{:S(2)}, u32[]{:S(2)}) collective-permute-start(bf16[128,3072]{1,0:T(8,128)(2,1)S(1)} %constant_dynamic-update-slice_fusion.refs_0_.refs_16_), channel_id=1, source_target_pairs={{0,4},{1,5},{2,6},{3,7},{4,0},{5,1},{6,2},{7,3},{8,12},{9,13},{10,... | collective-permute-start | bytes 2359304 | tf_op jit(solution)/shard_map/ppermute | solution.py:226
  15.4 95.9 %collective-permute-start.1 = (bf16[128,3072]{1,0:T(8,128)(2,1)S(1)}, bf16[128,3072]{1,0:T(8,128)(2,1)}, u32[]{:S(2)}, u32[]{:S(2)}) collective-permute-start(bf16[128,3072]{1,0:T(8,128)(2,1)S(1)} %constant_dynamic-update-slice_fusion.refs_0_.refs_16_), channel_id=1, source_target_pairs={{0,2},{1,3},{2,0},{3,1},{4,6},{5,7},{6,4},{7,5},{8,10},{9,11},{10,... | collective-permute-start | bytes 2359304 | tf_op jit(solution)/shard_map/ppermute | solution.py:226
  111.3 33.3 %copy-start.3 = (bf16[128,3072]{1,0:T(8,128)(2,1)}, bf16[128,3072]{1,0:T(8,128)(2,1)S(1)}, u32[]{:S(2)}) copy-start(bf16[128,3072]{1,0:T(8,128)(2,1)S(1)} %collective-permute-done.refs_2_.refs_18_) | copy-start | bytes 2359300
  111.3 36.9 %collective-permute-start.2 = (bf16[128,1536]{1,0:T(8,128)(2,1)S(1)}, bf16[128,1536]{1,0:T(8,128)(2,1)S(1)}, u32[]{:S(2)}, u32[]{:S(2)}) collective-permute-start(bf16[128,1536]{1,0:T(8,128)(2,1)S(1)} %copy-done.8), channel_id=1, source_target_pairs={{0,8},{1,9},{2,10},{3,11},{4,12},{5,13},{6,14},{7,15},{8,0},{9,1},... | collective-permute-start | bytes 1179656 | tf_op jit(solution)/shard_map/ppermute | solution.py:226
  122.9 43.6 %collective-permute-start.3 = (bf16[128,3072]{1,0:T(8,128)(2,1)S(1)}, bf16[128,3072]{1,0:T(8,128)(2,1)}, u32[]{:S(2)}, u32[]{:S(2)}) collective-permute-start(bf16[128,3072]{1,0:T(8,128)(2,1)S(1)} %collective-permute-done.refs_2_.refs_18_), channel_id=1, source_target_pairs={{0,2},{1,3},{2,0},{3,1},{4,6},{5,7},{6,4},{7,5},{8,10},{9,11},{10,... | collective-permute-start | bytes 2359304 | tf_op jit(solution)/shard_map/ppermute | solution.py:226
  123.7 32.9 %collective-permute-start.4 = (bf16[128,1536]{1,0:T(8,128)(2,1)}, bf16[128,1536]{1,0:T(8,128)(2,1)S(1)}, u32[]{:S(2)}, u32[]{:S(2)}) collective-permute-start(bf16[128,1536]{1,0:T(8,128)(2,1)} %param.20), channel_id=1, source_target_pairs={{0,8},{1,9},{2,10},{3,11},{4,12},{5,13},{6,14},{7,15},{8,0},{9,1},... | collective-permute-start | bytes 1179656 | tf_op jit(solution)/shard_map/ppermute | solution.py:226
  148.2 0.8 copy-start.11
  148.2 66.5 %copy-start.25 = (s32[4]{0:T(128)S(1)}, s32[4]{0:T(128)}, u32[]{:S(2)}) copy-start(s32[4]{0:T(128)} %param.17) | copy-start | bytes 52
  148.2 77.0 %copy-start.26 = (s32[16]{0:T(128)S(1)}, s32[16]{0:T(128)}, u32[]{:S(2)}) copy-start(s32[16]{0:T(128)} %constant.138.clone) | copy-start | bytes 196
  148.2 16.8 %collective-permute-start.5 = (bf16[128,1536]{1,0:T(8,128)(2,1)S(1)}, bf16[128,1536]{1,0:T(8,128)(2,1)S(1)}, u32[]{:S(2)}, u32[]{:S(2)}) collective-permute-start(bf16[128,1536]{1,0:T(8,128)(2,1)S(1)} %collective-permute-done.2.refs_4_), channel_id=1, source_target_pairs={{0,4},{1,5},{2,6},{3,7},{4,0},{5,1},{6,2},{7,3},{8,12},{9,13},{10,... | collective-permute-start | bytes 1179656 | tf_op jit(solution)/shard_map/ppermute | solution.py:226
  149.0 16.0 %collective-permute-start.6 = (bf16[128,1536]{1,0:T(8,128)(2,1)S(1)}, bf16[128,1536]{1,0:T(8,128)(2,1)S(1)}, u32[]{:S(2)}, u32[]{:S(2)}) collective-permute-start(bf16[128,1536]{1,0:T(8,128)(2,1)S(1)} %collective-permute-done.2.refs_4_), channel_id=1, source_target_pairs={{0,2},{1,3},{2,0},{3,1},{4,6},{5,7},{6,4},{7,5},{8,10},{9,11},{10,... | collective-permute-start | bytes 1179656 | tf_op jit(solution)/shard_map/ppermute | solution.py:226
  156.6 8.3 %copy-start.12 = (bf16[128,1536]{1,0:T(8,128)(2,1)}, bf16[128,1536]{1,0:T(8,128)(2,1)S(1)}, u32[]{:S(2)}) copy-start(bf16[128,1536]{1,0:T(8,128)(2,1)S(1)} %collective-permute-done.4.refs_20_) | copy-start | bytes 1179652
  164.9 0.8 copy-start.13
  166.5 64.0 %all-to-all-start.1 = ((bf16[16,4,2,56,128]{4,3,2,1,0:T(8,128)(2,1)}), bf16[16,4,2,56,128]{4,3,2,1,0:T(8,128)(2,1)S(1)}, u32[]{:S(2)}, u32[]{:S(2)}) async-start(bf16[16,4,2,56,128]{4,3,2,1,0:T(8,128)(2,1)} %attention.1), calls=%async_computation.1 | async-start | bytes 3670016 | tf_op jit(solution)/shard_map/all_to_all | solution.py:398
  171.1 26.8 %collective-permute-start.17 = (bf16[128,1536]{1,0:T(8,128)(2,1)}, bf16[128,1536]{1,0:T(8,128)(2,1)S(1)}, u32[]{:S(2)}, u32[]{:S(2)}) collective-permute-start(bf16[128,1536]{1,0:T(8,128)(2,1)} %copy-done.12), channel_id=1, source_target_pairs={{0,2},{1,3},{2,0},{3,1},{4,6},{5,7},{6,4},{7,5},{8,10},{9,11},{10,... | collective-permute-start | bytes 1179656 | tf_op jit(solution)/shard_map/ppermute | solution.py:226
  173.1 39.1 %collective-permute-start.16 = (bf16[128,1536]{1,0:T(8,128)(2,1)}, bf16[128,1536]{1,0:T(8,128)(2,1)S(1)}, u32[]{:S(2)}, u32[]{:S(2)}) collective-permute-start(bf16[128,1536]{1,0:T(8,128)(2,1)} %copy-done.12), channel_id=1, source_target_pairs={{0,4},{1,5},{2,6},{3,7},{4,0},{5,1},{6,2},{7,3},{8,12},{9,13},{10,... | collective-permute-start | bytes 1179656 | tf_op jit(solution)/shard_map/ppermute | solution.py:226
  174.6 37.7 %collective-permute-start.7 = (bf16[128,1536]{1,0:T(8,128)(2,1)}, bf16[128,1536]{1,0:T(8,128)(2,1)}, u32[]{:S(2)}, u32[]{:S(2)}) collective-permute-start(bf16[128,1536]{1,0:T(8,128)(2,1)} %copy-done.13), channel_id=1, source_target_pairs={{0,2},{1,3},{2,0},{3,1},{4,6},{5,7},{6,4},{7,5},{8,10},{9,11},{10,... | collective-permute-start | bytes 1179656 | tf_op jit(solution)/shard_map/ppermute | solution.py:226
  175.1 37.8 %collective-permute-start.19 = (bf16[128,1536]{1,0:T(8,128)(2,1)}, bf16[128,1536]{1,0:T(8,128)(2,1)S(1)}, u32[]{:S(2)}, u32[]{:S(2)}) collective-permute-start(bf16[128,1536]{1,0:T(8,128)(2,1)} %copy-done.12), channel_id=1, source_target_pairs={{0,1},{1,0},{2,3},{3,2},{4,5},{5,4},{6,7},{7,6},{8,9},{9,8},{10,11... | collective-permute-start | bytes 1179656 | tf_op jit(solution)/shard_map/ppermute | solution.py:226
  175.1 38.6 %collective-permute-start.13 = (bf16[128,1536]{1,0:T(8,128)(2,1)}, bf16[128,1536]{1,0:T(8,128)(2,1)S(1)}, u32[]{:S(2)}, u32[]{:S(2)}) collective-permute-start(bf16[128,1536]{1,0:T(8,128)(2,1)} %copy-done.13), channel_id=1, source_target_pairs={{0,1},{1,0},{2,3},{3,2},{4,5},{5,4},{6,7},{7,6},{8,9},{9,8},{10,11... | collective-permute-start | bytes 1179656 | tf_op jit(solution)/shard_map/ppermute | solution.py:226
  197.9 15.1 %copy-start.15 = (bf16[128,1536]{1,0:T(8,128)(2,1)}, bf16[128,1536]{1,0:T(8,128)(2,1)S(1)}, u32[]{:S(2)}) copy-start(bf16[128,1536]{1,0:T(8,128)(2,1)S(1)} %collective-permute-done.17.refs_22_) | copy-start | bytes 1179652
  197.9 16.9 %collective-permute-start.12 = (bf16[128,1536]{1,0:T(8,128)(2,1)}, bf16[128,1536]{1,0:T(8,128)(2,1)S(1)}, u32[]{:S(2)}, u32[]{:S(2)}) collective-permute-start(bf16[128,1536]{1,0:T(8,128)(2,1)} %copy-done.11), channel_id=1, source_target_pairs={{0,1},{1,0},{2,3},{3,2},{4,5},{5,4},{6,7},{7,6},{8,9},{9,8},{10,11... | collective-permute-start | bytes 1179656 | tf_op jit(solution)/shard_map/ppermute | solution.py:226
  212.3 11.6 %copy-start.16 = (bf16[128,1536]{1,0:T(8,128)(2,1)}, bf16[128,1536]{1,0:T(8,128)(2,1)S(1)}, u32[]{:S(2)}) copy-start(bf16[128,1536]{1,0:T(8,128)(2,1)S(1)} %collective-permute-done.16.refs_21_) | copy-start | bytes 1179652
  212.3 3.0 collective-permute-start.14
  212.3 11.5 %collective-permute-start.18 = (bf16[128,1536]{1,0:T(8,128)(2,1)S(1)}, bf16[128,1536]{1,0:T(8,128)(2,1)S(1)}, u32[]{:S(2)}, u32[]{:S(2)}) collective-permute-start(bf16[128,1536]{1,0:T(8,128)(2,1)S(1)} %collective-permute-done.17.refs_22_), channel_id=1, source_target_pairs={{0,4},{1,5},{2,6},{3,7},{4,0},{5,1},{6,2},{7,3},{8,12},{9,13},{10,... | collective-permute-start | bytes 1179656 | tf_op jit(solution)/shard_map/ppermute | solution.py:226
  213.0 10.8 %collective-permute-start.21 = (bf16[128,1536]{1,0:T(8,128)(2,1)S(1)}, bf16[128,1536]{1,0:T(8,128)(2,1)S(1)}, u32[]{:S(2)}, u32[]{:S(2)}) collective-permute-start(bf16[128,1536]{1,0:T(8,128)(2,1)S(1)} %collective-permute-done.17.refs_22_), channel_id=1, source_target_pairs={{0,1},{1,0},{2,3},{3,2},{4,5},{5,4},{6,7},{7,6},{8,9},{9,8},{10,11... | collective-permute-start | bytes 1179656 | tf_op jit(solution)/shard_map/ppermute | solution.py:226
  213.7 0.8 copy-start.18
  214.5 9.9 %collective-permute-start.20 = (bf16[128,1536]{1,0:T(8,128)(2,1)S(1)}, bf16[128,1536]{1,0:T(8,128)(2,1)S(1)}, u32[]{:S(2)}, u32[]{:S(2)}) collective-permute-start(bf16[128,1536]{1,0:T(8,128)(2,1)S(1)} %collective-permute-done.16.refs_21_), channel_id=1, source_target_pairs={{0,1},{1,0},{2,3},{3,2},{4,5},{5,4},{6,7},{7,6},{8,9},{9,8},{10,11... | collective-permute-start | bytes 1179656 | tf_op jit(solution)/shard_map/ppermute | solution.py:226
  214.8 9.6 %copy-start.19 = (bf16[128,1536]{1,0:T(8,128)(2,1)}, bf16[128,1536]{1,0:T(8,128)(2,1)S(1)}, u32[]{:S(2)}) copy-start(bf16[128,1536]{1,0:T(8,128)(2,1)S(1)} %collective-permute-done.12.refs_12_) | copy-start | bytes 1179652
  214.8 14.2 %collective-permute-start.10 = (bf16[128,3072]{1,0:T(8,128)(2,1)}, bf16[128,3072]{1,0:T(8,128)(2,1)}, u32[]{:S(2)}, u32[]{:S(2)}) collective-permute-start(bf16[128,3072]{1,0:T(8,128)(2,1)} %copy-done.3), channel_id=1, source_target_pairs={{0,1},{1,0},{2,3},{3,2},{4,5},{5,4},{6,7},{7,6},{8,9},{9,8},{10,11... | collective-permute-start | bytes 2359304 | tf_op jit(solution)/shard_map/ppermute | solution.py:226
  215.2 9.3 %copy-start.20 = (bf16[128,1536]{1,0:T(8,128)(2,1)}, bf16[128,1536]{1,0:T(8,128)(2,1)S(1)}, u32[]{:S(2)}) copy-start(bf16[128,1536]{1,0:T(8,128)(2,1)S(1)} %collective-permute-done.14.refs_14_) | copy-start | bytes 1179652
  215.2 13.8 %collective-permute-start.11 = (bf16[128,3072]{1,0:T(8,128)(2,1)}, bf16[128,3072]{1,0:T(8,128)(2,1)}, u32[]{:S(2)}, u32[]{:S(2)}) collective-permute-start(bf16[128,3072]{1,0:T(8,128)(2,1)} %collective-permute-done.3.refs_3_.refs_19_), channel_id=1, source_target_pairs={{0,1},{1,0},{2,3},{3,2},{4,5},{5,4},{6,7},{7,6},{8,9},{9,8},{10,11... | collective-permute-start | bytes 2359304 | tf_op jit(solution)/shard_map/ppermute | solution.py:226
  223.8 0.8 copy-start.21
  223.8 5.2 %collective-permute-start.8 = (bf16[128,3072]{1,0:T(8,128)(2,1)}, bf16[128,3072]{1,0:T(8,128)(2,1)}, u32[]{:S(2)}, u32[]{:S(2)}) collective-permute-start(bf16[128,3072]{1,0:T(8,128)(2,1)} %copy-done.2), channel_id=1, source_target_pairs={{0,1},{1,0},{2,3},{3,2},{4,5},{5,4},{6,7},{7,6},{8,9},{9,8},{10,11... | collective-permute-start | bytes 2359304 | tf_op jit(solution)/shard_map/ppermute | solution.py:226
  223.8 0.9 copy-start.22
  223.8 5.2 %collective-permute-start.9 = (bf16[128,3072]{1,0:T(8,128)(2,1)}, bf16[128,3072]{1,0:T(8,128)(2,1)}, u32[]{:S(2)}, u32[]{:S(2)}) collective-permute-start(bf16[128,3072]{1,0:T(8,128)(2,1)} %collective-permute-done.1.refs_1_.refs_17_), channel_id=1, source_target_pairs={{0,1},{1,0},{2,3},{3,2},{4,5},{5,4},{6,7},{7,6},{8,9},{9,8},{10,11... | collective-permute-start | bytes 2359304 | tf_op jit(solution)/shard_map/ppermute | solution.py:226
  224.4 0.8 copy-start.23
  224.4 3.9 %collective-permute-start.15 = (bf16[128,1536]{1,0:T(8,128)(2,1)}, bf16[128,1536]{1,0:T(8,128)(2,1)}, u32[]{:S(2)}, u32[]{:S(2)}) collective-permute-start(bf16[128,1536]{1,0:T(8,128)(2,1)} %collective-permute-done.7.refs_7_), channel_id=1, source_target_pairs={{0,1},{1,0},{2,3},{3,2},{4,5},{5,4},{6,7},{7,6},{8,9},{9,8},{10,11... | collective-permute-start | bytes 1179656 | tf_op jit(solution)/shard_map/ppermute | solution.py:226
  228.3 2.1 collective-permute-start.22
  230.4 1.2 copy-start.1
  231.7 15.6 %copy-start.24 = (s32[4]{0:T(128)S(1)}, s32[4]{0:T(128)}, u32[]{:S(2)}) copy-start(s32[4]{0:T(128)} %constant.140.clone) | copy-start | bytes 52
  245.5 3.3 %collective-permute-start.24 = (bf16[224,1536]{1,0:T(8,128)(2,1)}, bf16[224,1536]{1,0:T(8,128)(2,1)S(1)}, u32[]{:S(2)}, u32[]{:S(2)}) collective-permute-start(bf16[224,1536]{1,0:T(8,128)(2,1)} %get-tuple-element.50.cot_ref), channel_id=1, source_target_pairs={{0,1},{1,0},{2,3},{3,2},{4,5},{5,4},{6,7},{7,6},{8,9},{9,8},{10,11... | collective-permute-start | bytes 2064392 | tf_op jit(solution)/shard_map/ppermute | solution.py:301
  246.8 2.0 collective-permute-start.23
  248.8 0.8 copy-start.6
  248.8 1.0 copy-start.4
  253.6 12.2 %collective-permute-start.25 = (bf16[4,128,384]{2,1,0:T(8,128)(2,1)}, bf16[4,128,384]{2,1,0:T(8,128)(2,1)S(1)}, u32[]{:S(2)}, u32[]{:S(2)}) collective-permute-start(bf16[4,128,384]{2,1,0:T(8,128)(2,1)} %get-tuple-element.52), channel_id=1, source_target_pairs={{0,2},{1,3},{2,0},{3,1},{4,6},{5,7},{6,4},{7,5},{8,10},{9,11},{10,... | collective-permute-start | bytes 1179656 | tf_op jit(solution)/shard_map/ppermute | solution.py:301
  255.2 18.5 %collective-permute-start.28 = (bf16[4,128,384]{2,1,0:T(8,128)(2,1)}, bf16[4,128,384]{2,1,0:T(8,128)(2,1)S(1)}, u32[]{:S(2)}, u32[]{:S(2)}) collective-permute-start(bf16[4,128,384]{2,1,0:T(8,128)(2,1)} %get-tuple-element.54), channel_id=1, source_target_pairs={{0,2},{1,3},{2,0},{3,1},{4,6},{5,7},{6,4},{7,5},{8,10},{9,11},{10,... | collective-permute-start | bytes 1179656 | tf_op jit(solution)/shard_map/ppermute | solution.py:301
  255.7 19.9 %collective-permute-start.31 = (bf16[4,128,384]{2,1,0:T(8,128)(2,1)}, bf16[4,128,384]{2,1,0:T(8,128)(2,1)S(1)}, u32[]{:S(2)}, u32[]{:S(2)}) collective-permute-start(bf16[4,128,384]{2,1,0:T(8,128)(2,1)} %get-tuple-element.56), channel_id=1, source_target_pairs={{0,4},{1,5},{2,6},{3,7},{4,0},{5,1},{6,2},{7,3},{8,12},{9,13},{10,... | collective-permute-start | bytes 1179656 | tf_op jit(solution)/shard_map/ppermute | solution.py:301
  256.3 22.2 %collective-permute-start.34 = (bf16[4,128,384]{2,1,0:T(8,128)(2,1)}, bf16[4,128,384]{2,1,0:T(8,128)(2,1)S(1)}, u32[]{:S(2)}, u32[]{:S(2)}) collective-permute-start(bf16[4,128,384]{2,1,0:T(8,128)(2,1)} %get-tuple-element.58), channel_id=1, source_target_pairs={{0,4},{1,5},{2,6},{3,7},{4,0},{5,1},{6,2},{7,3},{8,12},{9,13},{10,... | collective-permute-start | bytes 1179656 | tf_op jit(solution)/shard_map/ppermute | solution.py:301
  261.5 17.0 %copy-start.10 = (bf16[4,128,384]{2,1,0:T(8,128)(2,1)S(1)}, bf16[4,128,384]{2,1,0:T(8,128)(2,1)}, u32[]{:S(2)}) copy-start(bf16[4,128,384]{2,1,0:T(8,128)(2,1)} %get-tuple-element.57) | copy-start | bytes 1179652
  266.9 13.6 %collective-permute-start.26 = (bf16[2,128,384]{2,1,0:T(8,128)(2,1)S(1)}, bf16[2,128,384]{2,1,0:T(8,128)(2,1)S(1)}, u32[]{:S(2)}, u32[]{:S(2)}) collective-permute-start(bf16[2,128,384]{2,1,0:T(8,128)(2,1)S(1)} %get-tuple-element.64), channel_id=1, source_target_pairs={{0,4},{1,5},{2,6},{3,7},{4,0},{5,1},{6,2},{7,3},{8,12},{9,13},{10,... | collective-permute-start | bytes 589832 | tf_op jit(solution)/shard_map/ppermute | solution.py:301
  274.8 9.8 %collective-permute-start.29 = (bf16[2,128,384]{2,1,0:T(8,128)(2,1)S(1)}, bf16[2,128,384]{2,1,0:T(8,128)(2,1)S(1)}, u32[]{:S(2)}, u32[]{:S(2)}) collective-permute-start(bf16[2,128,384]{2,1,0:T(8,128)(2,1)S(1)} %get-tuple-element.66), channel_id=1, source_target_pairs={{0,4},{1,5},{2,6},{3,7},{4,0},{5,1},{6,2},{7,3},{8,12},{9,13},{10,... | collective-permute-start | bytes 589832 | tf_op jit(solution)/shard_map/ppermute | solution.py:301
  276.7 10.6 %collective-permute-start.32 = (bf16[2,128,384]{2,1,0:T(8,128)(2,1)S(1)}, bf16[2,128,384]{2,1,0:T(8,128)(2,1)S(1)}, u32[]{:S(2)}, u32[]{:S(2)}) collective-permute-start(bf16[2,128,384]{2,1,0:T(8,128)(2,1)S(1)} %get-tuple-element.68), channel_id=1, source_target_pairs={{0,2},{1,3},{2,0},{3,1},{4,6},{5,7},{6,4},{7,5},{8,10},{9,11},{10,... | collective-permute-start | bytes 589832 | tf_op jit(solution)/shard_map/ppermute | solution.py:301
  278.6 9.1 %collective-permute-start.35 = (bf16[2,128,384]{2,1,0:T(8,128)(2,1)S(1)}, bf16[2,128,384]{2,1,0:T(8,128)(2,1)S(1)}, u32[]{:S(2)}, u32[]{:S(2)}) collective-permute-start(bf16[2,128,384]{2,1,0:T(8,128)(2,1)S(1)} %get-tuple-element.70), channel_id=1, source_target_pairs={{0,2},{1,3},{2,0},{3,1},{4,6},{5,7},{6,4},{7,5},{8,10},{9,11},{10,... | collective-permute-start | bytes 589832 | tf_op jit(solution)/shard_map/ppermute | solution.py:301
  280.6 13.7 %collective-permute-start.27 = (bf16[128,384]{1,0:T(8,128)(2,1)S(1)}, bf16[128,384]{1,0:T(8,128)(2,1)S(1)}, u32[]{:S(2)}, u32[]{:S(2)}) collective-permute-start(bf16[128,384]{1,0:T(8,128)(2,1)S(1)} %fusion.13), channel_id=1, source_target_pairs={{0,8},{1,9},{2,10},{3,11},{4,12},{5,13},{6,14},{7,15},{8,0},{9,1},... | collective-permute-start | bytes 294920 | tf_op jit(solution)/shard_map/ppermute | solution.py:301
  284.7 11.7 %collective-permute-start.30 = (bf16[128,384]{1,0:T(8,128)(2,1)S(1)}, bf16[128,384]{1,0:T(8,128)(2,1)S(1)}, u32[]{:S(2)}, u32[]{:S(2)}) collective-permute-start(bf16[128,384]{1,0:T(8,128)(2,1)S(1)} %fusion.15), channel_id=1, source_target_pairs={{0,8},{1,9},{2,10},{3,11},{4,12},{5,13},{6,14},{7,15},{8,0},{9,1},... | collective-permute-start | bytes 294920 | tf_op jit(solution)/shard_map/ppermute | solution.py:301
  287.4 11.1 %collective-permute-start.33 = (bf16[128,384]{1,0:T(8,128)(2,1)S(1)}, bf16[128,384]{1,0:T(8,128)(2,1)S(1)}, u32[]{:S(2)}, u32[]{:S(2)}) collective-permute-start(bf16[128,384]{1,0:T(8,128)(2,1)S(1)} %fusion.17), channel_id=1, source_target_pairs={{0,8},{1,9},{2,10},{3,11},{4,12},{5,13},{6,14},{7,15},{8,0},{9,1},... | collective-permute-start | bytes 294920 | tf_op jit(solution)/shard_map/ppermute | solution.py:301
  287.8 12.7 %collective-permute-start.36 = (bf16[128,384]{1,0:T(8,128)(2,1)S(1)}, bf16[128,384]{1,0:T(8,128)(2,1)S(1)}, u32[]{:S(2)}, u32[]{:S(2)}) collective-permute-start(bf16[128,384]{1,0:T(8,128)(2,1)S(1)} %fusion.19), channel_id=1, source_target_pairs={{0,8},{1,9},{2,10},{3,11},{4,12},{5,13},{6,14},{7,15},{8,0},{9,1},... | collective-permute-start | bytes 294920 | tf_op jit(solution)/shard_map/ppermute | solution.py:301
  (2 other events, 1.5 us)

commit v7 on v6

--- a/solution.py
+++ b/solution.py
@@ -98,13 +98,14 @@
 
 
 def head_kernel(
-    samples, image_dev, pieces, heads, back_ref, states_ref, gate_ref, scale_ref, head_ref, *refs,
+    samples, image_dev, counts, heads, blocks, back_ref, states_ref, gate_ref, scale_ref, head_ref, *refs,
 ):
-    frozen_refs, trainee_refs = refs[:pieces], refs[pieces:2 * pieces]
-    cot_ref, att_ref, both_s, mixed_s, square_s = refs[2 * pieces:]
+    own_refs, other_refs = refs[:counts[0]], refs[counts[0]:counts[0] + counts[1]]
+    trainee_refs = refs[counts[0] + counts[1]:sum(counts)]
+    cot_ref, att_ref, both_s, mixed_s, square_s = refs[sum(counts):]
     step = pl.program_id(0)
     rows = samples * image_dev
-    width = frozen_refs[0].shape[1]
+    width = own_refs[0].shape[1]
 
     @pl.when(step == 0)
     def _():
@@ -120,20 +121,20 @@
             [jnp.broadcast_to(values[b:b + 1, :], (image_dev, values.shape[1])) for b in range(samples)], axis=0
         )
 
-    def times(count, weight_refs):
-        weights = jnp.concatenate([weight_ref[...] for weight_ref in weight_refs], axis=0)
-        return jnp.dot(both_s[:count, :], weights, preferred_element_type=jnp.float32)
+    def stacked(weight_refs):
+        return jnp.concatenate([weight_ref[...] for weight_ref in weight_refs], axis=0)
 
     share = -(-HEADS // (WIDTH // width))
     for i in range(share):
         k = jnp.minimum(step * share + i, HEADS - 1)
         piece = both_s[:rows, pl.ds(pl.multiple_of(k * HEAD_DIM, HEAD_DIM), HEAD_DIM)]
         att_ref[heads[k]] = piece.T
-    columns = pl.ds(pl.multiple_of(step * width, 128), width)
+    columns = pl.ds(pl.multiple_of(blocks[step] * width, 128), width)
     states = states_ref[:, :, columns].astype(jnp.float32).reshape(rows, width)
     gate = spread(gate_ref[:, columns])
-    frozen = times(2 * rows, frozen_refs)
-    trainee = times(rows, trainee_refs)
+    weights = jnp.where(step < pl.num_programs(0) // 2, stacked(own_refs), stacked(other_refs))
+    frozen = jnp.dot(both_s[...], weights, preferred_element_type=jnp.float32)
+    trainee = jnp.dot(both_s[:rows, :], stacked(trainee_refs), preferred_element_type=jnp.float32)
     for k, branch in enumerate((frozen[:rows], frozen[rows:], trainee)):
         mixed = states + gate * branch
         mixed_s[k, :, columns] = mixed
@@ -146,20 +147,22 @@
     @pl.when(step == pl.num_programs(0) - 1)
     def _():
         lift = 1.0 + spread(scale_ref[...])
+        contract = (((1,), (1,)), ((), ()))
         velocities = []
         for k in range(3):
             mean = jnp.sum(square_s[k], axis=1, keepdims=True) * (1.0 / WIDTH)
             root = lax.rsqrt(mean + 1e-06)
             normed = (mixed_s[k] * root * lift).astype(jnp.bfloat16)
-            velocities.append(jnp.dot(normed, head_ref[...], preferred_element_type=jnp.float32))
+            velocities.append(
+                lax.dot_general(normed, head_ref[...], contract, preferred_element_type=jnp.float32)
+            )
         velocity_c, velocity_n, velocity_s = velocities
         target = velocity_n - (velocity_c - velocity_n)
         pull = (velocity_s - target) * (2.0 / SAMPLES)
         high = pull.astype(jnp.bfloat16)
         low = (pull - high.astype(jnp.float32)).astype(jnp.bfloat16)
-        contract = (((1,), (1,)), ((), ()))
-        inner = lax.dot_general(high, head_ref[...], contract, preferred_element_type=jnp.float32)
-        inner += lax.dot_general(low, head_ref[...], contract, preferred_element_type=jnp.float32)
+        inner = jnp.dot(high, head_ref[...], preferred_element_type=jnp.float32)
+        inner += jnp.dot(low, head_ref[...], preferred_element_type=jnp.float32)
         inner = inner * lift
         mixed = mixed_s[2]
         along = jnp.sum(inner * mixed, axis=1, keepdims=True) * (1.0 / WIDTH)
@@ -167,32 +170,35 @@
         cot_ref[...] = (cot * spread(gate_ref[...])).astype(cot_ref.dtype)
 
 
-def project(back, heads, weights, states, gate, scale, final_head):
+def project(back, heads, half, weights, states, gate, scale, head_rows):
     samples, image_dev = states.shape[:2]
     rows = samples * image_dev
     inner = HEADS * HEAD_DIM
     width = 256
     steps = WIDTH // width
-    whole = lambda shape: pl.BlockSpec(shape, lambda n, heads: (0,) * len(shape))
-    pieces = len(weights)
-
-    def block_of(piece):
-        x, first = piece
-        return pl.BlockSpec((x.shape[0], width), lambda n, heads: (0, n + first // width))
+    blocks = (jnp.arange(steps, dtype=jnp.int32) + half * (steps // 2)) % steps
+    whole = lambda shape: pl.BlockSpec(shape, lambda n, heads, blocks: (0,) * len(shape))
+    places = (
+        lambda n, blocks: jnp.minimum(n, steps // 2 - 1),
+        lambda n, blocks: jnp.maximum(n - steps // 2, 0),
+        lambda n, blocks: blocks[n],
+    )
+
+    def block_of(x, first, place):
+        return pl.BlockSpec((x.shape[0], width), lambda n, heads, blocks: (0, place(n, blocks) + first // width))
 
     return pl.pallas_call(
-        functools.partial(head_kernel, samples, image_dev, pieces),
+        functools.partial(head_kernel, samples, image_dev, tuple(len(pieces) for pieces in weights)),
         grid_spec=pltpu.PrefetchScalarGridSpec(
-            num_scalar_prefetch=1,
+            num_scalar_prefetch=2,
             grid=(steps,),
             in_specs=[
                 whole(back.shape),
                 whole(states.shape),
                 whole(gate.shape),
                 whole(scale.shape),
-                whole(final_head.shape),
-                *[block_of(frozen) for frozen, _ in weights],
-                *[block_of(trainee) for _, trainee in weights],
+                whole(head_rows.shape),
+                *[block_of(x, first, place) for pieces, place in zip(weights, places) for x, first in pieces],
             ],
             out_specs=[whole((rows, WIDTH)), whole((HEADS, HEAD_DIM, rows))],
             scratch_shapes=[
@@ -212,50 +218,53 @@
             transcendentals=3 * rows,
         ),
         name="project",
-    )(heads, back, states, gate, scale, final_head, *[x for (x, _), _ in weights],
-      *[x for _, (x, _) in weights])
+    )(heads, blocks, back, states, gate, scale, head_rows, *[x for pieces in weights for x, _ in pieces])
 
 
 class RowGather:
-    def __init__(self, frozen, trainee, group_size):
-        self.group_size = group_size
-        self.parts = (frozen, trainee)
-        self.own = jnp.concatenate([frozen, trainee], axis=1)
+    def __init__(self, frozen, trainee, half, group_size, groups):
+        self.group_size, self.groups = group_size, groups
+        self.cut = WIDTH // 2
+        self.own = jnp.concatenate(
+            [lax.dynamic_slice_in_dim(frozen, half * self.cut, self.cut, axis=1), trainee], axis=1
+        )
 
     def swap(self, x, k):
         return lax.ppermute(x, "seq", [(s, s ^ (1 << k)) for s in range(self.group_size)])
 
+    def across(self, *blocks):
+        halves = jnp.concatenate([x[:, :self.cut] for x in blocks])
+        return lax.ppermute(halves, "grp", [(g, g ^ 1) for g in range(self.groups)])
+
     def near(self, value):
         line, pair = self.swap(self.own, 2), self.swap(self.own, 1)
-        value, self.own, self.parts, line, pair = lax.optimization_barrier(
-            (value, self.own, self.parts, line, pair)
-        )
-        self.blocks = {0: self.own, 4: line, 2: pair, 6: self.swap(line, 1)}
-        self.across = [self.swap(x, 3) for x in self.parts]
+        value, self.own, line, pair = lax.optimization_barrier((value, self.own, line, pair))
+        self.blocks = [self.own, line, pair, self.swap(line, 1), self.swap(self.own, 3)]
         return value
 
     def far(self, value):
-        value, self.across[0] = lax.optimization_barrier((value, self.across[0]))
-        line, pair = [self.swap(self.across[0], k) for k in (2, 1)]
-        value, self.blocks, self.across, line, pair = lax.optimization_barrier(
-            (value, self.blocks, self.across, line, pair)
-        )
-        corner = self.swap(line, 1)
-        line_t, pair_t = [self.swap(self.across[1], k) for k in (2, 1)]
-        self.split = {8: tuple(self.across), 12: (line, line_t), 10: (pair, pair_t),
-                      14: (corner, self.swap(pair_t, 2))}
+        value, self.blocks = lax.optimization_barrier((value, self.blocks))
+        line, pair = self.swap(self.blocks[4], 2), self.swap(self.blocks[4], 1)
+        value, line, pair = lax.optimization_barrier((value, line, pair))
+        self.corner = (self.swap(line[:, :self.cut], 1), self.swap(pair[:, self.cut:], 2))
+        self.others = [self.across(*self.blocks[:4])]
+        self.blocks += [line, pair]
+        self.others += [self.across(*self.blocks[4:]), self.across(self.corner[0])]
         return value
 
     def rows(self, position):
-        pieces = {n: ((x, 0), (x, WIDTH)) for n, x in self.blocks.items()}
-        pieces |= {n: tuple((x, 0) for x in pair) for n, pair in self.split.items()}
-        for offset, x in self.blocks.items():
-            other = self.swap(x, 0)
-            pieces[offset + 1] = ((other, 0), (other, WIDTH))
-        for offset, pair in self.split.items():
-            pieces[offset + 1] = tuple((self.swap(x, 0), 0) for x in pair)
-        offsets = jnp.array(list(pieces), jnp.int32)
-        return list(pieces.values()), (position ^ offsets).astype(jnp.int32)
+        def pieces(blocks, corner, others):
+            return (
+                [(x, 0) for x in blocks] + [(corner[0], 0)],
+                [(x, 0) for x in others],
+                [(x, self.cut) for x in blocks] + [(corner[1], 0)],
+            )
+
+        mine = pieces(self.blocks, self.corner, self.others)
+        core = pieces(*[[self.swap(x, 0) for x in group] for group in (self.blocks, self.corner, self.others)])
+        offsets = jnp.array([0, 4, 2, 6, 8, 12, 10, 14], jnp.int32)
+        heads = position ^ jnp.concatenate([offsets, offsets + 1])
+        return [a + b for a, b in zip(mine, core)], heads.astype(jnp.int32)
 
 
 def product_kernel(starts, mine, peer, att_ref, att_peer_ref, cot_ref, cot_peer_ref, *out_refs):
@@ -383,20 +392,24 @@
     scale = modulation[:, WIDTH:]
     exchange = functools.partial(lax.all_to_all, axis_name="seq", split_axis=0, concat_axis=0, tiled=True)
     gathered = exchange(jnp.concatenate([text_items, image_items], axis=2))
-    if group_size == HEADS:
-        rows = RowGather(frozen_out, trainee_out, group_size)
+    groups = lax.axis_size("grp")
+    staged = group_size == HEADS and groups % 2 == 0
+    gathered, gate, scale = lax.optimization_barrier((gathered, gate, scale))
+    if staged:
+        half = lax.axis_index("grp") % 2
+        rows = RowGather(frozen_out, trainee_out, half, group_size, groups)
         gathered = rows.near(gathered)
     both = attend(gathered, live, image_dev, text_dev)
-    if group_size == HEADS:
+    if staged:
         both = rows.far(both)
         weights, heads = rows.rows(position)
     else:
+        half, heads = jnp.int32(0), jnp.arange(HEADS, dtype=jnp.int32)
         block = jnp.concatenate([frozen_out, trainee_out], axis=1)
         everything = lax.all_gather(block, "seq", axis=0, tiled=True)
-        all_rows = [((everything, 0), (everything, WIDTH))]
-        weights, heads = all_rows, jnp.arange(HEADS, dtype=jnp.int32)
+        weights = [[(everything, first)] for first in (0, WIDTH // 2, WIDTH)]
     back = exchange(both).reshape(HEADS, SAMPLES, 2, image_dev, HEAD_DIM)
-    cot, att = project(back, heads, weights, image_states, gate, scale, final_head)
+    cot, att = project(back, heads, half, weights, image_states, gate, scale, final_head.T)
     if group_size == HEADS:
         return reduce_by_halving(att, cot, position, group_size)
     partial = jnp.einsum("hdr,rc->hdc", att, cot, preferred_element_type=jnp.float32)

time: 302 us -> 290 us (0.960)
  waiting for transfers between devices: 181 us -> 158 us
  starting transfers between devices: 52.2 us -> 62.1 us
    ppermute x23 -> x20, waiting for transfers between devices: 157 us -> 48.3 us  [swap(): lax.ppermute(x, 'seq', [(s, s ^ 1 << k) for s in range(self.group_size)])]
    all_to_all x1, waiting for transfers between devices: 0.01 us -> 84.1 us  [shards(): gathered = exchange(jnp.concatenate([text_items, image_items], axis=2))]
    slice x0 -> x9, local copies, waits for them, and re-layouts: none -> 6.67 us  [the longest x7 4.71 us: across(): halves = jnp.concatenate([x[:, :self.cut] for x in blocks])]
    ppermute x23 -> x20, starting transfers between devices: 23.3 us -> 29.3 us  [swap(): lax.ppermute(x, 'seq', [(s, s ^ 1 << k) for s in range(self.group_size)])]
    unnamed x56 -> x52, local copies, waits for them, and re-layouts: 8.61 us -> 3.33 us
    ppermute x0 -> x3, starting transfers between devices: none -> 3.65 us  [across(): return lax.ppermute(halves, 'grp', [(g, g ^ 1) for g in range(self.groups)])]
  transfers between devices with their start and end apart: 39 -> 39, of which waited for: 17 -> 18; matrix products, arithmetic and copies ran while one was open for 4% -> 5% of each run, Pallas kernels for 8% -> 9%
where the time goes in v7:
time: 290 us; the launch traced here: 289 us
  waiting for transfers between devices  158 us (54%)
  starting transfers between devices  62.1 us (21%)
  Pallas kernels  43.9 us (15%)
  local copies, waits for them, and re-layouts  15.3 us (5%)
  other arithmetic  8.58 us (3%)
    all_to_all x1, waiting for transfers between devices, shards(): gathered = exchange(jnp.concatenate([text_items, image_items], axis=2))  84.1 us
    ppermute x20, waiting for transfers between devices, swap(): lax.ppermute(x, 'seq', [(s, s ^ 1 << k) for s in range(self.group_size)])  48.3 us
    ppermute x20, starting transfers between devices, swap(): lax.ppermute(x, 'seq', [(s, s ^ 1 << k) for s in range(self.group_size)])  29.3 us
    ppermute x14, waiting for transfers between devices, swap(): return lax.ppermute(x, 'seq', [(s, s ^ 1 << k) for s in range(group_size)])  25 us
    pallas_call x1, Pallas kernels, attend(): pl.pallas_call(functools.partial(attention_kernel, image_dev, text_dev, b...  20.9 us
    ppermute x14, starting transfers between devices, swap(): return lax.ppermute(x, 'seq', [(s, s ^ 1 << k) for s in range(group_size)])  16.8 us
    pallas_call x1, Pallas kernels, project(): pl.pallas_call(functools.partial(head_kernel, samples, image_dev, tuple((...  15.4 us
    pallas_call x2, Pallas kernels, product(): pl.pallas_call(functools.partial(product_kernel, starts), in_specs=[pl.Bl...  7.65 us
  transfers between devices with their start and end apart: 39, of which 18 were waited for; matrix products, arithmetic and copies ran while one was open for 5% of the time, Pallas kernels for 9%

profile of v7, /device:TPU:0, one launch (start us, length us, event | category | flops | bytes accessed | tf_op | source)
XLA Modules:
  0.0 288.8 jit_solution(9564826145650759370)
XLA Ops:
  0.0 2.4 copy.19
  3.1 2.6 pad_maximum_fusion
  5.8 7.6 %all-to-all-start = ((bf16[16,4,296,128]{3,2,1,0:T(8,128)(2,1)}), bf16[16,4,296,128]{3,2,1,0:T(8,128)(2,1)}, u32[]{:S(2)}, u32[]{:S(2)}) async-start(bf16[16,4,296,128]{3,2,1,0:T(8,128)(2,1)} %pad_maximum_fusion), calls=%async_computation | async-start | bytes 9699328 | tf_op jit(solution)/shard_map/all_to_all | solution.py:394
  13.5 1.9 collective-permute-start
  15.4 1.5 collective-permute-start.1
  17.0 0.7 fusion.20
  17.8 0.6 fusion.30
  18.4 84.1 %all-to-all-done.x_ref = bf16[16,4,296,128]{3,2,1,0:T(8,128)(2,1)} async-done(((bf16[16,4,296,128]{3,2,1,0:T(8,128)(2,1)}), bf16[16,4,296,128]{3,2,1,0:T(8,128)(2,1)}, u32[]{:S(2)}, u32[]{:S(2)}) %all-to-all-start) | async-done | bytes 4849696 | tf_op jit(solution)/shard_map/all_to_all | solution.py:394
  102.5 2.7 collective-permute-done.refs_1_.refs_23_
  105.2 4.5 %collective-permute-start.2 = (bf16[128,2304]{1,0:T(8,128)(2,1)S(1)}, bf16[128,2304]{1,0:T(8,128)(2,1)}, u32[]{:S(2)}, u32[]{:S(2)}) collective-permute-start(bf16[128,2304]{1,0:T(8,128)(2,1)S(1)} %collective-permute-done.refs_1_.refs_23_), channel_id=1, source_target_pairs={{0,2},{1,3},{2,0},{3,1},{4,6},{5,7},{6,4},{7,5},{8,10},{9,11},{10,... | collective-permute-start | bytes 1769480 | tf_op jit(solution)/shard_map/ppermute | solution.py:233
  109.6 13.4 %collective-permute-start.3 = (bf16[128,2304]{1,0:T(8,128)(2,1)S(1)}, bf16[128,2304]{1,0:T(8,128)(2,1)}, u32[]{:S(2)}, u32[]{:S(2)}) collective-permute-start(bf16[128,2304]{1,0:T(8,128)(2,1)S(1)} %pad_maximum_fusion.3.refs_0_.refs_22_), channel_id=1, source_target_pairs={{0,8},{1,9},{2,10},{3,11},{4,12},{5,13},{6,14},{7,15},{8,0},{9,1},... | collective-permute-start | bytes 1769480 | tf_op jit(solution)/shard_map/ppermute | solution.py:233
  123.1 0.6 gather_fusion
  123.7 20.9 %attention.1 = bf16[16,4,2,56,128]{4,3,2,1,0:T(8,128)(2,1)} custom-call(bf16[16,4,296,128]{3,2,1,0:T(8,128)(2,1)} %all-to-all-done.x_ref, s32[4,2,512]{2,1,0:T(2,128)S(1)} %compare_convert_fusion.live_ref), custom_call_target="tpu_custom_call" | custom-call | flops 3523215360 | bytes 6684672 | tf_op jit(solution)/shard_map/attention/pallas_call | solution.py:72
  144.6 4.3 %collective-permute-done.3.refs_4_.refs_26_ = bf16[128,2304]{1,0:T(8,128)(2,1)} collective-permute-done((bf16[128,2304]{1,0:T(8,128)(2,1)S(1)}, bf16[128,2304]{1,0:T(8,128)(2,1)}, u32[]{:S(2)}, u32[]{:S(2)}) %collective-permute-start.3) | collective-permute-done | bytes 589856 | tf_op jit(solution)/shard_map/ppermute | solution.py:233
  148.9 0.6 collective-permute-start.4
  149.5 1.1 collective-permute-start.5
  150.6 12.9 %collective-permute-done.4.refs_5_.refs_27_ = bf16[128,2304]{1,0:T(8,128)(2,1)} collective-permute-done((bf16[128,2304]{1,0:T(8,128)(2,1)}, bf16[128,2304]{1,0:T(8,128)(2,1)}, u32[]{:S(2)}, u32[]{:S(2)}) %collective-permute-start.4) | collective-permute-done | bytes 589856 | tf_op jit(solution)/shard_map/ppermute | solution.py:233
  163.5 1.3 collective-permute-done.5.refs_6_.refs_28_
  164.8 4.9 %all-to-all-start.1 = ((bf16[16,4,2,56,128]{4,3,2,1,0:T(8,128)(2,1)}), bf16[16,4,2,56,128]{4,3,2,1,0:T(8,128)(2,1)S(1)}, u32[]{:S(2)}, u32[]{:S(2)}) async-start(bf16[16,4,2,56,128]{4,3,2,1,0:T(8,128)(2,1)} %attention.1), calls=%async_computation.1 | async-start | bytes 3670016 | tf_op jit(solution)/shard_map/all_to_all | solution.py:411
  170.3 0.9 slice.37
  171.2 0.9 slice.34
  172.7 0.9 slice.35
  173.8 1.6 collective-permute-start.15
  175.6 0.9 slice.38
  176.6 0.9 slice.33
  177.5 0.9 slice.39
  178.5 0.6 collective-permute-start.16
  179.1 1.0 slice.40
  180.2 2.0 collective-permute-start.21
  182.2 1.5 collective-permute-start.6
  183.6 8.8 %collective-permute-done.6.refs_7_ = bf16[128,768]{1,0:T(8,128)(2,1)S(1)} collective-permute-done((bf16[128,768]{1,0:T(8,128)(2,1)S(1)}, bf16[128,768]{1,0:T(8,128)(2,1)S(1)}, u32[]{:S(2)}, u32[]{:S(2)}) %collective-permute-start.6) | collective-permute-done | bytes 196640 | tf_op jit(solution)/shard_map/ppermute | solution.py:233
  192.5 1.5 collective-permute-start.17
  194.8 16.1 %collective-permute-done.21.refs_29_ = bf16[128,1536]{1,0:T(8,128)(2,1)} collective-permute-done((bf16[128,1536]{1,0:T(8,128)(2,1)S(1)}, bf16[128,1536]{1,0:T(8,128)(2,1)}, u32[]{:S(2)}, u32[]{:S(2)}) %collective-permute-start.21) | collective-permute-done | bytes 393248 | tf_op jit(solution)/shard_map/ppermute | solution.py:233
  211.9 1.4 collective-permute-done.20.refs_21_
  213.3 0.7 copy-done.21
  214.2 0.6 and_select_fusion.2.blocks
  215.3 0.7 collective-permute-done.22.refs_37_
  216.1 1.2 copy-done.1
  217.3 15.4 %project.1 = (bf16[224,1536]{1,0:T(8,128)(2,1)}, bf16[16,128,224]{2,1,0:T(8,128)(2,1)}) custom-call(s32[16]{0:T(128)} %broadcast_xor_fusion.heads, s32[6]{0:T(128)} %and_select_fusion.2.blocks, bf16[16,4,2,56,128]{4,3,2,1,0:T(8,128)(2,1)} %copy-done.1, bf16[4,56,1536]{2,1,0:T(8,128)(2,1)} %states_ref.1, f32[4,1536]{1,0:T(4,128)} %get-tuple-element.39.gate_ref, ...), custom_call_target="tpu_custom_call" | custom-call | flops 4227858432 | bytes 14417920 | tf_op jit(solution)/shard_map/project/pallas_call | solution.py:190
  233.0 1.1 dynamic-slice_bitcast_fusion
  234.5 0.7 multiply_add_fusion
  235.2 0.9 collective-permute-done.23.att_peer_ref
  236.1 0.8 copy-done.13
  237.1 3.8 %product.3 = (bf16[4,128,384]{2,1,0:T(8,128)(2,1)}, bf16[4,128,384]{2,1,0:T(8,128)(2,1)}, bf16[4,128,384]{2,1,0:T(8,128)(2,1)}, bf16[4,128,384]{2,1,0:T(8,128)(2,1)}) custom-call(s32[8]{0:T(128)} %get-tuple-element.59.mine, s32[8]{0:T(128)} %get-tuple-element.60.peer, bf16[16,128,224]{2,1,0:T(8,128)(2,1)} %get-tuple-element.47.att_ref, ...), custom_call_target="tpu_custom_call" | custom-call | flops 704643072 | bytes 3866624 | tf_op jit(solution)/shard_map/product/pallas_call | solution.py:288
  240.9 1.6 collective-permute-start.25
  242.9 0.6 collective-permute-start.31
  243.5 1.4 collective-permute-start.34
  245.0 3.8 %product.2 = (bf16[4,128,384]{2,1,0:T(8,128)(2,1)}, bf16[4,128,384]{2,1,0:T(8,128)(2,1)}, bf16[4,128,384]{2,1,0:T(8,128)(2,1)}, bf16[4,128,384]{2,1,0:T(8,128)(2,1)}) custom-call(s32[8]{0:T(128)} %get-tuple-element.75.mine, s32[8]{0:T(128)} %get-tuple-element.76.peer, bf16[16,128,224]{2,1,0:T(8,128)(2,1)} %get-tuple-element.47.att_ref, ...), custom_call_target="tpu_custom_call" | custom-call | flops 704643072 | bytes 3866624 | tf_op jit(solution)/shard_map/product/pallas_call | solution.py:288
  248.8 4.3 %collective-permute-done.25 = bf16[4,128,384]{2,1,0:T(8,128)(2,1)S(1)} collective-permute-done((bf16[4,128,384]{2,1,0:T(8,128)(2,1)}, bf16[4,128,384]{2,1,0:T(8,128)(2,1)S(1)}, u32[]{:S(2)}, u32[]{:S(2)}) %collective-permute-start.25) | collective-permute-done | bytes 393248 | tf_op jit(solution)/shard_map/ppermute | solution.py:310
  253.1 1.2 add_convert_fusion.7
  254.2 0.7 collective-permute-start.26
  254.9 6.0 %collective-permute-done.28 = bf16[4,128,384]{2,1,0:T(8,128)(2,1)S(1)} collective-permute-done((bf16[4,128,384]{2,1,0:T(8,128)(2,1)}, bf16[4,128,384]{2,1,0:T(8,128)(2,1)S(1)}, u32[]{:S(2)}, u32[]{:S(2)}) %collective-permute-start.28) | collective-permute-done | bytes 393248 | tf_op jit(solution)/shard_map/ppermute | solution.py:310
  260.9 1.1 add_convert_fusion.5
  262.0 0.9 collective-permute-start.29
  263.1 1.8 collective-permute-start.32
  265.4 2.4 collective-permute-done.26
  267.8 2.6 collective-permute-start.27
  270.5 1.4 collective-permute-done.29
  271.9 2.6 collective-permute-start.30
  275.0 2.6 collective-permute-start.36
  277.7 6.1 %collective-permute-done.30 = bf16[128,384]{1,0:T(8,128)(2,1)S(1)} collective-permute-done((bf16[128,384]{1,0:T(8,128)(2,1)S(1)}, bf16[128,384]{1,0:T(8,128)(2,1)S(1)}, u32[]{:S(2)}, u32[]{:S(2)}) %collective-permute-start.30) | collective-permute-done | bytes 98336 | tf_op jit(solution)/shard_map/ppermute | solution.py:310
  283.8 2.1 collective-permute-done.33
  285.9 1.8 collective-permute-done.36
  287.8 1.0 pad_maximum_fusion.2
  (116 shorter events, 7.8 us)
Async XLA Ops:
  0.0 17.0 %copy-start = (bf16[256,3072]{1,0:T(8,128)(2,1)S(1)}, bf16[256,3072]{1,0:T(8,128)(2,1)}, u32[]{:S(2)}) copy-start(bf16[256,3072]{1,0:T(8,128)(2,1)} %param.21) | copy-start | bytes 4718596
  0.0 2.5 copy-start.12
  5.8 7.6 %copy-start.22 = (bf16[128,1536]{1,0:T(8,128)(2,1)S(1)}, bf16[128,1536]{1,0:T(8,128)(2,1)}, u32[]{:S(2)}) copy-start(bf16[128,1536]{1,0:T(8,128)(2,1)} %param.19) | copy-start | bytes 1179652
  5.8 7.7 %copy-start.15 = (bf16[128,1536]{1,0:T(8,128)(2,1)S(1)}, bf16[128,1536]{1,0:T(8,128)(2,1)}, u32[]{:S(2)}) copy-start(bf16[128,1536]{1,0:T(8,128)(2,1)} %param.20) | copy-start | bytes 1179652
  5.8 96.7 %all-to-all-start = ((bf16[16,4,296,128]{3,2,1,0:T(8,128)(2,1)}), bf16[16,4,296,128]{3,2,1,0:T(8,128)(2,1)}, u32[]{:S(2)}, u32[]{:S(2)}) async-start(bf16[16,4,296,128]{3,2,1,0:T(8,128)(2,1)} %pad_maximum_fusion), calls=%async_computation | async-start | bytes 9699328 | tf_op jit(solution)/shard_map/all_to_all | solution.py:394
  13.3 3.6 %copy-start.24 = (s32[4]{0:T(128)S(1)}, s32[4]{0:T(128)}, u32[]{:S(2)}) copy-start(s32[4]{0:T(128)} %param.17) | copy-start | bytes 52
  13.4 109.7 %copy-start.14 = (s32[2,4,512]{2,1,0:T(4,128)S(1)}, s32[2,4,512]{2,1,0:T(4,128)}, u32[]{:S(2)}) copy-start(s32[2,4,512]{2,1,0:T(4,128)} %param.16) | copy-start | bytes 49156
  13.5 131.1 %copy-start.2 = (bf16[128,2304]{1,0:T(8,128)(2,1)}, bf16[128,2304]{1,0:T(8,128)(2,1)S(1)}, u32[]{:S(2)}) copy-start(bf16[128,2304]{1,0:T(8,128)(2,1)S(1)} %pad_maximum_fusion.3.refs_0_.refs_22_) | copy-start | bytes 1769476
  13.5 91.7 %collective-permute-start = (bf16[128,2304]{1,0:T(8,128)(2,1)S(1)}, bf16[128,2304]{1,0:T(8,128)(2,1)S(1)}, u32[]{:S(2)}, u32[]{:S(2)}) collective-permute-start(bf16[128,2304]{1,0:T(8,128)(2,1)S(1)} %pad_maximum_fusion.3.refs_0_.refs_22_), channel_id=1, source_target_pairs={{0,4},{1,5},{2,6},{3,7},{4,0},{5,1},{6,2},{7,3},{8,12},{9,13},{10,... | collective-permute-start | bytes 1769480 | tf_op jit(solution)/shard_map/ppermute | solution.py:233
  15.4 89.7 %collective-permute-start.1 = (bf16[128,2304]{1,0:T(8,128)(2,1)S(1)}, bf16[128,2304]{1,0:T(8,128)(2,1)S(1)}, u32[]{:S(2)}, u32[]{:S(2)}) collective-permute-start(bf16[128,2304]{1,0:T(8,128)(2,1)S(1)} %pad_maximum_fusion.3.refs_0_.refs_22_), channel_id=1, source_target_pairs={{0,2},{1,3},{2,0},{3,1},{4,6},{5,7},{6,4},{7,5},{8,10},{9,11},{10,... | collective-permute-start | bytes 1769480 | tf_op jit(solution)/shard_map/ppermute | solution.py:233
  105.2 39.4 %copy-start.3 = (bf16[128,2304]{1,0:T(8,128)(2,1)}, bf16[128,2304]{1,0:T(8,128)(2,1)S(1)}, u32[]{:S(2)}) copy-start(bf16[128,2304]{1,0:T(8,128)(2,1)S(1)} %collective-permute-done.refs_1_.refs_23_) | copy-start | bytes 1769476
  105.2 39.4 %copy-start.4 = (bf16[128,2304]{1,0:T(8,128)(2,1)}, bf16[128,2304]{1,0:T(8,128)(2,1)S(1)}, u32[]{:S(2)}) copy-start(bf16[128,2304]{1,0:T(8,128)(2,1)S(1)} %collective-permute-done.1.refs_2_.refs_24_) | copy-start | bytes 1769476
  105.2 39.4 %collective-permute-start.2 = (bf16[128,2304]{1,0:T(8,128)(2,1)S(1)}, bf16[128,2304]{1,0:T(8,128)(2,1)}, u32[]{:S(2)}, u32[]{:S(2)}) collective-permute-start(bf16[128,2304]{1,0:T(8,128)(2,1)S(1)} %collective-permute-done.refs_1_.refs_23_), channel_id=1, source_target_pairs={{0,2},{1,3},{2,0},{3,1},{4,6},{5,7},{6,4},{7,5},{8,10},{9,11},{10,... | collective-permute-start | bytes 1769480 | tf_op jit(solution)/shard_map/ppermute | solution.py:233
  109.6 39.3 %collective-permute-start.3 = (bf16[128,2304]{1,0:T(8,128)(2,1)S(1)}, bf16[128,2304]{1,0:T(8,128)(2,1)}, u32[]{:S(2)}, u32[]{:S(2)}) collective-permute-start(bf16[128,2304]{1,0:T(8,128)(2,1)S(1)} %pad_maximum_fusion.3.refs_0_.refs_22_), channel_id=1, source_target_pairs={{0,8},{1,9},{2,10},{3,11},{4,12},{5,13},{6,14},{7,15},{8,0},{9,1},... | collective-permute-start | bytes 1769480 | tf_op jit(solution)/shard_map/ppermute | solution.py:233
  148.9 14.6 %collective-permute-start.4 = (bf16[128,2304]{1,0:T(8,128)(2,1)}, bf16[128,2304]{1,0:T(8,128)(2,1)}, u32[]{:S(2)}, u32[]{:S(2)}) collective-permute-start(bf16[128,2304]{1,0:T(8,128)(2,1)} %collective-permute-done.3.refs_4_.refs_26_), channel_id=1, source_target_pairs={{0,4},{1,5},{2,6},{3,7},{4,0},{5,1},{6,2},{7,3},{8,12},{9,13},{10,... | collective-permute-start | bytes 1769480 | tf_op jit(solution)/shard_map/ppermute | solution.py:233
  149.5 15.3 %collective-permute-start.5 = (bf16[128,2304]{1,0:T(8,128)(2,1)}, bf16[128,2304]{1,0:T(8,128)(2,1)}, u32[]{:S(2)}, u32[]{:S(2)}) collective-permute-start(bf16[128,2304]{1,0:T(8,128)(2,1)} %collective-permute-done.3.refs_4_.refs_26_), channel_id=1, source_target_pairs={{0,2},{1,3},{2,0},{3,1},{4,6},{5,7},{6,4},{7,5},{8,10},{9,11},{10,... | collective-permute-start | bytes 1769480 | tf_op jit(solution)/shard_map/ppermute | solution.py:233
  164.8 51.3 %all-to-all-start.1 = ((bf16[16,4,2,56,128]{4,3,2,1,0:T(8,128)(2,1)}), bf16[16,4,2,56,128]{4,3,2,1,0:T(8,128)(2,1)S(1)}, u32[]{:S(2)}, u32[]{:S(2)}) async-start(bf16[16,4,2,56,128]{4,3,2,1,0:T(8,128)(2,1)} %attention.1), calls=%async_computation.1 | async-start | bytes 3670016 | tf_op jit(solution)/shard_map/all_to_all | solution.py:411
  169.7 4.1 %slice-start = ((bf16[128,2304]{1,0:T(8,128)(2,1)}), bf16[128,768]{1,0:T(8,128)(2,1)S(1)}, s32[]{:S(2)}) async-start(bf16[128,2304]{1,0:T(8,128)(2,1)} %copy-done.4), calls=%async_computation.2 | async-start | bytes 393216 | tf_op jit(solution)/shard_map/slice | solution.py:236
  169.7 5.7 %copy-start.5 = (bf16[128,2304]{1,0:T(8,128)(2,1)S(1)}, bf16[128,2304]{1,0:T(8,128)(2,1)}, u32[]{:S(2)}) copy-start(bf16[128,2304]{1,0:T(8,128)(2,1)} %copy-done.4) | copy-start | bytes 1769476
  169.7 5.7 %collective-permute-start.10 = (bf16[128,2304]{1,0:T(8,128)(2,1)}, bf16[128,2304]{1,0:T(8,128)(2,1)S(1)}, u32[]{:S(2)}, u32[]{:S(2)}) collective-permute-start(bf16[128,2304]{1,0:T(8,128)(2,1)} %collective-permute-done.2.refs_3_.refs_25_), channel_id=1, source_target_pairs={{0,1},{1,0},{2,3},{3,2},{4,5},{5,4},{6,7},{7,6},{8,9},{9,8},{10,11... | collective-permute-start | bytes 1769480 | tf_op jit(solution)/shard_map/ppermute | solution.py:233
  170.2 8.3 %collective-permute-start.11 = (bf16[128,2304]{1,0:T(8,128)(2,1)}, bf16[128,2304]{1,0:T(8,128)(2,1)S(1)}, u32[]{:S(2)}, u32[]{:S(2)}) collective-permute-start(bf16[128,2304]{1,0:T(8,128)(2,1)} %collective-permute-done.3.refs_4_.refs_26_), channel_id=1, source_target_pairs={{0,1},{1,0},{2,3},{3,2},{4,5},{5,4},{6,7},{7,6},{8,9},{9,8},{10,11... | collective-permute-start | bytes 1769480 | tf_op jit(solution)/shard_map/ppermute | solution.py:233
  172.2 8.0 %collective-permute-start.7 = (bf16[128,2304]{1,0:T(8,128)(2,1)}, bf16[128,2304]{1,0:T(8,128)(2,1)S(1)}, u32[]{:S(2)}, u32[]{:S(2)}) collective-permute-start(bf16[128,2304]{1,0:T(8,128)(2,1)} %copy-done.2), channel_id=1, source_target_pairs={{0,1},{1,0},{2,3},{3,2},{4,5},{5,4},{6,7},{7,6},{8,9},{9,8},{10,11... | collective-permute-start | bytes 1769480 | tf_op jit(solution)/shard_map/ppermute | solution.py:233
  173.6 8.6 %collective-permute-start.8 = (bf16[128,2304]{1,0:T(8,128)(2,1)}, bf16[128,2304]{1,0:T(8,128)(2,1)S(1)}, u32[]{:S(2)}, u32[]{:S(2)}) collective-permute-start(bf16[128,2304]{1,0:T(8,128)(2,1)} %copy-done.3), channel_id=1, source_target_pairs={{0,1},{1,0},{2,3},{3,2},{4,5},{5,4},{6,7},{7,6},{8,9},{9,8},{10,11... | collective-permute-start | bytes 1769480 | tf_op jit(solution)/shard_map/ppermute | solution.py:233
  173.8 40.9 %copy-start.25 = (s32[16]{0:T(128)S(1)}, s32[16]{0:T(128)}, u32[]{:S(2)}) copy-start(s32[16]{0:T(128)} %constant.174) | copy-start | bytes 196
  173.8 20.5 %collective-permute-start.15 = (bf16[512,768]{1,0:T(8,128)(2,1)S(1)}, bf16[512,768]{1,0:T(8,128)(2,1)}, u32[]{:S(2)}, u32[]{:S(2)}) collective-permute-start(bf16[512,768]{1,0:T(8,128)(2,1)S(1)} %pad_maximum_fusion.1), channel_id=1, source_target_pairs={{0,16},{16,0},{1,17},{17,1},{2,18},{18,2},{3,19},{19,3},{4,20},{20... | collective-permute-start | bytes 2359304 | tf_op jit(solution)/shard_map/ppermute | solution.py:237
  175.4 4.7 %copy-start.7 = (bf16[128,2304]{1,0:T(8,128)(2,1)}, bf16[128,2304]{1,0:T(8,128)(2,1)S(1)}, u32[]{:S(2)}) copy-start(bf16[128,2304]{1,0:T(8,128)(2,1)S(1)} %collective-permute-done.10.refs_11_.refs_33_) | copy-start | bytes 1769476
  175.4 18.5 %collective-permute-start.9 = (bf16[128,2304]{1,0:T(8,128)(2,1)S(1)}, bf16[128,2304]{1,0:T(8,128)(2,1)S(1)}, u32[]{:S(2)}, u32[]{:S(2)}) collective-permute-start(bf16[128,2304]{1,0:T(8,128)(2,1)S(1)} %copy-done.5), channel_id=1, source_target_pairs={{0,1},{1,0},{2,3},{3,2},{4,5},{5,4},{6,7},{7,6},{8,9},{9,8},{10,11... | collective-permute-start | bytes 1769480 | tf_op jit(solution)/shard_map/ppermute | solution.py:233
  178.5 15.4 %copy-start.8 = (bf16[128,2304]{1,0:T(8,128)(2,1)}, bf16[128,2304]{1,0:T(8,128)(2,1)S(1)}, u32[]{:S(2)}) copy-start(bf16[128,2304]{1,0:T(8,128)(2,1)S(1)} %collective-permute-done.11.refs_12_.refs_34_) | copy-start | bytes 1769476
  178.5 32.9 %collective-permute-start.16 = (bf16[384,768]{1,0:T(8,128)(2,1)S(1)}, bf16[384,768]{1,0:T(8,128)(2,1)}, u32[]{:S(2)}, u32[]{:S(2)}) collective-permute-start(bf16[384,768]{1,0:T(8,128)(2,1)S(1)} %pad_maximum_fusion.4), channel_id=1, source_target_pairs={{0,16},{16,0},{1,17},{17,1},{2,18},{18,2},{3,19},{19,3},{4,20},{20... | collective-permute-start | bytes 1769480 | tf_op jit(solution)/shard_map/ppermute | solution.py:237
  180.2 13.9 %copy-start.9 = (bf16[128,2304]{1,0:T(8,128)(2,1)}, bf16[128,2304]{1,0:T(8,128)(2,1)S(1)}, u32[]{:S(2)}) copy-start(bf16[128,2304]{1,0:T(8,128)(2,1)S(1)} %collective-permute-done.7.refs_8_.refs_30_) | copy-start | bytes 1769476
  180.2 30.7 %collective-permute-start.21 = (bf16[128,1536]{1,0:T(8,128)(2,1)S(1)}, bf16[128,1536]{1,0:T(8,128)(2,1)}, u32[]{:S(2)}, u32[]{:S(2)}) collective-permute-start(bf16[128,1536]{1,0:T(8,128)(2,1)S(1)} %slice.40), channel_id=1, source_target_pairs={{0,4},{1,5},{2,6},{3,7},{4,0},{5,1},{6,2},{7,3},{8,12},{9,13},{10,... | collective-permute-start | bytes 1179656 | tf_op jit(solution)/shard_map/ppermute | solution.py:233
  182.2 12.2 %copy-start.10 = (bf16[128,2304]{1,0:T(8,128)(2,1)}, bf16[128,2304]{1,0:T(8,128)(2,1)S(1)}, u32[]{:S(2)}) copy-start(bf16[128,2304]{1,0:T(8,128)(2,1)S(1)} %collective-permute-done.8.refs_9_.refs_31_) | copy-start | bytes 1769476
  182.2 10.3 %collective-permute-start.6 = (bf16[128,768]{1,0:T(8,128)(2,1)S(1)}, bf16[128,768]{1,0:T(8,128)(2,1)S(1)}, u32[]{:S(2)}, u32[]{:S(2)}) collective-permute-start(bf16[128,768]{1,0:T(8,128)(2,1)S(1)} %slice.33), channel_id=1, source_target_pairs={{0,2},{1,3},{2,0},{3,1},{4,6},{5,7},{6,4},{7,5},{8,10},{9,11},{10,... | collective-permute-start | bytes 589832 | tf_op jit(solution)/shard_map/ppermute | solution.py:233
  192.5 19.0 %copy-start.18 = (bf16[128,768]{1,0:T(8,128)(2,1)}, bf16[128,768]{1,0:T(8,128)(2,1)S(1)}, u32[]{:S(2)}) copy-start(bf16[128,768]{1,0:T(8,128)(2,1)S(1)} %collective-permute-done.6.refs_7_) | copy-start | bytes 589828
  192.5 18.4 %collective-permute-start.17 = (bf16[128,768]{1,0:T(8,128)(2,1)S(1)}, bf16[128,768]{1,0:T(8,128)(2,1)S(1)}, u32[]{:S(2)}, u32[]{:S(2)}) collective-permute-start(bf16[128,768]{1,0:T(8,128)(2,1)S(1)} %collective-permute-done.6.refs_7_), channel_id=1, source_target_pairs={{0,16},{16,0},{1,17},{17,1},{2,18},{18,2},{3,19},{19,3},{4,20},{20... | collective-permute-start | bytes 589832 | tf_op jit(solution)/shard_map/ppermute | solution.py:237
  194.0 0.8 copy-start.11
  194.0 17.4 %collective-permute-start.14 = (bf16[128,768]{1,0:T(8,128)(2,1)S(1)}, bf16[128,768]{1,0:T(8,128)(2,1)S(1)}, u32[]{:S(2)}, u32[]{:S(2)}) collective-permute-start(bf16[128,768]{1,0:T(8,128)(2,1)S(1)} %collective-permute-done.6.refs_7_), channel_id=1, source_target_pairs={{0,1},{1,0},{2,3},{3,2},{4,5},{5,4},{6,7},{7,6},{8,9},{9,8},{10,11... | collective-permute-start | bytes 589832 | tf_op jit(solution)/shard_map/ppermute | solution.py:233
  194.4 21.7 %collective-permute-start.18 = (bf16[512,768]{1,0:T(8,128)(2,1)}, bf16[512,768]{1,0:T(8,128)(2,1)}, u32[]{:S(2)}, u32[]{:S(2)}) collective-permute-start(bf16[512,768]{1,0:T(8,128)(2,1)} %collective-permute-done.15.refs_16_), channel_id=1, source_target_pairs={{0,1},{1,0},{2,3},{3,2},{4,5},{5,4},{6,7},{7,6},{8,9},{9,8},{10,11... | collective-permute-start | bytes 2359304 | tf_op jit(solution)/shard_map/ppermute | solution.py:233
  210.8 4.5 %collective-permute-start.12 = (bf16[128,2304]{1,0:T(8,128)(2,1)}, bf16[128,2304]{1,0:T(8,128)(2,1)}, u32[]{:S(2)}, u32[]{:S(2)}) collective-permute-start(bf16[128,2304]{1,0:T(8,128)(2,1)} %collective-permute-done.4.refs_5_.refs_27_), channel_id=1, source_target_pairs={{0,1},{1,0},{2,3},{3,2},{4,5},{5,4},{6,7},{7,6},{8,9},{9,8},{10,11... | collective-permute-start | bytes 1769480 | tf_op jit(solution)/shard_map/ppermute | solution.py:233
  210.9 1.0 copy-start.19
  210.9 2.5 collective-permute-start.20
  211.4 2.0 copy-start.20
  211.4 4.0 %collective-permute-start.13 = (bf16[128,2304]{1,0:T(8,128)(2,1)}, bf16[128,2304]{1,0:T(8,128)(2,1)}, u32[]{:S(2)}, u32[]{:S(2)}) collective-permute-start(bf16[128,2304]{1,0:T(8,128)(2,1)} %collective-permute-done.5.refs_6_.refs_28_), channel_id=1, source_target_pairs={{0,1},{1,0},{2,3},{3,2},{4,5},{5,4},{6,7},{7,6},{8,9},{9,8},{10,11... | collective-permute-start | bytes 1769480 | tf_op jit(solution)/shard_map/ppermute | solution.py:233
  211.5 4.6 %collective-permute-start.19 = (bf16[384,768]{1,0:T(8,128)(2,1)}, bf16[384,768]{1,0:T(8,128)(2,1)}, u32[]{:S(2)}, u32[]{:S(2)}) collective-permute-start(bf16[384,768]{1,0:T(8,128)(2,1)} %collective-permute-done.16.refs_17_), channel_id=1, source_target_pairs={{0,1},{1,0},{2,3},{3,2},{4,5},{5,4},{6,7},{7,6},{8,9},{9,8},{10,11... | collective-permute-start | bytes 1769480 | tf_op jit(solution)/shard_map/ppermute | solution.py:233
  214.0 2.1 collective-permute-start.22
  216.1 1.2 copy-start.1
  217.3 17.2 %copy-start.23 = (s32[4]{0:T(128)S(1)}, s32[4]{0:T(128)}, u32[]{:S(2)}) copy-start(s32[4]{0:T(128)} %constant.170.clone) | copy-start | bytes 52
  232.8 3.3 %collective-permute-start.24 = (bf16[224,1536]{1,0:T(8,128)(2,1)}, bf16[224,1536]{1,0:T(8,128)(2,1)S(1)}, u32[]{:S(2)}, u32[]{:S(2)}) collective-permute-start(bf16[224,1536]{1,0:T(8,128)(2,1)} %get-tuple-element.48.cot_ref), channel_id=1, source_target_pairs={{0,1},{1,0},{2,3},{3,2},{4,5},{5,4},{6,7},{7,6},{8,9},{9,8},{10,11... | collective-permute-start | bytes 2064392 | tf_op jit(solution)/shard_map/ppermute | solution.py:310
  234.1 2.0 collective-permute-start.23
  236.1 1.0 copy-start.6
  240.9 12.2 %collective-permute-start.25 = (bf16[4,128,384]{2,1,0:T(8,128)(2,1)}, bf16[4,128,384]{2,1,0:T(8,128)(2,1)S(1)}, u32[]{:S(2)}, u32[]{:S(2)}) collective-permute-start(bf16[4,128,384]{2,1,0:T(8,128)(2,1)} %get-tuple-element.50), channel_id=1, source_target_pairs={{0,2},{1,3},{2,0},{3,1},{4,6},{5,7},{6,4},{7,5},{8,10},{9,11},{10,... | collective-permute-start | bytes 1179656 | tf_op jit(solution)/shard_map/ppermute | solution.py:310
  242.5 18.5 %collective-permute-start.28 = (bf16[4,128,384]{2,1,0:T(8,128)(2,1)}, bf16[4,128,384]{2,1,0:T(8,128)(2,1)S(1)}, u32[]{:S(2)}, u32[]{:S(2)}) collective-permute-start(bf16[4,128,384]{2,1,0:T(8,128)(2,1)} %get-tuple-element.52), channel_id=1, source_target_pairs={{0,2},{1,3},{2,0},{3,1},{4,6},{5,7},{6,4},{7,5},{8,10},{9,11},{10,... | collective-permute-start | bytes 1179656 | tf_op jit(solution)/shard_map/ppermute | solution.py:310
  242.9 20.0 %collective-permute-start.31 = (bf16[4,128,384]{2,1,0:T(8,128)(2,1)}, bf16[4,128,384]{2,1,0:T(8,128)(2,1)S(1)}, u32[]{:S(2)}, u32[]{:S(2)}) collective-permute-start(bf16[4,128,384]{2,1,0:T(8,128)(2,1)} %get-tuple-element.54), channel_id=1, source_target_pairs={{0,4},{1,5},{2,6},{3,7},{4,0},{5,1},{6,2},{7,3},{8,12},{9,13},{10,... | collective-permute-start | bytes 1179656 | tf_op jit(solution)/shard_map/ppermute | solution.py:310
  243.5 21.4 %collective-permute-start.34 = (bf16[4,128,384]{2,1,0:T(8,128)(2,1)}, bf16[4,128,384]{2,1,0:T(8,128)(2,1)S(1)}, u32[]{:S(2)}, u32[]{:S(2)}) collective-permute-start(bf16[4,128,384]{2,1,0:T(8,128)(2,1)} %get-tuple-element.56), channel_id=1, source_target_pairs={{0,4},{1,5},{2,6},{3,7},{4,0},{5,1},{6,2},{7,3},{8,12},{9,13},{10,... | collective-permute-start | bytes 1179656 | tf_op jit(solution)/shard_map/ppermute | solution.py:310
  248.8 14.2 %copy-start.17 = (bf16[4,128,384]{2,1,0:T(8,128)(2,1)S(1)}, bf16[4,128,384]{2,1,0:T(8,128)(2,1)}, u32[]{:S(2)}) copy-start(bf16[4,128,384]{2,1,0:T(8,128)(2,1)} %get-tuple-element.53) | copy-start | bytes 1179652
  253.1 11.8 %copy-start.16 = (bf16[4,128,384]{2,1,0:T(8,128)(2,1)S(1)}, bf16[4,128,384]{2,1,0:T(8,128)(2,1)}, u32[]{:S(2)}) copy-start(bf16[4,128,384]{2,1,0:T(8,128)(2,1)} %get-tuple-element.55) | copy-start | bytes 1179652
  254.2 13.6 %collective-permute-start.26 = (bf16[2,128,384]{2,1,0:T(8,128)(2,1)S(1)}, bf16[2,128,384]{2,1,0:T(8,128)(2,1)S(1)}, u32[]{:S(2)}, u32[]{:S(2)}) collective-permute-start(bf16[2,128,384]{2,1,0:T(8,128)(2,1)S(1)} %get-tuple-element.62), channel_id=1, source_target_pairs={{0,4},{1,5},{2,6},{3,7},{4,0},{5,1},{6,2},{7,3},{8,12},{9,13},{10,... | collective-permute-start | bytes 589832 | tf_op jit(solution)/shard_map/ppermute | solution.py:310
  262.0 9.8 %collective-permute-start.29 = (bf16[2,128,384]{2,1,0:T(8,128)(2,1)S(1)}, bf16[2,128,384]{2,1,0:T(8,128)(2,1)S(1)}, u32[]{:S(2)}, u32[]{:S(2)}) collective-permute-start(bf16[2,128,384]{2,1,0:T(8,128)(2,1)S(1)} %get-tuple-element.64), channel_id=1, source_target_pairs={{0,4},{1,5},{2,6},{3,7},{4,0},{5,1},{6,2},{7,3},{8,12},{9,13},{10,... | collective-permute-start | bytes 589832 | tf_op jit(solution)/shard_map/ppermute | solution.py:310
  263.1 11.4 %collective-permute-start.32 = (bf16[2,128,384]{2,1,0:T(8,128)(2,1)S(1)}, bf16[2,128,384]{2,1,0:T(8,128)(2,1)S(1)}, u32[]{:S(2)}, u32[]{:S(2)}) collective-permute-start(bf16[2,128,384]{2,1,0:T(8,128)(2,1)S(1)} %get-tuple-element.66), channel_id=1, source_target_pairs={{0,2},{1,3},{2,0},{3,1},{4,6},{5,7},{6,4},{7,5},{8,10},{9,11},{10,... | collective-permute-start | bytes 589832 | tf_op jit(solution)/shard_map/ppermute | solution.py:310
  265.0 10.0 %collective-permute-start.35 = (bf16[2,128,384]{2,1,0:T(8,128)(2,1)S(1)}, bf16[2,128,384]{2,1,0:T(8,128)(2,1)S(1)}, u32[]{:S(2)}, u32[]{:S(2)}) collective-permute-start(bf16[2,128,384]{2,1,0:T(8,128)(2,1)S(1)} %get-tuple-element.68), channel_id=1, source_target_pairs={{0,2},{1,3},{2,0},{3,1},{4,6},{5,7},{6,4},{7,5},{8,10},{9,11},{10,... | collective-permute-start | bytes 589832 | tf_op jit(solution)/shard_map/ppermute | solution.py:310
  267.8 9.8 %collective-permute-start.27 = (bf16[128,384]{1,0:T(8,128)(2,1)S(1)}, bf16[128,384]{1,0:T(8,128)(2,1)S(1)}, u32[]{:S(2)}, u32[]{:S(2)}) collective-permute-start(bf16[128,384]{1,0:T(8,128)(2,1)S(1)} %fusion.13), channel_id=1, source_target_pairs={{0,8},{1,9},{2,10},{3,11},{4,12},{5,13},{6,14},{7,15},{8,0},{9,1},... | collective-permute-start | bytes 294920 | tf_op jit(solution)/shard_map/ppermute | solution.py:310
  271.9 11.9 %collective-permute-start.30 = (bf16[128,384]{1,0:T(8,128)(2,1)S(1)}, bf16[128,384]{1,0:T(8,128)(2,1)S(1)}, u32[]{:S(2)}, u32[]{:S(2)}) collective-permute-start(bf16[128,384]{1,0:T(8,128)(2,1)S(1)} %fusion.15), channel_id=1, source_target_pairs={{0,8},{1,9},{2,10},{3,11},{4,12},{5,13},{6,14},{7,15},{8,0},{9,1},... | collective-permute-start | bytes 294920 | tf_op jit(solution)/shard_map/ppermute | solution.py:310
  274.6 11.3 %collective-permute-start.33 = (bf16[128,384]{1,0:T(8,128)(2,1)S(1)}, bf16[128,384]{1,0:T(8,128)(2,1)S(1)}, u32[]{:S(2)}, u32[]{:S(2)}) collective-permute-start(bf16[128,384]{1,0:T(8,128)(2,1)S(1)} %fusion.17), channel_id=1, source_target_pairs={{0,8},{1,9},{2,10},{3,11},{4,12},{5,13},{6,14},{7,15},{8,0},{9,1},... | collective-permute-start | bytes 294920 | tf_op jit(solution)/shard_map/ppermute | solution.py:310
  275.0 12.8 %collective-permute-start.36 = (bf16[128,384]{1,0:T(8,128)(2,1)S(1)}, bf16[128,384]{1,0:T(8,128)(2,1)S(1)}, u32[]{:S(2)}, u32[]{:S(2)}) collective-permute-start(bf16[128,384]{1,0:T(8,128)(2,1)S(1)} %fusion.19), channel_id=1, source_target_pairs={{0,8},{1,9},{2,10},{3,11},{4,12},{5,13},{6,14},{7,15},{8,0},{9,1},... | collective-permute-start | bytes 294920 | tf_op jit(solution)/shard_map/ppermute | solution.py:310
  (2 other events, 1.5 us)

commit v8 on v7

--- a/solution.py
+++ b/solution.py
@@ -240,16 +240,19 @@
         line, pair = self.swap(self.own, 2), self.swap(self.own, 1)
         value, self.own, line, pair = lax.optimization_barrier((value, self.own, line, pair))
         self.blocks = [self.own, line, pair, self.swap(line, 1), self.swap(self.own, 3)]
+        self.others = [self.across(self.own, line, pair)]
         return value
 
     def far(self, value):
-        value, self.blocks = lax.optimization_barrier((value, self.blocks))
+        value, self.blocks, self.others = lax.optimization_barrier((value, self.blocks, self.others))
         line, pair = self.swap(self.blocks[4], 2), self.swap(self.blocks[4], 1)
         value, line, pair = lax.optimization_barrier((value, line, pair))
-        self.corner = (self.swap(line[:, :self.cut], 1), self.swap(pair[:, self.cut:], 2))
-        self.others = [self.across(*self.blocks[:4])]
+        self.corner = (
+            self.swap(line[:, :self.cut], 1),
+            self.swap(line[:, self.cut:], 1),
+        )
         self.blocks += [line, pair]
-        self.others += [self.across(*self.blocks[4:]), self.across(self.corner[0])]
+        self.others += [self.across(*self.blocks[3:]), self.across(self.corner[0])]
         return value
 
     def rows(self, position):

time: 290 us -> 287 us (0.990)
  waiting for transfers between devices: 158 us -> 152 us
  starting transfers between devices: 62.1 us -> 65.9 us
    ppermute x20, waiting for transfers between devices: 48.3 us -> 27.3 us  [swap(): lax.ppermute(x, 'seq', [(s, s ^ 1 << k) for s in range(self.group_size)])]
    ppermute x3, waiting for transfers between devices: 0.32 us -> 18 us  [across(): return lax.ppermute(halves, 'grp', [(g, g ^ 1) for g in range(self.groups)])]
  transfers between devices with their start and end apart: 39 -> 39, of which waited for: 18 -> 17; matrix products, arithmetic and copies ran while one was open for 5% -> 5% of each run, Pallas kernels for 9% -> 9%
where the time goes in v8:
time: 287 us; the launch traced here: 286 us
  waiting for transfers between devices  152 us (53%)
  starting transfers between devices  65.9 us (23%)
  Pallas kernels  43.9 us (15%)
  local copies, waits for them, and re-layouts  13.9 us (5%)
  other arithmetic  9.37 us (3%)
    all_to_all x1, waiting for transfers between devices, shards(): gathered = exchange(jnp.concatenate([text_items, image_items], axis=2))  84.1 us
    ppermute x20, starting transfers between devices, swap(): lax.ppermute(x, 'seq', [(s, s ^ 1 << k) for s in range(self.group_size)])  30 us
    ppermute x20, waiting for transfers between devices, swap(): lax.ppermute(x, 'seq', [(s, s ^ 1 << k) for s in range(self.group_size)])  27.3 us
    ppermute x14, waiting for transfers between devices, swap(): return lax.ppermute(x, 'seq', [(s, s ^ 1 << k) for s in range(group_size)])  22.9 us
    pallas_call x1, Pallas kernels, attend(): pl.pallas_call(functools.partial(attention_kernel, image_dev, text_dev, b...  20.9 us
    ppermute x14, starting transfers between devices, swap(): return lax.ppermute(x, 'seq', [(s, s ^ 1 << k) for s in range(group_size)])  19.7 us
    ppermute x3, waiting for transfers between devices, across(): return lax.ppermute(halves, 'grp', [(g, g ^ 1) for g in range(self.groups)])  18 us
    pallas_call x1, Pallas kernels, project(): pl.pallas_call(functools.partial(head_kernel, samples, image_dev, tuple((...  15.4 us
  transfers between devices with their start and end apart: 39, of which 17 were waited for; matrix products, arithmetic and copies ran while one was open for 5% of the time, Pallas kernels for 9%

profile of v8, /device:TPU:0, one launch (start us, length us, event | category | flops | bytes accessed | tf_op | source)
XLA Modules:
  0.0 286.4 jit_solution(10558089021878738129)
XLA Ops:
  0.0 2.4 copy.19
  2.5 0.6 copy.18
  3.1 2.6 pad_maximum_fusion
  5.8 7.6 %all-to-all-start = ((bf16[16,4,296,128]{3,2,1,0:T(8,128)(2,1)}), bf16[16,4,296,128]{3,2,1,0:T(8,128)(2,1)}, u32[]{:S(2)}, u32[]{:S(2)}) async-start(bf16[16,4,296,128]{3,2,1,0:T(8,128)(2,1)} %pad_maximum_fusion), calls=%async_computation | async-start | bytes 9699328 | tf_op jit(solution)/shard_map/all_to_all | solution.py:397
  13.5 1.9 collective-permute-start
  15.4 1.5 collective-permute-start.1
  17.0 0.7 fusion.20
  17.8 0.6 fusion.30
  18.4 84.1 %all-to-all-done.x_ref = bf16[16,4,296,128]{3,2,1,0:T(8,128)(2,1)} async-done(((bf16[16,4,296,128]{3,2,1,0:T(8,128)(2,1)}), bf16[16,4,296,128]{3,2,1,0:T(8,128)(2,1)}, u32[]{:S(2)}, u32[]{:S(2)}) %all-to-all-start) | async-done | bytes 4849696 | tf_op jit(solution)/shard_map/all_to_all | solution.py:397
  102.5 2.7 collective-permute-done.refs_1_.refs_23_
  105.2 4.5 %collective-permute-start.2 = (bf16[128,2304]{1,0:T(8,128)(2,1)S(1)}, bf16[128,2304]{1,0:T(8,128)(2,1)}, u32[]{:S(2)}, u32[]{:S(2)}) collective-permute-start(bf16[128,2304]{1,0:T(8,128)(2,1)S(1)} %collective-permute-done.refs_1_.refs_23_), channel_id=1, source_target_pairs={{0,2},{1,3},{2,0},{3,1},{4,6},{5,7},{6,4},{7,5},{8,10},{9,11},{10,... | collective-permute-start | bytes 1769480 | tf_op jit(solution)/shard_map/ppermute | solution.py:233
  109.6 13.4 %collective-permute-start.3 = (bf16[128,2304]{1,0:T(8,128)(2,1)S(1)}, bf16[128,2304]{1,0:T(8,128)(2,1)}, u32[]{:S(2)}, u32[]{:S(2)}) collective-permute-start(bf16[128,2304]{1,0:T(8,128)(2,1)S(1)} %pad_maximum_fusion.3.refs_0_.refs_22_), channel_id=1, source_target_pairs={{0,8},{1,9},{2,10},{3,11},{4,12},{5,13},{6,14},{7,15},{8,0},{9,1},... | collective-permute-start | bytes 1769480 | tf_op jit(solution)/shard_map/ppermute | solution.py:233
  123.1 0.9 pad_maximum_fusion.4
  123.9 1.5 collective-permute-start.4
  125.4 0.6 gather_fusion
  126.1 20.9 %attention.1 = bf16[16,4,2,56,128]{4,3,2,1,0:T(8,128)(2,1)} custom-call(bf16[16,4,296,128]{3,2,1,0:T(8,128)(2,1)} %all-to-all-done.x_ref, s32[4,2,512]{2,1,0:T(2,128)S(1)} %compare_convert_fusion.live_ref), custom_call_target="tpu_custom_call" | custom-call | flops 3523215360 | bytes 6684672 | tf_op jit(solution)/shard_map/attention/pallas_call | solution.py:72
  147.0 1.9 collective-permute-done.3.refs_4_.refs_26_
  148.9 0.6 collective-permute-start.5
  149.5 1.1 collective-permute-start.6
  150.7 12.9 %collective-permute-done.5.refs_5_.refs_27_ = bf16[128,2304]{1,0:T(8,128)(2,1)} collective-permute-done((bf16[128,2304]{1,0:T(8,128)(2,1)}, bf16[128,2304]{1,0:T(8,128)(2,1)}, u32[]{:S(2)}, u32[]{:S(2)}) %collective-permute-start.5) | collective-permute-done | bytes 589856 | tf_op jit(solution)/shard_map/ppermute | solution.py:233
  163.5 1.3 collective-permute-done.6.refs_6_.refs_28_
  164.8 4.9 %all-to-all-start.1 = ((bf16[16,4,2,56,128]{4,3,2,1,0:T(8,128)(2,1)}), bf16[16,4,2,56,128]{4,3,2,1,0:T(8,128)(2,1)S(1)}, u32[]{:S(2)}, u32[]{:S(2)}) async-start(bf16[16,4,2,56,128]{4,3,2,1,0:T(8,128)(2,1)} %attention.1), calls=%async_computation.1 | async-start | bytes 3670016 | tf_op jit(solution)/shard_map/all_to_all | solution.py:414
  170.3 0.9 slice.37
  171.3 0.9 slice.38
  172.2 0.9 slice.36
  173.2 0.9 slice.39
  174.2 1.6 collective-permute-start.16
  176.9 1.0 slice.40
  177.9 2.0 collective-permute-start.21
  179.9 1.6 collective-permute-start.7
  181.6 12.7 %collective-permute-done.16.refs_17_ = bf16[512,768]{1,0:T(8,128)(2,1)} collective-permute-done((bf16[512,768]{1,0:T(8,128)(2,1)S(1)}, bf16[512,768]{1,0:T(8,128)(2,1)}, u32[]{:S(2)}, u32[]{:S(2)}) %collective-permute-start.16) | collective-permute-done | bytes 786464 | tf_op jit(solution)/shard_map/ppermute | solution.py:237
  194.7 7.7 %collective-permute-done.7.refs_7_ = bf16[128,768]{1,0:T(8,128)(2,1)} collective-permute-done((bf16[128,768]{1,0:T(8,128)(2,1)S(1)}, bf16[128,768]{1,0:T(8,128)(2,1)}, u32[]{:S(2)}, u32[]{:S(2)}) %collective-permute-start.7) | collective-permute-done | bytes 196640 | tf_op jit(solution)/shard_map/ppermute | solution.py:233
  202.4 0.8 collective-permute-start.17
  203.9 5.4 %collective-permute-done.17.refs_18_ = bf16[128,768]{1,0:T(8,128)(2,1)S(1)} collective-permute-done((bf16[128,768]{1,0:T(8,128)(2,1)}, bf16[128,768]{1,0:T(8,128)(2,1)S(1)}, u32[]{:S(2)}, u32[]{:S(2)}) %collective-permute-start.17) | collective-permute-done | bytes 196640 | tf_op jit(solution)/shard_map/ppermute | solution.py:237
  209.2 0.7 copy-done.20
  209.9 0.6 and_select_fusion.2.blocks
  211.6 0.7 collective-permute-done.20.refs_21_
  212.3 0.7 copy-done.21
  213.0 1.2 copy-done.1
  214.2 15.4 %project.1 = (bf16[224,1536]{1,0:T(8,128)(2,1)}, bf16[16,128,224]{2,1,0:T(8,128)(2,1)}) custom-call(s32[16]{0:T(128)} %broadcast_xor_fusion.heads, s32[6]{0:T(128)} %and_select_fusion.2.blocks, bf16[16,4,2,56,128]{4,3,2,1,0:T(8,128)(2,1)} %copy-done.1, bf16[4,56,1536]{2,1,0:T(8,128)(2,1)} %states_ref.1, f32[4,1536]{1,0:T(4,128)} %get-tuple-element.40.gate_ref, ...), custom_call_target="tpu_custom_call" | custom-call | flops 4227858432 | bytes 14417920 | tf_op jit(solution)/shard_map/project/pallas_call | solution.py:190
  230.1 1.1 dynamic-slice_bitcast_fusion
  231.4 0.7 multiply_add_fusion
  232.1 1.1 collective-permute-done.23.att_peer_ref
  233.2 0.8 copy-done.14
  234.2 3.8 %product.3 = (bf16[4,128,384]{2,1,0:T(8,128)(2,1)}, bf16[4,128,384]{2,1,0:T(8,128)(2,1)}, bf16[4,128,384]{2,1,0:T(8,128)(2,1)}, bf16[4,128,384]{2,1,0:T(8,128)(2,1)}) custom-call(s32[8]{0:T(128)} %get-tuple-element.61.mine, s32[8]{0:T(128)} %get-tuple-element.62.peer, bf16[16,128,224]{2,1,0:T(8,128)(2,1)} %get-tuple-element.49.att_ref, ...), custom_call_target="tpu_custom_call" | custom-call | flops 704643072 | bytes 3866624 | tf_op jit(solution)/shard_map/product/pallas_call | solution.py:291
  238.0 2.6 collective-permute-start.25
  240.6 1.8 collective-permute-start.31
  242.7 3.8 %product.2 = (bf16[4,128,384]{2,1,0:T(8,128)(2,1)}, bf16[4,128,384]{2,1,0:T(8,128)(2,1)}, bf16[4,128,384]{2,1,0:T(8,128)(2,1)}, bf16[4,128,384]{2,1,0:T(8,128)(2,1)}) custom-call(s32[8]{0:T(128)} %get-tuple-element.77.mine, s32[8]{0:T(128)} %get-tuple-element.78.peer, bf16[16,128,224]{2,1,0:T(8,128)(2,1)} %get-tuple-element.49.att_ref, ...), custom_call_target="tpu_custom_call" | custom-call | flops 704643072 | bytes 3866624 | tf_op jit(solution)/shard_map/product/pallas_call | solution.py:291
  246.5 4.2 %collective-permute-done.25 = bf16[4,128,384]{2,1,0:T(8,128)(2,1)S(1)} collective-permute-done((bf16[4,128,384]{2,1,0:T(8,128)(2,1)}, bf16[4,128,384]{2,1,0:T(8,128)(2,1)S(1)}, u32[]{:S(2)}, u32[]{:S(2)}) %collective-permute-start.25) | collective-permute-done | bytes 393248 | tf_op jit(solution)/shard_map/ppermute | solution.py:313
  250.7 1.2 add_convert_fusion.7
  251.9 1.9 collective-permute-start.26
  253.8 4.9 %collective-permute-done.28 = bf16[4,128,384]{2,1,0:T(8,128)(2,1)S(1)} collective-permute-done((bf16[4,128,384]{2,1,0:T(8,128)(2,1)}, bf16[4,128,384]{2,1,0:T(8,128)(2,1)S(1)}, u32[]{:S(2)}, u32[]{:S(2)}) %collective-permute-start.28) | collective-permute-done | bytes 393248 | tf_op jit(solution)/shard_map/ppermute | solution.py:313
  258.7 1.1 add_convert_fusion.5
  259.8 1.6 collective-permute-start.29
  261.5 1.8 collective-permute-start.32
  263.8 1.7 collective-permute-done.26
  265.5 3.0 %collective-permute-start.27 = (bf16[128,384]{1,0:T(8,128)(2,1)S(1)}, bf16[128,384]{1,0:T(8,128)(2,1)S(1)}, u32[]{:S(2)}, u32[]{:S(2)}) collective-permute-start(bf16[128,384]{1,0:T(8,128)(2,1)S(1)} %fusion.13), channel_id=1, source_target_pairs={{0,8},{1,9},{2,10},{3,11},{4,12},{5,13},{6,14},{7,15},{8,0},{9,1},... | collective-permute-start | bytes 294920 | tf_op jit(solution)/shard_map/ppermute | solution.py:313
  268.5 1.1 collective-permute-done.29
  269.7 2.7 collective-permute-start.30
  272.8 2.7 collective-permute-start.36
  275.5 6.1 %collective-permute-done.30 = bf16[128,384]{1,0:T(8,128)(2,1)S(1)} collective-permute-done((bf16[128,384]{1,0:T(8,128)(2,1)S(1)}, bf16[128,384]{1,0:T(8,128)(2,1)S(1)}, u32[]{:S(2)}, u32[]{:S(2)}) %collective-permute-start.30) | collective-permute-done | bytes 98336 | tf_op jit(solution)/shard_map/ppermute | solution.py:313
  281.7 2.1 collective-permute-done.33
  283.8 1.6 collective-permute-done.36
  285.5 1.0 pad_maximum_fusion.2
  (115 shorter events, 7.0 us)
Async XLA Ops:
  0.0 17.0 %copy-start = (bf16[256,3072]{1,0:T(8,128)(2,1)S(1)}, bf16[256,3072]{1,0:T(8,128)(2,1)}, u32[]{:S(2)}) copy-start(bf16[256,3072]{1,0:T(8,128)(2,1)} %param.21) | copy-start | bytes 4718596
  0.0 2.5 copy-start.13
  5.7 7.6 %copy-start.22 = (bf16[128,1536]{1,0:T(8,128)(2,1)S(1)}, bf16[128,1536]{1,0:T(8,128)(2,1)}, u32[]{:S(2)}) copy-start(bf16[128,1536]{1,0:T(8,128)(2,1)} %param.19) | copy-start | bytes 1179652
  5.7 7.6 %copy-start.17 = (bf16[128,1536]{1,0:T(8,128)(2,1)S(1)}, bf16[128,1536]{1,0:T(8,128)(2,1)}, u32[]{:S(2)}) copy-start(bf16[128,1536]{1,0:T(8,128)(2,1)} %param.20) | copy-start | bytes 1179652
  5.8 96.7 %all-to-all-start = ((bf16[16,4,296,128]{3,2,1,0:T(8,128)(2,1)}), bf16[16,4,296,128]{3,2,1,0:T(8,128)(2,1)}, u32[]{:S(2)}, u32[]{:S(2)}) async-start(bf16[16,4,296,128]{3,2,1,0:T(8,128)(2,1)} %pad_maximum_fusion), calls=%async_computation | async-start | bytes 9699328 | tf_op jit(solution)/shard_map/all_to_all | solution.py:397
  13.3 3.5 %copy-start.24 = (s32[4]{0:T(128)S(1)}, s32[4]{0:T(128)}, u32[]{:S(2)}) copy-start(s32[4]{0:T(128)} %param.17) | copy-start | bytes 52
  13.4 110.5 %copy-start.2 = (bf16[128,2304]{1,0:T(8,128)(2,1)}, bf16[128,2304]{1,0:T(8,128)(2,1)S(1)}, u32[]{:S(2)}) copy-start(bf16[128,2304]{1,0:T(8,128)(2,1)S(1)} %pad_maximum_fusion.3.refs_0_.refs_22_) | copy-start | bytes 1769476
  13.5 91.7 %collective-permute-start = (bf16[128,2304]{1,0:T(8,128)(2,1)S(1)}, bf16[128,2304]{1,0:T(8,128)(2,1)S(1)}, u32[]{:S(2)}, u32[]{:S(2)}) collective-permute-start(bf16[128,2304]{1,0:T(8,128)(2,1)S(1)} %pad_maximum_fusion.3.refs_0_.refs_22_), channel_id=1, source_target_pairs={{0,4},{1,5},{2,6},{3,7},{4,0},{5,1},{6,2},{7,3},{8,12},{9,13},{10,... | collective-permute-start | bytes 1769480 | tf_op jit(solution)/shard_map/ppermute | solution.py:233
  15.4 89.7 %collective-permute-start.1 = (bf16[128,2304]{1,0:T(8,128)(2,1)S(1)}, bf16[128,2304]{1,0:T(8,128)(2,1)S(1)}, u32[]{:S(2)}, u32[]{:S(2)}) collective-permute-start(bf16[128,2304]{1,0:T(8,128)(2,1)S(1)} %pad_maximum_fusion.3.refs_0_.refs_22_), channel_id=1, source_target_pairs={{0,2},{1,3},{2,0},{3,1},{4,6},{5,7},{6,4},{7,5},{8,10},{9,11},{10,... | collective-permute-start | bytes 1769480 | tf_op jit(solution)/shard_map/ppermute | solution.py:233
  17.7 107.7 %copy-start.15 = (s32[2,4,512]{2,1,0:T(4,128)S(1)}, s32[2,4,512]{2,1,0:T(4,128)}, u32[]{:S(2)}) copy-start(s32[2,4,512]{2,1,0:T(4,128)} %param.16) | copy-start | bytes 49156
  105.1 41.9 %copy-start.4 = (bf16[128,2304]{1,0:T(8,128)(2,1)}, bf16[128,2304]{1,0:T(8,128)(2,1)S(1)}, u32[]{:S(2)}) copy-start(bf16[128,2304]{1,0:T(8,128)(2,1)S(1)} %collective-permute-done.refs_1_.refs_23_) | copy-start | bytes 1769476
  105.1 41.8 %copy-start.6 = (bf16[128,2304]{1,0:T(8,128)(2,1)}, bf16[128,2304]{1,0:T(8,128)(2,1)S(1)}, u32[]{:S(2)}) copy-start(bf16[128,2304]{1,0:T(8,128)(2,1)S(1)} %collective-permute-done.1.refs_2_.refs_24_) | copy-start | bytes 1769476
  105.2 41.8 %collective-permute-start.2 = (bf16[128,2304]{1,0:T(8,128)(2,1)S(1)}, bf16[128,2304]{1,0:T(8,128)(2,1)}, u32[]{:S(2)}, u32[]{:S(2)}) collective-permute-start(bf16[128,2304]{1,0:T(8,128)(2,1)S(1)} %collective-permute-done.refs_1_.refs_23_), channel_id=1, source_target_pairs={{0,2},{1,3},{2,0},{3,1},{4,6},{5,7},{6,4},{7,5},{8,10},{9,11},{10,... | collective-permute-start | bytes 1769480 | tf_op jit(solution)/shard_map/ppermute | solution.py:233
  109.6 39.3 %collective-permute-start.3 = (bf16[128,2304]{1,0:T(8,128)(2,1)S(1)}, bf16[128,2304]{1,0:T(8,128)(2,1)}, u32[]{:S(2)}, u32[]{:S(2)}) collective-permute-start(bf16[128,2304]{1,0:T(8,128)(2,1)S(1)} %pad_maximum_fusion.3.refs_0_.refs_22_), channel_id=1, source_target_pairs={{0,8},{1,9},{2,10},{3,11},{4,12},{5,13},{6,14},{7,15},{8,0},{9,1},... | collective-permute-start | bytes 1769480 | tf_op jit(solution)/shard_map/ppermute | solution.py:233
  123.9 23.1 %collective-permute-start.4 = (bf16[384,768]{1,0:T(8,128)(2,1)}, bf16[384,768]{1,0:T(8,128)(2,1)}, u32[]{:S(2)}, u32[]{:S(2)}) collective-permute-start(bf16[384,768]{1,0:T(8,128)(2,1)} %pad_maximum_fusion.4), channel_id=1, source_target_pairs={{0,16},{16,0},{1,17},{17,1},{2,18},{18,2},{3,19},{19,3},{4,20},{20... | collective-permute-start | bytes 1769480 | tf_op jit(solution)/shard_map/ppermute | solution.py:237
  148.9 14.6 %collective-permute-start.5 = (bf16[128,2304]{1,0:T(8,128)(2,1)}, bf16[128,2304]{1,0:T(8,128)(2,1)}, u32[]{:S(2)}, u32[]{:S(2)}) collective-permute-start(bf16[128,2304]{1,0:T(8,128)(2,1)} %collective-permute-done.3.refs_4_.refs_26_), channel_id=1, source_target_pairs={{0,4},{1,5},{2,6},{3,7},{4,0},{5,1},{6,2},{7,3},{8,12},{9,13},{10,... | collective-permute-start | bytes 1769480 | tf_op jit(solution)/shard_map/ppermute | solution.py:233
  149.5 15.3 %collective-permute-start.6 = (bf16[128,2304]{1,0:T(8,128)(2,1)}, bf16[128,2304]{1,0:T(8,128)(2,1)}, u32[]{:S(2)}, u32[]{:S(2)}) collective-permute-start(bf16[128,2304]{1,0:T(8,128)(2,1)} %collective-permute-done.3.refs_4_.refs_26_), channel_id=1, source_target_pairs={{0,2},{1,3},{2,0},{3,1},{4,6},{5,7},{6,4},{7,5},{8,10},{9,11},{10,... | collective-permute-start | bytes 1769480 | tf_op jit(solution)/shard_map/ppermute | solution.py:233
  164.8 48.1 %all-to-all-start.1 = ((bf16[16,4,2,56,128]{4,3,2,1,0:T(8,128)(2,1)}), bf16[16,4,2,56,128]{4,3,2,1,0:T(8,128)(2,1)S(1)}, u32[]{:S(2)}, u32[]{:S(2)}) async-start(bf16[16,4,2,56,128]{4,3,2,1,0:T(8,128)(2,1)} %attention.1), calls=%async_computation.1 | async-start | bytes 3670016 | tf_op jit(solution)/shard_map/all_to_all | solution.py:414
  169.7 6.5 %copy-start.3 = (bf16[128,2304]{1,0:T(8,128)(2,1)S(1)}, bf16[128,2304]{1,0:T(8,128)(2,1)}, u32[]{:S(2)}) copy-start(bf16[128,2304]{1,0:T(8,128)(2,1)} %copy-done.2) | copy-start | bytes 1769476
  169.7 6.7 %copy-start.5 = (bf16[128,2304]{1,0:T(8,128)(2,1)S(1)}, bf16[128,2304]{1,0:T(8,128)(2,1)}, u32[]{:S(2)}) copy-start(bf16[128,2304]{1,0:T(8,128)(2,1)} %copy-done.4) | copy-start | bytes 1769476
  169.7 6.5 %collective-permute-start.10 = (bf16[128,2304]{1,0:T(8,128)(2,1)}, bf16[128,2304]{1,0:T(8,128)(2,1)S(1)}, u32[]{:S(2)}, u32[]{:S(2)}) collective-permute-start(bf16[128,2304]{1,0:T(8,128)(2,1)} %copy-done.6), channel_id=1, source_target_pairs={{0,1},{1,0},{2,3},{3,2},{4,5},{5,4},{6,7},{7,6},{8,9},{9,8},{10,11... | collective-permute-start | bytes 1769480 | tf_op jit(solution)/shard_map/ppermute | solution.py:233
  170.2 6.3 %collective-permute-start.11 = (bf16[128,2304]{1,0:T(8,128)(2,1)}, bf16[128,2304]{1,0:T(8,128)(2,1)S(1)}, u32[]{:S(2)}, u32[]{:S(2)}) collective-permute-start(bf16[128,2304]{1,0:T(8,128)(2,1)} %collective-permute-done.2.refs_3_.refs_25_), channel_id=1, source_target_pairs={{0,1},{1,0},{2,3},{3,2},{4,5},{5,4},{6,7},{7,6},{8,9},{9,8},{10,11... | collective-permute-start | bytes 1769480 | tf_op jit(solution)/shard_map/ppermute | solution.py:233
  172.2 38.8 %copy-start.25 = (s32[16]{0:T(128)S(1)}, s32[16]{0:T(128)}, u32[]{:S(2)}) copy-start(s32[16]{0:T(128)} %constant.174) | copy-start | bytes 196
  174.2 20.0 %collective-permute-start.16 = (bf16[512,768]{1,0:T(8,128)(2,1)S(1)}, bf16[512,768]{1,0:T(8,128)(2,1)}, u32[]{:S(2)}, u32[]{:S(2)}) collective-permute-start(bf16[512,768]{1,0:T(8,128)(2,1)S(1)} %pad_maximum_fusion.1), channel_id=1, source_target_pairs={{0,16},{16,0},{1,17},{17,1},{2,18},{18,2},{3,19},{19,3},{4,20},{20... | collective-permute-start | bytes 2359304 | tf_op jit(solution)/shard_map/ppermute | solution.py:237
  175.7 2.2 collective-permute-start.12
  175.9 4.0 %collective-permute-start.18 = (bf16[384,768]{1,0:T(8,128)(2,1)}, bf16[384,768]{1,0:T(8,128)(2,1)S(1)}, u32[]{:S(2)}, u32[]{:S(2)}) collective-permute-start(bf16[384,768]{1,0:T(8,128)(2,1)} %collective-permute-done.4.refs_16_), channel_id=1, source_target_pairs={{0,1},{1,0},{2,3},{3,2},{4,5},{5,4},{6,7},{7,6},{8,9},{9,8},{10,11... | collective-permute-start | bytes 1769480 | tf_op jit(solution)/shard_map/ppermute | solution.py:233
  176.2 27.0 %copy-start.8 = (bf16[128,2304]{1,0:T(8,128)(2,1)}, bf16[128,2304]{1,0:T(8,128)(2,1)S(1)}, u32[]{:S(2)}) copy-start(bf16[128,2304]{1,0:T(8,128)(2,1)S(1)} %collective-permute-done.10.refs_10_.refs_32_) | copy-start | bytes 1769476
  176.3 18.0 %collective-permute-start.8 = (bf16[128,2304]{1,0:T(8,128)(2,1)S(1)}, bf16[128,2304]{1,0:T(8,128)(2,1)S(1)}, u32[]{:S(2)}, u32[]{:S(2)}) collective-permute-start(bf16[128,2304]{1,0:T(8,128)(2,1)S(1)} %copy-done.3), channel_id=1, source_target_pairs={{0,1},{1,0},{2,3},{3,2},{4,5},{5,4},{6,7},{7,6},{8,9},{9,8},{10,11... | collective-permute-start | bytes 1769480 | tf_op jit(solution)/shard_map/ppermute | solution.py:233
  176.5 26.8 %copy-start.9 = (bf16[128,2304]{1,0:T(8,128)(2,1)}, bf16[128,2304]{1,0:T(8,128)(2,1)S(1)}, u32[]{:S(2)}) copy-start(bf16[128,2304]{1,0:T(8,128)(2,1)S(1)} %collective-permute-done.11.refs_11_.refs_33_) | copy-start | bytes 1769476
  176.5 26.7 %collective-permute-start.9 = (bf16[128,2304]{1,0:T(8,128)(2,1)S(1)}, bf16[128,2304]{1,0:T(8,128)(2,1)S(1)}, u32[]{:S(2)}, u32[]{:S(2)}) collective-permute-start(bf16[128,2304]{1,0:T(8,128)(2,1)S(1)} %copy-done.5), channel_id=1, source_target_pairs={{0,1},{1,0},{2,3},{3,2},{4,5},{5,4},{6,7},{7,6},{8,9},{9,8},{10,11... | collective-permute-start | bytes 1769480 | tf_op jit(solution)/shard_map/ppermute | solution.py:233
  177.9 25.4 %copy-start.10 = (bf16[128,2304]{1,0:T(8,128)(2,1)}, bf16[128,2304]{1,0:T(8,128)(2,1)S(1)}, u32[]{:S(2)}) copy-start(bf16[128,2304]{1,0:T(8,128)(2,1)S(1)} %collective-permute-done.12.refs_12_.refs_34_) | copy-start | bytes 1769476
  177.9 25.3 %collective-permute-start.21 = (bf16[128,1536]{1,0:T(8,128)(2,1)S(1)}, bf16[128,1536]{1,0:T(8,128)(2,1)}, u32[]{:S(2)}, u32[]{:S(2)}) collective-permute-start(bf16[128,1536]{1,0:T(8,128)(2,1)S(1)} %slice.40), channel_id=1, source_target_pairs={{0,2},{1,3},{2,0},{3,1},{4,6},{5,7},{6,4},{7,5},{8,10},{9,11},{10,... | collective-permute-start | bytes 1179656 | tf_op jit(solution)/shard_map/ppermute | solution.py:233
  179.9 29.3 %copy-start.16 = (bf16[384,768]{1,0:T(8,128)(2,1)}, bf16[384,768]{1,0:T(8,128)(2,1)S(1)}, u32[]{:S(2)}) copy-start(bf16[384,768]{1,0:T(8,128)(2,1)S(1)} %collective-permute-done.18.refs_19_) | copy-start | bytes 1769476
  179.9 22.5 %collective-permute-start.7 = (bf16[128,768]{1,0:T(8,128)(2,1)S(1)}, bf16[128,768]{1,0:T(8,128)(2,1)}, u32[]{:S(2)}, u32[]{:S(2)}) collective-permute-start(bf16[128,768]{1,0:T(8,128)(2,1)S(1)} %slice.36), channel_id=1, source_target_pairs={{0,2},{1,3},{2,0},{3,1},{4,6},{5,7},{6,4},{7,5},{8,10},{9,11},{10,... | collective-permute-start | bytes 589832 | tf_op jit(solution)/shard_map/ppermute | solution.py:233
  194.2 18.8 %collective-permute-start.19 = (bf16[512,768]{1,0:T(8,128)(2,1)}, bf16[512,768]{1,0:T(8,128)(2,1)}, u32[]{:S(2)}, u32[]{:S(2)}) collective-permute-start(bf16[512,768]{1,0:T(8,128)(2,1)} %collective-permute-done.16.refs_17_), channel_id=1, source_target_pairs={{0,1},{1,0},{2,3},{3,2},{4,5},{5,4},{6,7},{7,6},{8,9},{9,8},{10,11... | collective-permute-start | bytes 2359304 | tf_op jit(solution)/shard_map/ppermute | solution.py:233
  194.2 9.6 %copy-start.11 = (bf16[128,2304]{1,0:T(8,128)(2,1)}, bf16[128,2304]{1,0:T(8,128)(2,1)S(1)}, u32[]{:S(2)}) copy-start(bf16[128,2304]{1,0:T(8,128)(2,1)S(1)} %collective-permute-done.8.refs_8_.refs_30_) | copy-start | bytes 1769476
  194.2 18.1 %collective-permute-start.13 = (bf16[128,2304]{1,0:T(8,128)(2,1)}, bf16[128,2304]{1,0:T(8,128)(2,1)}, u32[]{:S(2)}, u32[]{:S(2)}) collective-permute-start(bf16[128,2304]{1,0:T(8,128)(2,1)} %collective-permute-done.5.refs_5_.refs_27_), channel_id=1, source_target_pairs={{0,1},{1,0},{2,3},{3,2},{4,5},{5,4},{6,7},{7,6},{8,9},{9,8},{10,11... | collective-permute-start | bytes 1769480 | tf_op jit(solution)/shard_map/ppermute | solution.py:233
  202.4 6.8 %collective-permute-start.17 = (bf16[128,768]{1,0:T(8,128)(2,1)}, bf16[128,768]{1,0:T(8,128)(2,1)S(1)}, u32[]{:S(2)}, u32[]{:S(2)}) collective-permute-start(bf16[128,768]{1,0:T(8,128)(2,1)} %collective-permute-done.7.refs_7_), channel_id=1, source_target_pairs={{0,16},{16,0},{1,17},{17,1},{2,18},{18,2},{3,19},{19,3},{4,20},{20... | collective-permute-start | bytes 589832 | tf_op jit(solution)/shard_map/ppermute | solution.py:237
  203.2 6.0 %copy-start.12 = (bf16[128,2304]{1,0:T(8,128)(2,1)}, bf16[128,2304]{1,0:T(8,128)(2,1)S(1)}, u32[]{:S(2)}) copy-start(bf16[128,2304]{1,0:T(8,128)(2,1)S(1)} %collective-permute-done.9.refs_9_.refs_31_) | copy-start | bytes 1769476
  203.2 9.1 %collective-permute-start.14 = (bf16[128,2304]{1,0:T(8,128)(2,1)}, bf16[128,2304]{1,0:T(8,128)(2,1)}, u32[]{:S(2)}, u32[]{:S(2)}) collective-permute-start(bf16[128,2304]{1,0:T(8,128)(2,1)} %collective-permute-done.6.refs_6_.refs_28_), channel_id=1, source_target_pairs={{0,1},{1,0},{2,3},{3,2},{4,5},{5,4},{6,7},{7,6},{8,9},{9,8},{10,11... | collective-permute-start | bytes 1769480 | tf_op jit(solution)/shard_map/ppermute | solution.py:233
  203.3 7.2 %collective-permute-start.15 = (bf16[128,768]{1,0:T(8,128)(2,1)}, bf16[128,768]{1,0:T(8,128)(2,1)}, u32[]{:S(2)}, u32[]{:S(2)}) collective-permute-start(bf16[128,768]{1,0:T(8,128)(2,1)} %collective-permute-done.7.refs_7_), channel_id=1, source_target_pairs={{0,1},{1,0},{2,3},{3,2},{4,5},{5,4},{6,7},{7,6},{8,9},{9,8},{10,11... | collective-permute-start | bytes 589832 | tf_op jit(solution)/shard_map/ppermute | solution.py:233
  209.9 2.4 collective-permute-start.22
  210.5 1.8 collective-permute-start.20
  212.3 0.7 copy-start.21
  213.0 1.2 copy-start.1
  214.2 17.2 %copy-start.23 = (s32[4]{0:T(128)S(1)}, s32[4]{0:T(128)}, u32[]{:S(2)}) copy-start(s32[4]{0:T(128)} %constant.170.clone) | copy-start | bytes 52
  229.7 3.5 %collective-permute-start.24 = (bf16[224,1536]{1,0:T(8,128)(2,1)}, bf16[224,1536]{1,0:T(8,128)(2,1)S(1)}, u32[]{:S(2)}, u32[]{:S(2)}) collective-permute-start(bf16[224,1536]{1,0:T(8,128)(2,1)} %get-tuple-element.50.cot_ref), channel_id=1, source_target_pairs={{0,1},{1,0},{2,3},{3,2},{4,5},{5,4},{6,7},{7,6},{8,9},{9,8},{10,11... | collective-permute-start | bytes 2064392 | tf_op jit(solution)/shard_map/ppermute | solution.py:313
  231.2 2.0 collective-permute-start.23
  233.2 0.8 copy-start.14
  233.2 1.0 copy-start.7
  238.0 12.7 %collective-permute-start.25 = (bf16[4,128,384]{2,1,0:T(8,128)(2,1)}, bf16[4,128,384]{2,1,0:T(8,128)(2,1)S(1)}, u32[]{:S(2)}, u32[]{:S(2)}) collective-permute-start(bf16[4,128,384]{2,1,0:T(8,128)(2,1)} %get-tuple-element.52), channel_id=1, source_target_pairs={{0,2},{1,3},{2,0},{3,1},{4,6},{5,7},{6,4},{7,5},{8,10},{9,11},{10,... | collective-permute-start | bytes 1179656 | tf_op jit(solution)/shard_map/ppermute | solution.py:313
  240.6 18.1 %collective-permute-start.28 = (bf16[4,128,384]{2,1,0:T(8,128)(2,1)}, bf16[4,128,384]{2,1,0:T(8,128)(2,1)S(1)}, u32[]{:S(2)}, u32[]{:S(2)}) collective-permute-start(bf16[4,128,384]{2,1,0:T(8,128)(2,1)} %get-tuple-element.54), channel_id=1, source_target_pairs={{0,2},{1,3},{2,0},{3,1},{4,6},{5,7},{6,4},{7,5},{8,10},{9,11},{10,... | collective-permute-start | bytes 1179656 | tf_op jit(solution)/shard_map/ppermute | solution.py:313
  240.6 20.7 %collective-permute-start.31 = (bf16[4,128,384]{2,1,0:T(8,128)(2,1)}, bf16[4,128,384]{2,1,0:T(8,128)(2,1)S(1)}, u32[]{:S(2)}, u32[]{:S(2)}) collective-permute-start(bf16[4,128,384]{2,1,0:T(8,128)(2,1)} %get-tuple-element.56), channel_id=1, source_target_pairs={{0,4},{1,5},{2,6},{3,7},{4,0},{5,1},{6,2},{7,3},{8,12},{9,13},{10,... | collective-permute-start | bytes 1179656 | tf_op jit(solution)/shard_map/ppermute | solution.py:313
  242.4 20.8 %collective-permute-start.34 = (bf16[4,128,384]{2,1,0:T(8,128)(2,1)}, bf16[4,128,384]{2,1,0:T(8,128)(2,1)S(1)}, u32[]{:S(2)}, u32[]{:S(2)}) collective-permute-start(bf16[4,128,384]{2,1,0:T(8,128)(2,1)} %get-tuple-element.58), channel_id=1, source_target_pairs={{0,4},{1,5},{2,6},{3,7},{4,0},{5,1},{6,2},{7,3},{8,12},{9,13},{10,... | collective-permute-start | bytes 1179656 | tf_op jit(solution)/shard_map/ppermute | solution.py:313
  246.5 14.9 %copy-start.19 = (bf16[4,128,384]{2,1,0:T(8,128)(2,1)S(1)}, bf16[4,128,384]{2,1,0:T(8,128)(2,1)}, u32[]{:S(2)}) copy-start(bf16[4,128,384]{2,1,0:T(8,128)(2,1)} %get-tuple-element.55) | copy-start | bytes 1179652
  250.7 12.5 %copy-start.18 = (bf16[4,128,384]{2,1,0:T(8,128)(2,1)S(1)}, bf16[4,128,384]{2,1,0:T(8,128)(2,1)}, u32[]{:S(2)}) copy-start(bf16[4,128,384]{2,1,0:T(8,128)(2,1)} %get-tuple-element.57) | copy-start | bytes 1179652
  251.9 13.6 %collective-permute-start.26 = (bf16[2,128,384]{2,1,0:T(8,128)(2,1)S(1)}, bf16[2,128,384]{2,1,0:T(8,128)(2,1)S(1)}, u32[]{:S(2)}, u32[]{:S(2)}) collective-permute-start(bf16[2,128,384]{2,1,0:T(8,128)(2,1)S(1)} %get-tuple-element.64), channel_id=1, source_target_pairs={{0,4},{1,5},{2,6},{3,7},{4,0},{5,1},{6,2},{7,3},{8,12},{9,13},{10,... | collective-permute-start | bytes 589832 | tf_op jit(solution)/shard_map/ppermute | solution.py:313
  259.8 9.9 %collective-permute-start.29 = (bf16[2,128,384]{2,1,0:T(8,128)(2,1)S(1)}, bf16[2,128,384]{2,1,0:T(8,128)(2,1)S(1)}, u32[]{:S(2)}, u32[]{:S(2)}) collective-permute-start(bf16[2,128,384]{2,1,0:T(8,128)(2,1)S(1)} %get-tuple-element.66), channel_id=1, source_target_pairs={{0,4},{1,5},{2,6},{3,7},{4,0},{5,1},{6,2},{7,3},{8,12},{9,13},{10,... | collective-permute-start | bytes 589832 | tf_op jit(solution)/shard_map/ppermute | solution.py:313
  261.5 10.9 %collective-permute-start.32 = (bf16[2,128,384]{2,1,0:T(8,128)(2,1)S(1)}, bf16[2,128,384]{2,1,0:T(8,128)(2,1)S(1)}, u32[]{:S(2)}, u32[]{:S(2)}) collective-permute-start(bf16[2,128,384]{2,1,0:T(8,128)(2,1)S(1)} %get-tuple-element.68), channel_id=1, source_target_pairs={{0,2},{1,3},{2,0},{3,1},{4,6},{5,7},{6,4},{7,5},{8,10},{9,11},{10,... | collective-permute-start | bytes 589832 | tf_op jit(solution)/shard_map/ppermute | solution.py:313
  263.4 9.4 %collective-permute-start.35 = (bf16[2,128,384]{2,1,0:T(8,128)(2,1)S(1)}, bf16[2,128,384]{2,1,0:T(8,128)(2,1)S(1)}, u32[]{:S(2)}, u32[]{:S(2)}) collective-permute-start(bf16[2,128,384]{2,1,0:T(8,128)(2,1)S(1)} %get-tuple-element.70), channel_id=1, source_target_pairs={{0,2},{1,3},{2,0},{3,1},{4,6},{5,7},{6,4},{7,5},{8,10},{9,11},{10,... | collective-permute-start | bytes 589832 | tf_op jit(solution)/shard_map/ppermute | solution.py:313
  265.5 10.0 %collective-permute-start.27 = (bf16[128,384]{1,0:T(8,128)(2,1)S(1)}, bf16[128,384]{1,0:T(8,128)(2,1)S(1)}, u32[]{:S(2)}, u32[]{:S(2)}) collective-permute-start(bf16[128,384]{1,0:T(8,128)(2,1)S(1)} %fusion.13), channel_id=1, source_target_pairs={{0,8},{1,9},{2,10},{3,11},{4,12},{5,13},{6,14},{7,15},{8,0},{9,1},... | collective-permute-start | bytes 294920 | tf_op jit(solution)/shard_map/ppermute | solution.py:313
  269.7 12.0 %collective-permute-start.30 = (bf16[128,384]{1,0:T(8,128)(2,1)S(1)}, bf16[128,384]{1,0:T(8,128)(2,1)S(1)}, u32[]{:S(2)}, u32[]{:S(2)}) collective-permute-start(bf16[128,384]{1,0:T(8,128)(2,1)S(1)} %fusion.15), channel_id=1, source_target_pairs={{0,8},{1,9},{2,10},{3,11},{4,12},{5,13},{6,14},{7,15},{8,0},{9,1},... | collective-permute-start | bytes 294920 | tf_op jit(solution)/shard_map/ppermute | solution.py:313
  272.4 11.4 %collective-permute-start.33 = (bf16[128,384]{1,0:T(8,128)(2,1)S(1)}, bf16[128,384]{1,0:T(8,128)(2,1)S(1)}, u32[]{:S(2)}, u32[]{:S(2)}) collective-permute-start(bf16[128,384]{1,0:T(8,128)(2,1)S(1)} %fusion.17), channel_id=1, source_target_pairs={{0,8},{1,9},{2,10},{3,11},{4,12},{5,13},{6,14},{7,15},{8,0},{9,1},... | collective-permute-start | bytes 294920 | tf_op jit(solution)/shard_map/ppermute | solution.py:313
  272.8 12.6 %collective-permute-start.36 = (bf16[128,384]{1,0:T(8,128)(2,1)S(1)}, bf16[128,384]{1,0:T(8,128)(2,1)S(1)}, u32[]{:S(2)}, u32[]{:S(2)}) collective-permute-start(bf16[128,384]{1,0:T(8,128)(2,1)S(1)} %fusion.19), channel_id=1, source_target_pairs={{0,8},{1,9},{2,10},{3,11},{4,12},{5,13},{6,14},{7,15},{8,0},{9,1},... | collective-permute-start | bytes 294920 | tf_op jit(solution)/shard_map/ppermute | solution.py:313
  (1 other events, 0.7 us)
